TPU v7x, 32 devices: a whole 2x2x4 slice. The times are simulated.
32 devices in a mesh: dp: 8 (over z, x), mp: 4 (over y, core).
Axes of the slice: x: 2, y: 2, z: 4, core: 2. Of those that a mesh axis runs over, the one named last changes fastest.
Arguments:
- inputs: bfloat16 [4096, 2048], P(('dp', 'mp')), may hold values from -6 to 6
- doc_lengths: int32 [8, 8], P('dp'), may hold values from 1 to 256, 512 in all within a row
- cotangent: bfloat16 [4096, 2048], P(('dp', 'mp')), may hold values from -6 to 6
- norm_gain: float32 [2048], replicated, may hold values from 0.5 to 1.5
- query_weight: bfloat16 [2048, 2048], P(None, 'mp'), may hold values from -0.125 to 0.125
- key_weight: bfloat16 [2048, 2048], P(None, 'mp'), may hold values from -0.125 to 0.125
- value_weight: bfloat16 [2048, 2048], P(None, 'mp'), may hold values from -0.125 to 0.125
- beta_weight: bfloat16 [2048, 16], P(None, 'mp'), may hold values from -0.125 to 0.125
- gating_weight: bfloat16 [2048, 2048], P(None, 'mp'), may hold values from -0.125 to 0.125
- conv_weight: float32 [3, 4, 2048], P(None, None, 'mp'), may hold values from -3 to 3
- head_gain: float32 [128], replicated, may hold values from 0.5 to 1.5
- output_weight: bfloat16 [2048, 2048], P('mp'), may hold values from -0.1875 to 0.1875
- ffn_gain: float32 [2048], replicated, may hold values from 0.5 to 1.5
- gate_weight: bfloat16 [2048, 5632], P(None, 'mp'), may hold values from -0.125 to 0.125
- up_weight: bfloat16 [2048, 5632], P(None, 'mp'), may hold values from -0.125 to 0.125
- down_weight: bfloat16 [5632, 2048], P('mp'), may hold values from -0.109375 to 0.109375
Outputs:
- output: bfloat16 [4096, 2048], P(('dp', 'mp'))
- input_grad: float32 [4096, 2048], P(('dp', 'mp'))
- norm_gain_grad: float32 [2048], replicated
- query_grad: float32 [2048, 2048], P(None, 'mp')
- key_grad: float32 [2048, 2048], P(None, 'mp')
- value_grad: float32 [2048, 2048], P(None, 'mp')
- beta_grad: float32 [2048, 16], P(None, 'mp')
- gating_grad: float32 [2048, 2048], P(None, 'mp')
- conv_grad: float32 [3, 4, 2048], P(None, None, 'mp')
- head_gain_grad: float32 [128], replicated
- output_grad: float32 [2048, 2048], P('mp')
- ffn_gain_grad: float32 [2048], replicated
- gate_grad: float32 [2048, 5632], P(None, 'mp')
- up_grad: float32 [2048, 5632], P(None, 'mp')
- down_grad: float32 [5632, 2048], P('mp')
Inputs may be any that keep to these rules, and one draw needn't show every extreme that they name: `doc_lengths`: row s lists the lengths of the documents packed in order into sequence s; each row sums to 512 and its largest entry is 256.
All inputs are finite; a program needn't handle non-finite values.
Results may differ from a plain program's by a relative error of at most 0.012.
Values may be sent and summed in bfloat16 or wider, within the bound.
A program may use at most 256 MiB of HBM per device.

v0:
```python
import jax
import jax.numpy as jnp
from jax import lax
from jax.sharding import PartitionSpec as P

DK = 128
CONV = 4
SPAN = 64


EPS_NORM = 1e-06
EPS_UNIT = 1e-06
EPS_HEAD = 0.05
PRECISE = lax.Precision.HIGHEST


def sigmoid_linear(values):
    return values * jax.nn.sigmoid(values)


def sigmoid_slope(values):
    logistic = jax.nn.sigmoid(values)
    return logistic * (1.0 + values * (1.0 - logistic))


def inverse_root(values, epsilon):
    return lax.rsqrt(jnp.mean(values * values, axis=-1, keepdims=True) + epsilon)


def norm_back(values, scales, gains, grads):
    weighted = grads * gains
    inner_sum = jnp.mean(weighted * values, axis=-1, keepdims=True)
    return scales * weighted - values * (scales * scales * scales) * inner_sum


def unit_back(values, scales, grads):
    inner_sum = jnp.sum(grads * values, axis=-1, keepdims=True)
    return scales * grads - values * (scales * scales * scales) * inner_sum


def doc_index(lengths, length):
    starts = jnp.cumsum(lengths, axis=1) - lengths
    places = jnp.arange(length, dtype=jnp.int32)
    within = jnp.sum((starts[:, :, None] <= places[None, None, :]).astype(jnp.int32), axis=1) - 1
    offsets = jnp.arange(lengths.shape[0], dtype=jnp.int32)[:, None] * lengths.shape[1]
    return (within + offsets).reshape(-1)


def make_masks(doc_ids):
    masks = []
    for lag_step in range(CONV):
        before = jnp.concatenate(
            [jnp.full((lag_step,), -1, jnp.int32), doc_ids[: doc_ids.shape[0] - lag_step]]
        )
        masks.append((doc_ids == before).astype(jnp.float32)[:, None])
    return masks


def lagged(values, lag_step):
    if lag_step == 0:
        return values
    padding = jnp.zeros((lag_step,) + values.shape[1:], values.dtype)
    return jnp.concatenate([padding, values[: values.shape[0] - lag_step]], axis=0)


def leading(values, lag_step):
    if lag_step == 0:
        return values
    padding = jnp.zeros((lag_step,) + values.shape[1:], values.dtype)
    return jnp.concatenate([values[lag_step:], padding], axis=0)


def conv_apply(values, conv_taps, masks):
    summed = conv_taps[0] * values * masks[0]
    for lag_step in range(1, CONV):
        summed = summed + conv_taps[lag_step] * lagged(values, lag_step) * masks[lag_step]
    return summed


def conv_back(values, conv_taps, masks, grads):
    d_values = jnp.zeros_like(values)
    tap_grads = []
    for lag_step in range(CONV):
        masked = grads * masks[lag_step]
        d_values = d_values + conv_taps[lag_step] * leading(masked, lag_step)
        tap_grads.append(jnp.sum(masked * lagged(values, lag_step), axis=0))
    return (d_values, jnp.stack(tap_grads))


def block_terms(query_blocks, key_blocks, value_blocks, rate_blocks, block_ids, prior):
    block_len = block_ids.shape[1]
    row_ids = lax.broadcasted_iota(jnp.int32, (block_len, block_len), 0)
    col_ids = lax.broadcasted_iota(jnp.int32, (block_len, block_len), 1)
    sameness = block_ids[:, :, None] == block_ids[:, None, :]
    strict = (sameness & (row_ids > col_ids)[None]).astype(jnp.float32)[:, None]
    inclusive = (sameness & (row_ids >= col_ids)[None]).astype(jnp.float32)[:, None]
    opening = (block_ids == prior[:, None]).astype(jnp.float32)[:, None, :, None]
    closing = (block_ids == block_ids[:, block_len - 1 :]).astype(jnp.float32)[:, None, :, None]
    carried = (block_ids[:, block_len - 1] == prior).astype(jnp.float32)
    gram_mat = jnp.einsum(
        "nhik,nhjk->nhij", key_blocks, key_blocks, preferred_element_type=jnp.float32
    )
    lower_mat = jnp.eye(block_len, dtype=jnp.float32) + rate_blocks[..., None] * gram_mat * strict
    stacked = jnp.concatenate([key_blocks, value_blocks], axis=-1).astype(jnp.float32)
    solved = jax.scipy.linalg.solve_triangular(
        lower_mat, rate_blocks[..., None] * stacked, lower=True, unit_diagonal=True
    )
    probes = (
        jnp.einsum("nhik,nhjk->nhij", query_blocks, key_blocks, preferred_element_type=jnp.float32)
        * inclusive
    )
    return (
        strict,
        inclusive,
        opening,
        closing,
        carried,
        gram_mat,
        lower_mat,
        stacked,
        solved,
        probes,
    )


def forward_step(carry_state, block):
    query_rows, key_rows, opening, closing, carried, solved, probes = block
    query_rows = query_rows.astype(jnp.float32)
    key_rows = key_rows.astype(jnp.float32)
    new_value = solved[..., DK:] - opening * jnp.einsum(
        "hck,hvk->hcv", solved[..., :DK], carry_state, precision=PRECISE
    )
    outputs = opening * jnp.einsum(
        "hck,hvk->hcv", query_rows, carry_state, precision=PRECISE
    ) + jnp.einsum("hij,hjv->hiv", probes, new_value, precision=PRECISE)
    updated = carried * carry_state + jnp.einsum(
        "hcv,hck->hvk", closing * new_value, key_rows, precision=PRECISE
    )
    return (updated, (outputs, carry_state))


def backward_step(d_carry, block):
    (
        query_rows,
        key_rows,
        rate_rows,
        strict,
        inclusive,
        opening,
        closing,
        carried,
        gram_mat,
        lower_mat,
        stacked,
        solved,
        probes,
        carry_state,
        d_outputs,
    ) = block
    query_rows = query_rows.astype(jnp.float32)
    key_rows = key_rows.astype(jnp.float32)
    w_rows = solved[..., :DK]
    new_value = solved[..., DK:] - opening * jnp.einsum(
        "hck,hvk->hcv", w_rows, carry_state, precision=PRECISE
    )
    d_new = jnp.einsum("hij,hiv->hjv", probes, d_outputs, precision=PRECISE) + closing * jnp.einsum(
        "hck,hvk->hcv", key_rows, d_carry, precision=PRECISE
    )
    d_key = jnp.einsum("hcv,hvk->hck", closing * new_value, d_carry, precision=PRECISE)
    d_state = carried * d_carry + jnp.einsum(
        "hcv,hck->hvk", opening * d_outputs, query_rows, precision=PRECISE
    )
    d_probe = jnp.einsum("hiv,hjv->hij", d_outputs, new_value, precision=PRECISE) * inclusive
    d_query = jnp.einsum(
        "hij,hjk->hik", d_probe, key_rows, precision=PRECISE
    ) + opening * jnp.einsum("hcv,hvk->hck", d_outputs, carry_state, precision=PRECISE)
    d_key = d_key + jnp.einsum("hij,hik->hjk", d_probe, query_rows, precision=PRECISE)
    d_lagged = -opening * d_new
    d_wrows = jnp.einsum("hcv,hvk->hck", d_lagged, carry_state, precision=PRECISE)
    d_state = d_state + jnp.einsum("hcv,hck->hvk", d_lagged, w_rows, precision=PRECISE)
    d_solved = jnp.concatenate([d_wrows, d_new], axis=-1)
    d_right = jax.scipy.linalg.solve_triangular(
        lower_mat, d_solved, trans=1, lower=True, unit_diagonal=True
    )
    d_lower = -jnp.einsum("hik,hjk->hij", d_right, solved, precision=PRECISE) * strict
    d_rate = jnp.sum(d_right * stacked, axis=-1) + jnp.sum(d_lower * gram_mat, axis=-1)
    d_stack = rate_rows[:, :, None] * d_right
    d_gram = rate_rows[:, :, None] * d_lower
    d_key = (
        d_key
        + d_stack[..., :DK]
        + jnp.einsum(
            "hij,hjk->hik", d_gram + jnp.swapaxes(d_gram, 1, 2), key_rows, precision=PRECISE
        )
    )
    d_value = d_stack[..., DK:]
    return (d_state, (d_query, d_key, d_value, d_rate))


def on_device(
    inputs,
    doc_lengths,
    cotangent,
    norm_gain,
    query_weight,
    key_weight,
    value_weight,
    beta_weight,
    gating_weight,
    conv_weight,
    head_gain,
    output_weight,
    ffn_gain,
    gate_weight,
    up_weight,
    down_weight,
):
    local_rows = inputs.shape[0]
    group_rows = local_rows * lax.axis_size("mp")
    doc_ids = doc_index(doc_lengths, group_rows // doc_lengths.shape[0])
    tap_masks = make_masks(doc_ids)
    head_count = query_weight.shape[1] // DK
    local_width = head_count * DK
    block_count = group_rows // SPAN

    def by_block(values):
        return jnp.transpose(values.reshape(block_count, SPAN, head_count, DK), (0, 2, 1, 3))

    def unblock(values):
        return jnp.transpose(values, (0, 2, 1, 3)).reshape(group_rows, head_count, DK)

    residual_in = inputs.astype(jnp.float32)
    scale_one = inverse_root(residual_in, EPS_NORM)
    normed_local = (residual_in * scale_one * norm_gain).astype(jnp.bfloat16)
    normed = lax.all_gather(normed_local, "mp", axis=0, tiled=True)

    def project(weights):
        return jnp.dot(normed, weights, preferred_element_type=jnp.float32)

    query_proj = project(query_weight)
    key_proj = project(key_weight)
    value_proj = project(value_weight)
    beta_logit = project(beta_weight)
    gate_proj = project(gating_weight)
    query_conv = conv_apply(query_proj, conv_weight[0], tap_masks)
    key_conv = conv_apply(key_proj, conv_weight[1], tap_masks)
    value_conv = conv_apply(value_proj, conv_weight[2], tap_masks)
    query_act = sigmoid_linear(query_conv).reshape(group_rows, head_count, DK)
    key_act = sigmoid_linear(key_conv).reshape(group_rows, head_count, DK)
    value_act = sigmoid_linear(value_conv).reshape(group_rows, head_count, DK)
    query_scale = lax.rsqrt(jnp.sum(query_act * query_act, axis=-1, keepdims=True) + EPS_UNIT)
    key_scale = lax.rsqrt(jnp.sum(key_act * key_act, axis=-1, keepdims=True) + EPS_UNIT)
    query_low = (query_act * query_scale).astype(jnp.bfloat16)
    key_low = (key_act * key_scale).astype(jnp.bfloat16)
    value_low = value_act.astype(jnp.bfloat16)
    betas = jax.nn.sigmoid(beta_logit)
    rate_blocks = jnp.transpose(betas.reshape(block_count, SPAN, head_count), (0, 2, 1))
    prior = jnp.concatenate([jnp.full((1,), -1, jnp.int32), doc_ids[:-1]]).reshape(
        block_count, SPAN
    )[:, 0]
    query_blocks = by_block(query_low)
    key_blocks = by_block(key_low)
    strict, inclusive, opening, closing, carried, gram_mat, lower_mat, stacked, solved, probes = (
        block_terms(
            query_blocks,
            key_blocks,
            by_block(value_low),
            rate_blocks,
            doc_ids.reshape(block_count, SPAN),
            prior,
        )
    )
    start_state = jnp.zeros((head_count, DK, DK), jnp.float32)
    final_state, (mixed_blocks, states_in) = lax.scan(
        forward_step,
        start_state,
        (query_blocks, key_blocks, opening, closing, carried, solved, probes),
    )
    mixed = unblock(mixed_blocks)
    head_scale = inverse_root(mixed, EPS_HEAD)
    head_normed = mixed * head_scale * head_gain
    gate_act = sigmoid_linear(gate_proj).reshape(group_rows, head_count, DK)
    mixer_low = (head_normed * gate_act).reshape(group_rows, local_width).astype(jnp.bfloat16)
    attended = lax.psum_scatter(
        jnp.dot(mixer_low, output_weight, preferred_element_type=jnp.float32),
        "mp",
        scatter_dimension=0,
        tiled=True,
    )
    residual_mid = residual_in + attended
    scale_two = inverse_root(residual_mid, EPS_NORM)
    ffn_local = (residual_mid * scale_two * ffn_gain).astype(jnp.bfloat16)
    ffn_input = lax.all_gather(ffn_local, "mp", axis=0, tiled=True)
    gate_pre = jnp.dot(ffn_input, gate_weight, preferred_element_type=jnp.float32)
    up_pre = jnp.dot(ffn_input, up_weight, preferred_element_type=jnp.float32)
    gate_swish = sigmoid_linear(gate_pre)
    hidden_low = (gate_swish * up_pre).astype(jnp.bfloat16)
    ffn_out = lax.psum_scatter(
        jnp.dot(hidden_low, down_weight, preferred_element_type=jnp.float32),
        "mp",
        scatter_dimension=0,
        tiled=True,
    )
    output = (residual_mid + ffn_out).astype(jnp.bfloat16)
    normed_back, ffn_back_in = (normed, ffn_input)
    grad_rows = lax.all_gather(cotangent, "mp", axis=0, tiled=True)
    d_down = jnp.einsum("tf,td->fd", hidden_low, grad_rows, preferred_element_type=jnp.float32)
    d_hidden = jnp.einsum("td,fd->tf", grad_rows, down_weight, preferred_element_type=jnp.float32)
    d_gate_low = (d_hidden * up_pre * sigmoid_slope(gate_pre)).astype(jnp.bfloat16)
    d_up_low = (d_hidden * gate_swish).astype(jnp.bfloat16)
    d_gate_w = jnp.einsum("td,tf->df", ffn_back_in, d_gate_low, preferred_element_type=jnp.float32)
    d_up_w = jnp.einsum("td,tf->df", ffn_back_in, d_up_low, preferred_element_type=jnp.float32)
    gate_part = jnp.einsum("tf,df->td", d_gate_low, gate_weight, preferred_element_type=jnp.float32)
    up_part = jnp.einsum("tf,df->td", d_up_low, up_weight, preferred_element_type=jnp.float32)
    d_ffn_norm = lax.psum_scatter(gate_part + up_part, "mp", scatter_dimension=0, tiled=True)
    d_mid = cotangent.astype(jnp.float32) + norm_back(residual_mid, scale_two, ffn_gain, d_ffn_norm)
    ffn_gain_part = jnp.sum(d_ffn_norm * residual_mid * scale_two, axis=0)
    mid_rows = lax.all_gather(d_mid.astype(jnp.bfloat16), "mp", axis=0, tiled=True)
    d_output_w = jnp.einsum("tf,td->fd", mixer_low, mid_rows, preferred_element_type=jnp.float32)
    d_mixer = jnp.einsum(
        "td,fd->tf", mid_rows, output_weight, preferred_element_type=jnp.float32
    ).reshape(group_rows, head_count, DK)
    d_head_normed = d_mixer * gate_act
    d_gating_low = (
        (d_mixer * head_normed).reshape(group_rows, local_width) * sigmoid_slope(gate_proj)
    ).astype(jnp.bfloat16)
    head_gain_part = jnp.sum(d_head_normed * mixed * head_scale, axis=(0, 1))
    d_mixed = norm_back(mixed, head_scale, head_gain, d_head_normed)
    back_inputs = (
        query_blocks,
        key_blocks,
        rate_blocks,
        strict,
        inclusive,
        opening,
        closing,
        carried,
        gram_mat,
        lower_mat,
        stacked,
        solved,
        probes,
        states_in,
        by_block(d_mixed),
    )
    first_grad, (d_query_b, d_key_b, d_value_b, d_rate_b) = lax.scan(
        backward_step, start_state, back_inputs, reverse=True
    )
    d_query_act = unit_back(query_act, query_scale, unblock(d_query_b))
    d_key_act = unit_back(key_act, key_scale, unblock(d_key_b))
    d_query_conv = d_query_act.reshape(group_rows, local_width) * sigmoid_slope(query_conv)
    d_key_conv = d_key_act.reshape(group_rows, local_width) * sigmoid_slope(key_conv)
    d_value_conv = unblock(d_value_b).reshape(group_rows, local_width) * sigmoid_slope(value_conv)
    d_query_proj, query_taps = conv_back(query_proj, conv_weight[0], tap_masks, d_query_conv)
    d_key_proj, key_taps = conv_back(key_proj, conv_weight[1], tap_masks, d_key_conv)
    d_value_proj, value_taps = conv_back(value_proj, conv_weight[2], tap_masks, d_value_conv)
    d_conv = jnp.stack([query_taps, key_taps, value_taps])
    d_rates = jnp.transpose(d_rate_b, (0, 2, 1)).reshape(group_rows, head_count)
    d_beta_low = (d_rates * betas * (1.0 - betas)).astype(jnp.bfloat16)
    low_grads = (
        d_query_proj.astype(jnp.bfloat16),
        d_key_proj.astype(jnp.bfloat16),
        d_value_proj.astype(jnp.bfloat16),
        d_beta_low,
        d_gating_low,
    )
    in_weights = (query_weight, key_weight, value_weight, beta_weight, gating_weight)
    proj_grads = tuple(
        (
            jnp.einsum("td,tf->df", normed_back, grads, preferred_element_type=jnp.float32)
            for grads in low_grads
        )
    )
    summed = jnp.zeros((lax.axis_size("mp") * local_rows, in_weights[0].shape[0]), jnp.float32)
    for grads, weights in zip(low_grads, in_weights):
        summed = summed + jnp.einsum(
            "tf,df->td", grads, weights, preferred_element_type=jnp.float32
        )
    d_normed = lax.psum_scatter(summed, "mp", scatter_dimension=0, tiled=True)
    input_grad = d_mid + norm_back(residual_in, scale_one, norm_gain, d_normed)
    norm_gain_part = jnp.sum(d_normed * residual_in * scale_one, axis=0)
    mixer_grads = proj_grads + (d_conv, d_output_w)
    summed_all = lax.psum(mixer_grads + (d_gate_w, d_up_w, d_down), "dp")
    mixer_grads = summed_all[:7]
    d_gate_w, d_up_w, d_down = (summed_all[7], summed_all[8], summed_all[9])
    gain_grads = lax.psum((norm_gain_part, ffn_gain_part, head_gain_part), ("dp", "mp"))
    return (
        output,
        input_grad,
        gain_grads[0],
        mixer_grads[0],
        mixer_grads[1],
        mixer_grads[2],
        mixer_grads[3],
        mixer_grads[4],
        mixer_grads[5],
        gain_grads[2],
        mixer_grads[6],
        gain_grads[1],
        d_gate_w,
        d_up_w,
        d_down,
    )


def solution(mesh):
    return jax.shard_map(
        on_device,
        mesh=mesh,
        in_specs=(
            P(("dp", "mp"), None),
            P("dp", None),
            P(("dp", "mp"), None),
            P(),
            P(None, "mp"),
            P(None, "mp"),
            P(None, "mp"),
            P(None, "mp"),
            P(None, "mp"),
            P(None, None, "mp"),
            P(),
            P("mp", None),
            P(),
            P(None, "mp"),
            P(None, "mp"),
            P("mp", None),
        ),
        out_specs=(
            P(("dp", "mp"), None),
            P(("dp", "mp"), None),
            P(),
            P(None, "mp"),
            P(None, "mp"),
            P(None, "mp"),
            P(None, "mp"),
            P(None, "mp"),
            P(None, None, "mp"),
            P(),
            P("mp", None),
            P(),
            P(None, "mp"),
            P(None, "mp"),
            P("mp", None),
        ),
        check_vma=False,
    )
```

profile of v0, /device:TPU:0, one launch (start us, length us, event | category | flops | bytes accessed | tf_op | source)
XLA Modules:
  0.0 2757.8 jit_solution(18418073688307675696)
XLA Ops:
  16.3 20.4 all-gather.5.cloned.1.call-done
  81.4 158.7 %custom-call.14 = f32[8,4,1,64,64]{3,4,2,1,0:T(8,128)} custom-call(f32[8,4,1,64,64]{4,3,2,1,0:T(8,128)} %get-tuple-element.887), custom_call_target="InvertDiagBlocksLowerTriangular" | custom-call | tf_op jit(solution)/shard_map/jit(_solve_triangular)/vmap(vmap())/triangular_solve | solution.py:105
  246.7 69.6 %while.38 = (s32[]{:T(128)}, f32[4,128,128]{2,1,0:T(8,128)S(1)}, f32[8,4,64,128]{3,1,2,0:T(4,128)}, f32[8,4,128,128]{3,2,1,0:T(8,128)}, f32[8]{0:T(128)S(1)}, /*...) while((s32[]{:T(128)}, f32[4,128,128]{2,1,0:T(8,128)S(1)}, ...), condition=%wide.region_6.7_spmd.clone, body=%wide.region_5.6_spmd.clone.sunk | while | flops 176717824 | bytes 3672506 | solution.py:274
  332.3 44.6 %reduce-scatter.5.cloned.1.call-done = f32[128,2048]{1,0:T(8,128)} async-done(((f32[512,2048]{1,0:T(8,128)}), f32[128,2048]{1,0:T(8,128)}) %reduce-scatter.5.cloned.1.call-update) | async-done | bytes 1048592 | tf_op jit(solution)/shard_map/reduce_scatter | solution.py:284
  381.1 22.1 all-gather.7.cloned.1.call-done
  427.3 10.3 multiply_convert_fusion
  461.4 35.2 %reduce-scatter.9.cloned.1.call-done = f32[128,2048]{1,0:T(8,128)} async-done(((f32[512,2048]{1,0:T(8,128)}), f32[128,2048]{1,0:T(8,128)}) %reduce-scatter.9.cloned.1.call-update) | async-done | bytes 1048592 | tf_op jit(solution)/shard_map/reduce_scatter | solution.py:315
  498.4 45.7 %reduce-scatter.7.cloned.1.call-done = f32[128,2048]{1,0:T(8,128)} async-done(((f32[512,2048]{1,0:T(8,128)}), f32[128,2048]{1,0:T(8,128)}) %reduce-scatter.7.cloned.1.call-update) | async-done | bytes 1048592 | tf_op jit(solution)/shard_map/reduce_scatter | solution.py:298
  553.2 17.4 all-gather.11.cloned.1.call-done
  591.4 366.6 %while.39 = (s32[]{:T(128)}, f32[4,128,128]{2,1,0:T(8,128)}, f32[8,4,64,128]{3,1,2,0:T(4,128)}, f32[8,4,64,128]{3,1,2,0:T(4,128)}, f32[8,4,64,128]{3,2,1,0:T(8,1...) while((s32[]{:T(128)}, f32[4,128,128]{2,1,0:T(8,128)}, ...), condition=%wide.region_17.18_spmd.clone, body=%wide.region_14.17_spmd.clone.sunk | while | flops 580104064 | bytes 11021913 | solution.py:346
  595.9 19.7 custom-call.20
  640.6 19.7 custom-call.20
  686.6 19.7 custom-call.20
  732.6 19.7 custom-call.20
  778.6 19.7 custom-call.20
  824.6 19.7 custom-call.20
  870.6 19.7 custom-call.20
  916.5 19.7 custom-call.20
  1003.6 10.6 fusion.178
  1043.9 39.2 %all-reduce.21 = (f32[2048,4]{0,1:T(4,128)}, f32[3,4,512]{2,1,0:T(4,128)}) all-reduce(f32[2048,4]{0,1:T(4,128)S(1)} %fusion.173, f32[3,4,512]{2,1,0:T(4,128)S(1)} %pad_maximum_fusion), channel_id=1, replica_groups=mesh['dp'=8,'mp'=4] {'dp'}, use_global_device_ids=true, to_apply=%region_27.28 | all-reduce | flops 14336 | bytes 114688 | tf_op jit(solution)/shard_map/psum | solution.py:383
  1084.8 43.2 %all-reduce.20 = (f32[2048]{0:T(1024)}, f32[128]{0:T(128)}, f32[2048]{0:T(1024)}) all-reduce(f32[2048]{0:T(1024)S(1)} %get-tuple-element.776, f32[128]{0:T(128)S(1)} %get-tuple-element.774, f32[2048]{0:T(1024)S(1)} %get-tuple-element.772), channel_id=1, replica_groups=mesh['dp'=8,'mp'=4] {'dp','mp'}, use_global_device_ids=true, to_apply=%region_23.24 | all-reduce | flops 4224 | bytes 33792 | tf_op jit(solution)/shard_map/psum | solution.py:386
  1130.8 1572.7 %all-reduce.25.cloned.1.call-done = (f32[2048,512]{1,0:T(8,128)}, f32[2048,512]{1,0:T(8,128)}, f32[2048,512]{1,0:T(8,128)}, f32[2048,512]{1,0:T(8,128)}, f32[512...) async-done(((f32[2048,512]{1,0:T(8,128)}, f32[2048,512]{1,0:T(8,128)}, f32[2048,512]{1,0:T(8,128)}, f32[2048,512]{1,0:T(8,128)}, ...) | async-done | bytes 55574544 | tf_op jit(solution)/shard_map/psum | solution.py:383
  2721.4 9.4 copy.459
  2740.3 10.8 copy.461
  (694 shorter events, 543.6 us)
Async XLA Ops:
  7.2 321.7 %copy-start = (bf16[512,2048]{1,0:T(8,128)(2,1)S(1)}, bf16[512,2048]{1,0:T(8,128)(2,1)}, u32[]{:S(2)}) copy-start(bf16[512,2048]{1,0:T(8,128)(2,1)} %param.31) | copy-start | bytes 6291460
  7.2 29.4 %all-gather.5.cloned.1.call-start = ((), (), s32[]{:S(2)}) async-start(), calls=%async_computation.4 | async-start | bytes 2621440 | tf_op jit(solution)/shard_map/all_gather | solution.py:235
  11.2 365.7 %reduce-scatter.5.cloned.1.call-start = ((), (), s32[]{:S(2)}) async-start(), calls=%async_computation.5 | async-start | bytes 5242880 | tf_op jit(solution)/shard_map/reduce_scatter | solution.py:284
  13.3 28.3 %copy-start.51 = (f32[512]{0:T(512)}, f32[512]{0:T(512)S(1)}, u32[]{:S(2)}) copy-start(f32[512]{0:T(512)S(1)} %get-tuple-element.959) | copy-start | bytes 6148
  13.4 28.3 %copy-start.54 = (f32[512]{0:T(512)}, f32[512]{0:T(512)S(1)}, u32[]{:S(2)}) copy-start(f32[512]{0:T(512)S(1)} %get-tuple-element.960) | copy-start | bytes 6148
  14.6 27.1 copy-start.71
  14.7 27.1 copy-start.73
  14.7 27.1 copy-start.75
  14.7 27.1 copy-start.77
  14.7 27.1 copy-start.79
  14.7 27.1 copy-start.81
  332.2 47.2 %copy-start.45 = (f32[2048]{0:T(1024)S(1)}, f32[2048]{0:T(1024)}, u32[]{:S(2)}) copy-start(f32[2048]{0:T(1024)} %param.32) | copy-start | bytes 24580
  332.3 70.9 %all-gather.7.cloned.1.call-start = ((), (), s32[]{:S(2)}) async-start(), calls=%async_computation.6 | async-start | bytes 2621440 | tf_op jit(solution)/shard_map/all_gather | solution.py:293
  380.4 46.9 %all-gather.9.cloned.1.call-start = ((), (), s32[]{:S(2)}) async-start(), calls=%async_computation.8 | async-start | bytes 2621440 | tf_op jit(solution)/shard_map/all_gather | solution.py:306
  381.0 115.6 %reduce-scatter.9.cloned.1.call-start = ((), (), s32[]{:S(2)}) async-start(), calls=%async_computation.9 | async-start | bytes 5242880 | tf_op jit(solution)/shard_map/reduce_scatter | solution.py:315
  451.9 92.1 %reduce-scatter.7.cloned.1.call-start = ((), (), s32[]{:S(2)}) async-start(), calls=%async_computation.7 | async-start | bytes 5242880 | tf_op jit(solution)/shard_map/reduce_scatter | solution.py:298
  461.4 109.2 %all-gather.11.cloned.1.call-start = ((), (), s32[]{:S(2)}) async-start(), calls=%async_computation.10 | async-start | bytes 2621440 | tf_op jit(solution)/shard_map/all_gather | solution.py:318
  547.8 535.3 %reduce-scatter.11.cloned.1.call-start = ((), (), s32[]{:S(2)}) async-start(), calls=%async_computation.11 | async-start | bytes 5242880 | tf_op jit(solution)/shard_map/reduce_scatter | solution.py:379
  1003.5 1699.9 %all-reduce.25.cloned.1.call-start = ((), (), s32[]{:S(2)}) async-start(), calls=%async_computation.12 | async-start | bytes 111149056 | tf_op jit(solution)/shard_map/psum | solution.py:383
  1043.4 39.8 %copy-start.13 = (bf16[128,2048]{1,0:T(8,128)(2,1)S(1)}, bf16[128,2048]{1,0:T(8,128)(2,1)}, u32[]{:S(2)}) copy-start(bf16[128,2048]{1,0:T(8,128)(2,1)} %param.20) | copy-start | bytes 1572868
  1043.4 39.7 %copy-start.46 = (f32[2048]{0:T(1024)S(1)}, f32[2048]{0:T(1024)}, u32[]{:S(2)}) copy-start(f32[2048]{0:T(1024)} %param.23) | copy-start | bytes 24580
  1043.4 39.7 %copy-start.84 = (f32[128]{0:T(128)S(1)}, f32[128]{0:T(128)}, u32[]{:S(2)}) copy-start(f32[128]{0:T(128)} %copy-done.83) | copy-start | bytes 1540
  1043.5 84.5 %copy-start.87 = (f32[128]{0:T(128)S(1)}, f32[128]{0:T(128)}, u32[]{:S(2)}) copy-start(f32[128]{0:T(128)} %get-tuple-element.961) | copy-start | bytes 1540
  1083.2 44.8 %copy-start.29 = (f32[128,2048]{1,0:T(8,128)S(1)}, f32[128,2048]{1,0:T(8,128)}, u32[]{:S(2)}) copy-start(f32[128,2048]{1,0:T(8,128)} %reduce-scatter.11.cloned.1.call-done) | copy-start | bytes 3145732
  (82 other events, 313.9 us)
Sparse Core Ops, SparseCore 0:
  11.3 25.2 all-gather.4
  332.4 44.4 reduce-scatter.4
  380.6 22.5 all-gather.6
  404.7 22.5 all-gather.8
  452.1 44.4 reduce-scatter.8
  499.5 44.4 reduce-scatter.6
  548.0 22.5 all-gather.10
  1003.6 44.4 reduce-scatter.10
  1055.0 1648.3 all-reduce.24
where the time goes:
time: 2770 us; the launch traced here: 2760 us
  waiting for transfers between devices  1770 us (64%)
  other arithmetic  405 us (15%)
  matrix products  296 us (11%)
  local copies, waits for them, and re-layouts  191 us (7%)
  blocking collectives  82.4 us (3%)
    psum x1, waiting for transfers between devices, on_device(): summed_all = lax.psum(mixer_grads + (d_gate_w, d_up_w, d_down), 'dp')  1570 us
    another operation x40, other arithmetic, backward_step(): jax.scipy.linalg.solve_triangular(lower_mat, d_solved, trans=1, lower=Tru...  165 us
    another operation x5, other arithmetic, block_terms(): jax.scipy.linalg.solve_triangular(lower_mat, rate_blocks[..., None] * sta...  161 us
    unnamed x206, local copies, waits for them, and re-layouts  61.1 us
  transfers between devices with their start and end apart: 9, of which 8 were waited for; matrix products, arithmetic and copies ran while one was open for 3% of the time, Pallas kernels for 0%

commit v1 on v0

v1 whole, which is shorter than its diff:
```python
import functools

import jax
import jax.numpy as jnp
from jax import lax
from jax.experimental import pallas as pl
from jax.experimental.pallas import tpu as pltpu
from jax.sharding import PartitionSpec as P

DK = 128
CONV = 4
SPAN = 128
PAD = 8


EPS_NORM = 1e-06
EPS_UNIT = 1e-06
EPS_HEAD = 0.05
LOW = jnp.bfloat16
FULL = jnp.float32


def sigmoid(values):
    return 1.0 / (1.0 + jnp.exp(-values))


def parts_of(values):
    high = values.astype(LOW)
    return (high, (values - high.astype(FULL)).astype(LOW))


def product(left, right, left_dim=1, right_dim=0):
    dims = (((left_dim,), (right_dim,)), ((), ()))
    right_free = 1 - right_dim
    width = right[0].shape[right_free]
    if len(left) == 2:
        left_all = jnp.concatenate(left, axis=left_dim)
        first = jnp.concatenate([right[0], right[0]], axis=right_dim)
    else:
        left_all, first = left[0], right[0]
    if len(right) == 1:
        return lax.dot_general(left_all, first, dims, preferred_element_type=FULL)
    second = right[1]
    if len(left) == 2:
        second = jnp.concatenate([second, jnp.zeros_like(second)], axis=right_dim)
    both = lax.dot_general(
        left_all,
        jnp.concatenate([first, second], axis=right_free),
        dims,
        preferred_element_type=FULL,
    )
    return both[:, :width] + both[:, width:]


def lag_rows(stacked, lag_step):
    if lag_step == 0:
        return stacked[PAD:]
    return pltpu.roll(stacked, lag_step, axis=0)[PAD:]


def lead_rows(stacked, lag_step):
    rows = stacked.shape[0]
    if lag_step == 0:
        return stacked[: rows - PAD]
    return pltpu.roll(stacked, rows - lag_step, axis=0)[: rows - PAD]


def with_earlier(ref, start, columns):
    before = pl.multiple_of(jnp.maximum(start - PAD, 0), PAD)
    return jnp.concatenate(
        [ref[pl.ds(before, PAD), columns], ref[pl.ds(start, SPAN), columns]], axis=0
    )


def block_masks(meta_ref, ids_ref, start, index):
    ids_col = meta_ref[pl.ds(start, SPAN), 0:1]
    ids_row = ids_ref[pl.ds(index, 1), :]
    row_ids = lax.broadcasted_iota(jnp.int32, (SPAN, SPAN), 0)
    col_ids = lax.broadcasted_iota(jnp.int32, (SPAN, SPAN), 1)
    same = ids_col == ids_row
    strict = jnp.where(same & (row_ids > col_ids), 1.0, 0.0)
    inclusive = jnp.where(same & (row_ids >= col_ids), 1.0, 0.0)
    return strict, inclusive, row_ids, col_ids


def spread(meta_ref, start, column, rows=SPAN):
    return jnp.broadcast_to(meta_ref[pl.ds(start, rows), column : column + 1], (rows, DK))


def inverse_lower(lower, row_ids, col_ids):
    size = lower.shape[0]
    step = 1
    result = jnp.where(row_ids == col_ids, 1.0, 0.0)
    while step < size:
        pair = (row_ids // (2 * step) == col_ids // (2 * step)) & (
            row_ids // step != col_ids // step
        )
        link = jnp.where(pair, lower, 0.0)
        if step == 1:
            result = result - link
        else:
            result_parts = parts_of(result)
            inner = product(parts_of(link), result_parts)
            result = result - product(result_parts, parts_of(inner))
        step = 2 * step
    return result


def mixer_forward(
    head_count,
    query_ref,
    key_ref,
    value_ref,
    gate_ref,
    logit_ref,
    taps_ref,
    gain_ref,
    meta_ref,
    ids_ref,
    mixer_ref,
    conv_ref,
    solve_ref,
    w_ref,
    u_ref,
    new_ref,
    mixed_ref,
    states_ref,
    state,
):
    state[...] = jnp.zeros_like(state)
    gain = gain_ref[...]

    def step(index, carry):
        start = pl.multiple_of(index * SPAN, SPAN)
        rows = pl.ds(start, SPAN)
        strict, inclusive, row_ids, col_ids = block_masks(meta_ref, ids_ref, start, index)
        tap_masks = [None] + [spread(meta_ref, start, lag_step) for lag_step in range(1, CONV)]
        opening = spread(meta_ref, start, 4)
        closing = spread(meta_ref, start, 5)
        carried = spread(meta_ref, start, 6)
        betas = sigmoid(logit_ref[rows, :])
        for head in range(head_count):
            columns = slice(head * DK, (head + 1) * DK)
            acts = []
            for which, ref in enumerate((query_ref, key_ref, value_ref)):
                stacked = with_earlier(ref, start, columns)
                tap = 4 * which
                total = taps_ref[tap : tap + 1, columns] * lag_rows(stacked, 0)
                for lag_step in range(1, CONV):
                    total = total + (
                        taps_ref[tap + lag_step : tap + lag_step + 1, columns]
                        * lag_rows(stacked, lag_step)
                        * tap_masks[lag_step]
                    )
                conv_ref[which, rows, columns] = total
                acts.append(total * sigmoid(total))
            unit = [
                act * lax.rsqrt(jnp.sum(act * act, axis=-1, keepdims=True) + EPS_UNIT)
                for act in acts[:2]
            ]
            queries, keys, values = unit[0].astype(LOW), unit[1].astype(LOW), acts[2].astype(LOW)
            beta = jnp.broadcast_to(betas[:, head : head + 1], (SPAN, DK))
            gram = product((keys,), (keys,), 1, 1)
            solve = inverse_lower(beta * gram * strict, row_ids, col_ids)
            solve_ref[head, rows, :] = solve
            solve_parts = parts_of(solve)
            w_rows = product(solve_parts, parts_of(beta * keys.astype(FULL)))
            u_rows = product(solve_parts, parts_of(beta * values.astype(FULL)))
            w_ref[rows, columns] = w_rows
            u_ref[rows, columns] = u_rows
            probes = product((queries,), (keys,), 1, 1) * inclusive
            before = state[head]
            states_ref[head, rows, :] = before
            before_parts = parts_of(before)
            new_value = u_rows - opening * product(parts_of(w_rows), before_parts)
            new_ref[rows, columns] = new_value
            mixed = opening * product((queries,), before_parts) + product(
                parts_of(probes), parts_of(new_value)
            )
            mixed_ref[rows, columns] = mixed
            state[head] = carried * before + product(
                (keys,), parts_of(closing * new_value), 0, 0
            )
            scale = lax.rsqrt(jnp.mean(mixed * mixed, axis=-1, keepdims=True) + EPS_HEAD)
            gates = gate_ref[rows, columns]
            mixer_ref[rows, columns] = (mixed * scale * gain * (gates * sigmoid(gates))).astype(LOW)
        return carry

    lax.fori_loop(0, query_ref.shape[0] // SPAN, step, 0)


def mixer_backward(
    head_count,
    d_mixer_ref,
    query_ref,
    key_ref,
    value_ref,
    gate_ref,
    logit_ref,
    taps_ref,
    gain_ref,
    meta_ref,
    ids_ref,
    conv_ref,
    solve_ref,
    w_ref,
    u_ref,
    new_ref,
    mixed_ref,
    states_ref,
    d_query_ref,
    d_key_ref,
    d_value_ref,
    d_gate_ref,
    d_logit_ref,
    d_taps_ref,
    d_gain_ref,
    d_state,
    later,
):
    d_state[...] = jnp.zeros_like(d_state)
    later[...] = jnp.zeros_like(later)
    d_taps_ref[...] = jnp.zeros_like(d_taps_ref)
    d_gain_ref[...] = jnp.zeros_like(d_gain_ref)
    gain = gain_ref[...]
    total_rows = query_ref.shape[0]
    count = total_rows // SPAN

    def step(back, carry):
        index = count - 1 - back
        start = pl.multiple_of(index * SPAN, SPAN)
        rows = pl.ds(start, SPAN)
        strict, inclusive, row_ids, col_ids = block_masks(meta_ref, ids_ref, start, index)
        after = pl.multiple_of(jnp.minimum(start + SPAN, total_rows - PAD), PAD)
        tap_masks = [None] + [
            jnp.concatenate(
                [
                    spread(meta_ref, start, lag_step),
                    spread(meta_ref, after, lag_step, PAD),
                ],
                axis=0,
            )
            for lag_step in range(1, CONV)
        ]
        opening = spread(meta_ref, start, 4)
        closing = spread(meta_ref, start, 5)
        carried = spread(meta_ref, start, 6)
        betas = sigmoid(logit_ref[rows, :])
        lanes = lax.broadcasted_iota(jnp.int32, (SPAN, DK), 1)
        d_logits = jnp.zeros((SPAN, DK), FULL)
        d_gain = jnp.zeros((1, DK), FULL)
        for head in range(head_count):
            columns = slice(head * DK, (head + 1) * DK)
            d_mixer = d_mixer_ref[rows, columns]
            gates = gate_ref[rows, columns]
            logistic = sigmoid(gates)
            mixed = mixed_ref[rows, columns]
            scale = lax.rsqrt(jnp.mean(mixed * mixed, axis=-1, keepdims=True) + EPS_HEAD)
            unit_mixed = mixed * scale
            d_gate_ref[rows, columns] = (
                d_mixer * (unit_mixed * gain) * (logistic * (1.0 + gates * (1.0 - logistic)))
            ).astype(LOW)
            d_normed = d_mixer * (gates * logistic)
            d_gain = d_gain + jnp.sum(d_normed * unit_mixed, axis=0, keepdims=True)
            weighted = d_normed * gain
            inner = jnp.mean(weighted * mixed, axis=-1, keepdims=True)
            d_out = scale * weighted - mixed * (scale * scale * scale) * inner
            convs = [conv_ref[which, rows, columns] for which in range(3)]
            logistics = [sigmoid(conv) for conv in convs]
            acts = [conv * logistic for conv, logistic in zip(convs, logistics)]
            scales = [
                lax.rsqrt(jnp.sum(act * act, axis=-1, keepdims=True) + EPS_UNIT)
                for act in acts[:2]
            ]
            queries = (acts[0] * scales[0]).astype(LOW)
            keys = (acts[1] * scales[1]).astype(LOW)
            values = acts[2].astype(LOW)
            beta = jnp.broadcast_to(betas[:, head : head + 1], (SPAN, DK))
            gram = product((keys,), (keys,), 1, 1)
            probes = product((queries,), (keys,), 1, 1) * inclusive
            solve_parts = parts_of(solve_ref[head, rows, :])
            w_parts = parts_of(w_ref[rows, columns])
            u_parts = parts_of(u_ref[rows, columns])
            new_value = new_ref[rows, columns]
            new_parts = parts_of(new_value)
            before_parts = parts_of(states_ref[head, rows, :])
            d_after = d_state[head]
            d_after_parts = parts_of(d_after)
            d_out_parts = parts_of(d_out)
            d_new = product(parts_of(probes), d_out_parts, 0, 0) + closing * product(
                (keys,), d_after_parts
            )
            opened_out = opening * d_out
            opened_new = opening * d_new
            d_state[head] = (
                carried * d_after
                + product((queries,), parts_of(opened_out), 0, 0)
                - product(w_parts, parts_of(opened_new), 0, 0)
            )
            d_probe = product(d_out_parts, new_parts, 1, 1) * inclusive
            d_probe_parts = parts_of(d_probe)
            d_query = product(d_probe_parts, (keys,)) + product(
                parts_of(opened_out), before_parts, 1, 1
            )
            d_key = product(d_probe_parts, (queries,), 0, 0) + closing * product(
                new_parts, d_after_parts, 1, 1
            )
            d_w = -product(parts_of(opened_new), before_parts, 1, 1)
            right_w = product(solve_parts, parts_of(d_w), 0, 0)
            right_u = product(solve_parts, parts_of(d_new), 0, 0)
            d_lower = (
                -(
                    product(parts_of(right_w), w_parts, 1, 1)
                    + product(parts_of(right_u), u_parts, 1, 1)
                )
                * strict
            )
            d_beta = jnp.sum(
                right_w * keys.astype(FULL) + right_u * values.astype(FULL) + d_lower * gram,
                axis=-1,
                keepdims=True,
            )
            beta_col = betas[:, head : head + 1]
            d_logits = d_logits + jnp.where(
                lanes == head, d_beta * beta_col * (1.0 - beta_col), 0.0
            )
            d_gram_parts = parts_of(beta * d_lower)
            d_key = (
                d_key
                + beta * right_w
                + product(d_gram_parts, (keys,))
                + product(d_gram_parts, (keys,), 0, 0)
            )
            d_value = beta * right_u
            d_acts = [
                scales[which] * grads
                - acts[which]
                * (scales[which] * scales[which] * scales[which])
                * jnp.sum(grads * acts[which], axis=-1, keepdims=True)
                for which, grads in enumerate((d_query, d_key))
            ] + [d_value]
            for which, (ref, out_ref) in enumerate(
                ((query_ref, d_query_ref), (key_ref, d_key_ref), (value_ref, d_value_ref))
            ):
                logistic = logistics[which]
                d_conv = d_acts[which] * (logistic * (1.0 + convs[which] * (1.0 - logistic)))
                tap = 4 * which
                following = jnp.concatenate([d_conv, later[which, :, columns]], axis=0)
                earlier = with_earlier(ref, start, columns)
                later[which, :, columns] = d_conv[:PAD]
                total = taps_ref[tap : tap + 1, columns] * d_conv
                d_taps = [jnp.sum(d_conv * lag_rows(earlier, 0), axis=0, keepdims=True)]
                for lag_step in range(1, CONV):
                    masked = following * tap_masks[lag_step]
                    total = total + taps_ref[
                        tap + lag_step : tap + lag_step + 1, columns
                    ] * lead_rows(masked, lag_step)
                    d_taps.append(
                        jnp.sum(
                            masked[:SPAN] * lag_rows(earlier, lag_step), axis=0, keepdims=True
                        )
                    )
                out_ref[rows, columns] = total.astype(LOW)
                for lag_step in range(CONV):
                    place = slice(tap + lag_step, tap + lag_step + 1)
                    d_taps_ref[place, columns] = d_taps_ref[place, columns] + d_taps[lag_step]
        d_logit_ref[rows, :] = d_logits.astype(LOW)
        d_gain_ref[...] = d_gain_ref[...] + d_gain
        return carry

    lax.fori_loop(0, count, step, 0)


def whole_blocks(count):
    return [pl.BlockSpec(memory_space=pltpu.VMEM)] * count


def run_mixer_forward(projections, logits, taps, gain, meta, ids):
    rows, width = projections[0].shape
    head_count = width // DK
    tall = jax.ShapeDtypeStruct((rows, width), FULL)
    square = jax.ShapeDtypeStruct((head_count, rows, DK), FULL)
    return pl.pallas_call(
        functools.partial(mixer_forward, head_count),
        out_shape=(
            jax.ShapeDtypeStruct((rows, width), LOW),
            jax.ShapeDtypeStruct((3, rows, width), FULL),
            square,
            tall,
            tall,
            tall,
            tall,
            square,
        ),
        in_specs=whole_blocks(9),
        out_specs=tuple(whole_blocks(8)),
        scratch_shapes=[pltpu.VMEM((head_count, DK, DK), FULL)],
        compiler_params=pltpu.CompilerParams(vmem_limit_bytes=56 * 1024 * 1024),
        name="mixer_forward",
    )(*projections, logits, taps, gain, meta, ids)


def run_mixer_backward(d_mixer, projections, logits, taps, gain, meta, ids, kept):
    rows, width = projections[0].shape
    head_count = width // DK
    low = jax.ShapeDtypeStruct((rows, width), LOW)
    return pl.pallas_call(
        functools.partial(mixer_backward, head_count),
        out_shape=(
            low,
            low,
            low,
            low,
            jax.ShapeDtypeStruct((rows, DK), LOW),
            jax.ShapeDtypeStruct(taps.shape, FULL),
            jax.ShapeDtypeStruct((1, DK), FULL),
        ),
        in_specs=whole_blocks(17),
        out_specs=tuple(whole_blocks(7)),
        scratch_shapes=[
            pltpu.VMEM((head_count, DK, DK), FULL),
            pltpu.VMEM((3, PAD, width), FULL),
        ],
        compiler_params=pltpu.CompilerParams(vmem_limit_bytes=56 * 1024 * 1024),
        name="mixer_backward",
    )(d_mixer, *projections, logits, taps, gain, meta, ids, *kept)


def document_tables(doc_ids):
    rows = doc_ids.shape[0]
    columns = [doc_ids.astype(FULL)]
    for lag_step in range(1, CONV):
        before = jnp.concatenate(
            [jnp.full((lag_step,), -1, jnp.int32), doc_ids[: rows - lag_step]]
        )
        columns.append((doc_ids == before).astype(FULL))
    blocks = doc_ids.reshape(rows // SPAN, SPAN)
    prior = jnp.concatenate([jnp.full((1,), -1, jnp.int32), blocks[:-1, SPAN - 1]])[:, None]
    last = blocks[:, SPAN - 1 :]
    columns.append((blocks == prior).astype(FULL).reshape(-1))
    columns.append((blocks == last).astype(FULL).reshape(-1))
    columns.append(jnp.broadcast_to(last == prior, blocks.shape).astype(FULL).reshape(-1))
    columns.append(jnp.zeros((rows,), FULL))
    return jnp.stack(columns, axis=1), blocks.astype(FULL)


def by_pairs(values, bit):
    count = lax.axis_size("mp")
    return lax.ppermute(values, "mp", [(here, here ^ bit) for here in range(count)])


def gather_rows(values):
    if lax.axis_size("mp") != 4:
        return lax.all_gather(values, "mp", axis=0, tiled=True)
    here = lax.axis_index("mp")
    other_core = by_pairs(values, 1)
    other_chip = by_pairs(values, 2)
    far = by_pairs(other_chip, 1)
    odd_core, odd_chip = here % 2 == 1, here // 2 == 1
    near_pair = jnp.where(
        odd_core,
        jnp.concatenate([other_core, values]),
        jnp.concatenate([values, other_core]),
    )
    far_pair = jnp.where(
        odd_core, jnp.concatenate([far, other_chip]), jnp.concatenate([other_chip, far])
    )
    return jnp.where(
        odd_chip, jnp.concatenate([far_pair, near_pair]), jnp.concatenate([near_pair, far_pair])
    )


def scatter_sum(values):
    if lax.axis_size("mp") != 4:
        return lax.psum_scatter(values, "mp", scatter_dimension=0, tiled=True)
    here = lax.axis_index("mp")
    core, chip = here % 2, here // 2
    quarters = values.reshape(2, 2, values.shape[0] // 4, values.shape[1])
    sent = lax.dynamic_index_in_dim(quarters, 1 - core, 1, keepdims=False).astype(LOW)
    kept = lax.dynamic_index_in_dim(quarters, core, 1, keepdims=False)
    halves = kept + by_pairs(sent, 1).astype(FULL)
    sent = lax.dynamic_index_in_dim(halves, 1 - chip, 0, keepdims=False).astype(LOW)
    kept = lax.dynamic_index_in_dim(halves, chip, 0, keepdims=False)
    return kept + by_pairs(sent, 2).astype(FULL)


def inverse_root(values, epsilon):
    return lax.rsqrt(jnp.mean(values * values, axis=-1, keepdims=True) + epsilon)


def norm_back(values, scales, gains, grads):
    weighted = grads * gains
    inner_sum = jnp.mean(weighted * values, axis=-1, keepdims=True)
    return scales * weighted - values * (scales * scales * scales) * inner_sum


def sigmoid_linear(values):
    return values * sigmoid(values)


def sigmoid_slope(values):
    logistic = sigmoid(values)
    return logistic * (1.0 + values * (1.0 - logistic))


def doc_index(lengths, length):
    starts = jnp.cumsum(lengths, axis=1) - lengths
    places = jnp.arange(length, dtype=jnp.int32)
    within = jnp.sum((starts[:, :, None] <= places[None, None, :]).astype(jnp.int32), axis=1) - 1
    offsets = jnp.arange(lengths.shape[0], dtype=jnp.int32)[:, None] * lengths.shape[1]
    return (within + offsets).reshape(-1)


def dot_full(equation, left, right):
    return jnp.einsum(equation, left, right, preferred_element_type=FULL)


def on_device(
    inputs,
    doc_lengths,
    cotangent,
    norm_gain,
    query_weight,
    key_weight,
    value_weight,
    beta_weight,
    gating_weight,
    conv_weight,
    head_gain,
    output_weight,
    ffn_gain,
    gate_weight,
    up_weight,
    down_weight,
):
    local_rows = inputs.shape[0]
    group_rows = local_rows * lax.axis_size("mp")
    width = query_weight.shape[1]
    head_count = width // DK
    meta, ids = document_tables(doc_index(doc_lengths, group_rows // doc_lengths.shape[0]))
    taps = conv_weight.reshape(3 * CONV, width)
    gain_row = head_gain[None, :]

    residual_in = inputs.astype(FULL)
    scale_one = inverse_root(residual_in, EPS_NORM)
    normed = gather_rows((residual_in * scale_one * norm_gain).astype(LOW))
    grad_rows = gather_rows(cotangent)
    weights = (query_weight, key_weight, value_weight, gating_weight)
    projections = tuple(dot_full("td,df->tf", normed, weight) for weight in weights)
    logits = dot_full("td,df->tf", normed, beta_weight)
    mixer_low, *kept = run_mixer_forward(projections, logits, taps, gain_row, meta, ids)
    attended = scatter_sum(dot_full("tf,fd->td", mixer_low, output_weight))
    residual_mid = residual_in + attended
    scale_two = inverse_root(residual_mid, EPS_NORM)
    ffn_input = gather_rows((residual_mid * scale_two * ffn_gain).astype(LOW))

    gate_pre = dot_full("td,df->tf", ffn_input, gate_weight)
    up_pre = dot_full("td,df->tf", ffn_input, up_weight)
    d_hidden = dot_full("td,fd->tf", grad_rows, down_weight)
    gate_swish = sigmoid_linear(gate_pre)
    hidden_low = (gate_swish * up_pre).astype(LOW)
    d_gate_low = (d_hidden * up_pre * sigmoid_slope(gate_pre)).astype(LOW)
    d_up_low = (d_hidden * gate_swish).astype(LOW)
    d_ffn_norm = scatter_sum(
        dot_full("tf,df->td", d_gate_low, gate_weight) + dot_full("tf,df->td", d_up_low, up_weight)
    )
    ffn_out = scatter_sum(dot_full("tf,fd->td", hidden_low, down_weight))
    output = (residual_mid + ffn_out).astype(LOW)
    d_down = dot_full("tf,td->fd", hidden_low, grad_rows)
    d_gate_w = dot_full("td,tf->df", ffn_input, d_gate_low)
    d_up_w = dot_full("td,tf->df", ffn_input, d_up_low)

    d_mid = cotangent.astype(FULL) + norm_back(residual_mid, scale_two, ffn_gain, d_ffn_norm)
    ffn_gain_part = jnp.sum(d_ffn_norm * residual_mid * scale_two, axis=0)
    mid_rows = gather_rows(d_mid.astype(LOW))
    d_output_w = dot_full("tf,td->fd", mixer_low, mid_rows)
    d_mixer = dot_full("td,fd->tf", mid_rows, output_weight)
    *low_grads, d_logits, d_taps, head_gain_part = run_mixer_backward(
        d_mixer, projections, logits, taps, gain_row, meta, ids, kept
    )
    d_logits = d_logits[:, :head_count]
    summed = dot_full("tf,df->td", d_logits, beta_weight)
    for grads, weight in zip(low_grads, weights):
        summed = summed + dot_full("tf,df->td", grads, weight)
    d_normed = scatter_sum(summed)
    input_grad = d_mid + norm_back(residual_in, scale_one, norm_gain, d_normed)
    norm_gain_part = jnp.sum(d_normed * residual_in * scale_one, axis=0)
    proj_grads = [dot_full("td,tf->df", normed, grads).astype(LOW) for grads in low_grads]
    d_beta_w = dot_full("td,tf->df", normed, d_logits)

    gains = jnp.concatenate([norm_gain_part, ffn_gain_part, head_gain_part[0]])
    gains = lax.psum(gains, "mp")
    small = jnp.concatenate([d_beta_w.reshape(-1), d_taps.reshape(-1), gains])
    size = small.shape[0]
    padded = -(-size // (16 * 512)) * 16 * 512
    small = jnp.pad(small, (0, padded - size)).reshape(-1, 512).astype(LOW)
    wide = [grads.astype(LOW) for grads in (d_gate_w, d_up_w, d_down)]
    narrow = proj_grads + [d_output_w.astype(LOW), small]
    d_gate_w, d_up_w, d_down, *proj_grads, d_output_w, small = [
        grads.astype(FULL) for grads in lax.psum(tuple(wide + narrow), "dp")
    ]
    small = small.reshape(-1)
    beta_size, taps_size = d_beta_w.size, taps.size
    d_beta_w = small[:beta_size].reshape(d_beta_w.shape)
    d_conv = small[beta_size : beta_size + taps_size].reshape(conv_weight.shape)
    gains = small[beta_size + taps_size : size]
    features = inputs.shape[1]
    return (
        output,
        input_grad,
        gains[:features],
        proj_grads[0],
        proj_grads[1],
        proj_grads[2],
        d_beta_w,
        proj_grads[3],
        d_conv,
        gains[2 * features :],
        d_output_w,
        gains[features : 2 * features],
        d_gate_w,
        d_up_w,
        d_down,
    )


def solution(mesh):
    rows, columns = P(("dp", "mp"), None), P(None, "mp")
    return jax.shard_map(
        on_device,
        mesh=mesh,
        in_specs=(
            rows,
            P("dp", None),
            rows,
            P(),
            columns,
            columns,
            columns,
            columns,
            columns,
            P(None, None, "mp"),
            P(),
            P("mp", None),
            P(),
            columns,
            columns,
            P("mp", None),
        ),
        out_specs=(
            rows,
            rows,
            P(),
            columns,
            columns,
            columns,
            columns,
            columns,
            P(None, None, "mp"),
            P(),
            P("mp", None),
            P(),
            columns,
            columns,
            P("mp", None),
        ),
        check_vma=False,
    )
```

time: 2770 us -> 1160 us (0.42)
  waiting for transfers between devices: 1770 us -> 816 us
  other arithmetic: 405 us -> 56.1 us
  matrix products: 296 us -> 99.6 us
  local copies, waits for them, and re-layouts: 191 us -> 22.6 us
  Pallas kernels: 0 us -> 76 us
  blocking collectives: 82.4 us -> 52.9 us
    psum x1, waiting for transfers between devices: 1570 us -> 740 us  [on_device(): lax.psum(tuple(wide + narrow), 'dp')]
    another operation x49 -> x2, other arithmetic: 327 us -> 0.08 us  [the longest x1 0.08 us: document_tables(): return (jnp.stack(columns, axis=1), blocks.astype(FULL))]
    dot_general x165 -> x27, matrix products: 289 us -> 99.6 us  [dot_full(): return jnp.einsum(equation, left, right, preferred_element_type=FULL)]
    reduce_scatter x4 -> x0, waiting for transfers between devices: 125 us -> none  [the longest x1 45.7 us: on_device(): lax.psum_scatter(jnp.dot(hidden_low, down_weight, preferred_element_type=...]
    ppermute x0 -> x20, waiting for transfers between devices: none -> 76.4 us  [by_pairs(): lax.ppermute(values, 'mp', [(here, here ^ bit) for here in range(count)])]
    pallas_call x0 -> x2, Pallas kernels: none -> 76 us  [the longest x1 48.7 us: run_mixer_forward(): pl.pallas_call(functools.partial(mixer_forward, head_count), out_shape=(j...]
    all_gather x4 -> x0, waiting for transfers between devices: 67.5 us -> none  [the longest x1 22.1 us: on_device(): ffn_input = lax.all_gather(ffn_local, 'mp', axis=0, tiled=True)]
    unnamed x206 -> x103, local copies, waits for them, and re-layouts: 61.1 us -> 11.9 us
  transfers between devices with their start and end apart: 9 -> 21, of which waited for: 8 -> 10; matrix products, arithmetic and copies ran while one was open for 3% -> 6% of each run, Pallas kernels for 0% -> 0%
where the time goes in v1:
time: 1160 us
  waiting for transfers between devices  816 us (70%)
  matrix products  99.6 us (9%)
  Pallas kernels  76 us (7%)
  other arithmetic  56.1 us (5%)
  blocking collectives  52.9 us (5%)
  local copies, waits for them, and re-layouts  22.6 us (2%)
  starting transfers between devices  17.1 us (1%)
  between operations  15.2 us (1%)
    psum x1, waiting for transfers between devices, on_device(): lax.psum(tuple(wide + narrow), 'dp')  740 us
    dot_general x27, matrix products, dot_full(): return jnp.einsum(equation, left, right, preferred_element_type=FULL)  99.6 us
    ppermute x20, waiting for transfers between devices, by_pairs(): lax.ppermute(values, 'mp', [(here, here ^ bit) for here in range(count)])  76.4 us
    pallas_call x1, Pallas kernels, run_mixer_forward(): pl.pallas_call(functools.partial(mixer_forward, head_count), out_shape=(j...  48.7 us
    psum x1, blocking collectives, on_device(): lax.psum(tuple(wide + narrow), 'dp')  41.1 us
    convert_element_type x8, other arithmetic, on_device(): grads.astype(FULL)  32 us
    pallas_call x1, Pallas kernels, run_mixer_backward(): pl.pallas_call(functools.partial(mixer_backward, head_count), out_shape=(...  27.3 us
  transfers between devices with their start and end apart: 21, of which 10 were waited for; matrix products, arithmetic and copies ran while one was open for 6% of the time, Pallas kernels for 0%

profile of v1, /device:TPU:0, one launch (start us, length us, event | category | flops | bytes accessed | tf_op | source)
XLA Modules:
  0.0 1156.0 jit_solution(2738762949889918377)
XLA Ops:
  16.3 9.7 collective-permute-done
  44.4 48.7 %mixer_forward.1 = (bf16[512,512]{1,0:T(8,128)(2,1)}, f32[3,512,512]{2,1,0:T(8,128)}, f32[4,512,128]{2,1,0:T(8,128)}, f32[512,512]{1,0:T(8,128)}, f32[512,512]{1...) custom-call(f32[512,512]{1,0:T(8,128)} %fusion.40.query_ref, ...), custom_call_target="tpu_custom_call" | custom-call | tf_op jit(solution)/shard_map/mixer_forward/pallas_call | solution.py:383
  108.1 13.0 %collective-permute-done.4 = bf16[128,2048]{1,0:T(8,128)(2,1)} collective-permute-done((bf16[128,2048]{1,0:T(8,128)(2,1)}, bf16[128,2048]{1,0:T(8,128)(2,1)}, u32[]{:S(2)}, u32[]{:S(2)}) %collective-permute-start.4) | collective-permute-done | bytes 524320 | tf_op jit(solution)/shard_map/ppermute | solution.py:449
  125.0 7.3 collective-permute-done.10
  132.8 10.1 collective-permute-done.5
  152.3 9.6 multiply_convert_fusion
  161.9 6.0 fusion.46
  169.4 17.2 %fusion.47 = f32[512,2048]{1,0:T(8,128)S(1)} fusion(bf16[512,1408]{1,0:T(8,128)(2,1)S(1)} %copy-done.35, bf16[2048,1408]{1,0:T(8,128)(2,1)} %param.29), kind=kOutput, calls=%fused_computation.127 | convolution fusion | flops 2952790016 | bytes 11403264 | tf_op jit(solution)/shard_map/tf,df->td/dot_general | solution.py:515
  186.5 5.6 convolution_add_fusion
  197.4 5.3 convolution_convert_fusion.1
  202.7 15.7 %collective-permute-done.14 = bf16[128,2048]{1,0:T(8,128)(2,1)S(1)} collective-permute-done((bf16[128,2048]{1,0:T(8,128)(2,1)S(1)}, bf16[128,2048]{1,0:T(8,128)(2,1)S(1)}, u32[]{:S(2)}, u32[]{:S(2)}) %collective-permute-start.14) | collective-permute-done | bytes 524320 | tf_op jit(solution)/shard_map/ppermute | solution.py:449
  222.2 5.3 convolution_convert_fusion.2
  227.6 5.9 collective-permute-done.15
  233.5 5.0 convolution_convert_fusion
  244.1 27.3 %mixer_backward.1 = (bf16[512,512]{1,0:T(8,128)(2,1)}, bf16[512,512]{1,0:T(8,128)(2,1)}, bf16[512,512]{1,0:T(8,128)(2,1)}, bf16[512,512]{1,0:T(8,128)(2,1)}, bf1...) custom-call(f32[512,512]{1,0:T(8,128)} %fusion.21.d_mixer_ref, f32[512,512]{1,0:T(8,128)} %fusion.40.query_ref, ...), custom_call_target="tpu_custom_call" | custom-call | tf_op jit(solution)/shard_map/mixer_backward/pallas_call | solution.py:407
  271.4 3.7 convolution_convert_fusion.7
  302.2 9.6 collective-permute-done.19
  313.2 11.8 %psum.70 = bf16[4224]{0:T(1024)(128)(2,1)S(1)} all-reduce(f32[4224]{0:T(1024)S(1)} %pad_maximum_fusion), channel_id=1, replica_groups=mesh['dp'=8,'mp'=4] {'mp'}, use_global_device_ids=true, to_apply=%region_8.9 | all-reduce | flops 4224 | bytes 25344 | tf_op jit(solution)/shard_map/psum | solution.py:592
  325.0 41.1 %psum.71 = bf16[48,512]{1,0:T(8,128)(2,1)S(1)} all-reduce(bf16[48,512]{1,0:T(8,128)(2,1)S(1)} %convert_element_type.260), channel_id=1, replica_groups=mesh['dp'=8,'mp'=4] {'dp'}, use_global_device_ids=true, to_apply=%region_9.10 | all-reduce | flops 24576 | bytes 98304 | tf_op jit(solution)/shard_map/psum | solution.py:600
  375.7 740.1 %all-reduce.6.cloned.1.call-done = (bf16[2048,512]{1,0:T(8,128)(2,1)}, bf16[2048,512]{1,0:T(8,128)(2,1)}, bf16[2048,512]{1,0:T(8,128)(2,1)}, bf16[2048,512]{1,0:...) async-done(((bf16[2048,512]{1,0:T(8,128)(2,1)}, bf16[2048,512]{1,0:T(8,128)(2,1)}, ...) | async-done | bytes 27787280 | tf_op jit(solution)/shard_map/psum | solution.py:600
  1115.7 4.3 convert_element_type.263
  1131.8 5.7 convert_element_type.273
  1137.6 5.2 convert_element_type.275
  1142.8 6.0 convert_element_type.277
  (232 shorter events, 121.4 us)
Async XLA Ops:
  7.2 85.9 %copy-start = (bf16[512,2048]{1,0:T(8,128)(2,1)S(1)}, bf16[512,2048]{1,0:T(8,128)(2,1)}, u32[]{:S(2)}) copy-start(bf16[512,2048]{1,0:T(8,128)(2,1)} %param.27) | copy-start | bytes 6291460
  7.2 1108.5 %all-reduce.6.cloned.1.call-start = ((), (), s32[]{:S(2)}) async-start(), calls=%async_computation | async-start | bytes 55574528 | tf_op jit(solution)/shard_map/psum | solution.py:600
  10.4 18.4 %collective-permute-start.2 = (bf16[128,2048]{1,0:T(8,128)(2,1)S(1)}, bf16[128,2048]{1,0:T(8,128)(2,1)}, u32[]{:S(2)}, u32[]{:S(2)}) collective-permute-start(bf16[128,2048]{1,0:T(8,128)(2,1)S(1)} %fusion.7), channel_id=1, source_target_pairs={{0,1},{1,0},{2,3},{3,2},{4,5},{5,4},{6,7},{7,6},{8,9},{9,8},{10,11... | collective-permute-start | bytes 1572872 | tf_op jit(solution)/shard_map/ppermute | solution.py:449
  10.9 15.1 %collective-permute-start = (bf16[128,2048]{1,0:T(8,128)(2,1)S(1)}, bf16[128,2048]{1,0:T(8,128)(2,1)S(1)}, u32[]{:S(2)}, u32[]{:S(2)}) collective-permute-start(bf16[128,2048]{1,0:T(8,128)(2,1)S(1)} %fusion.7), channel_id=1, source_target_pairs={{0,2},{1,3},{2,0},{3,1},{4,6},{5,7},{6,4},{7,5},{8,10},{9,11},{10,... | collective-permute-start | bytes 1572872 | tf_op jit(solution)/shard_map/ppermute | solution.py:449
  26.0 4.3 collective-permute-start.1
  98.5 3.1 collective-permute-start.3
  106.0 15.1 %collective-permute-start.4 = (bf16[128,2048]{1,0:T(8,128)(2,1)}, bf16[128,2048]{1,0:T(8,128)(2,1)}, u32[]{:S(2)}, u32[]{:S(2)}) collective-permute-start(bf16[128,2048]{1,0:T(8,128)(2,1)} %fusion.16), channel_id=1, source_target_pairs={{0,2},{1,3},{2,0},{3,1},{4,6},{5,7},{6,4},{7,5},{8,10},{9,11},{10,... | collective-permute-start | bytes 1572872 | tf_op jit(solution)/shard_map/ppermute | solution.py:449
  107.8 24.5 %collective-permute-start.10 = (bf16[128,2048]{1,0:T(8,128)(2,1)S(1)}, bf16[128,2048]{1,0:T(8,128)(2,1)}, u32[]{:S(2)}, u32[]{:S(2)}) collective-permute-start(bf16[128,2048]{1,0:T(8,128)(2,1)S(1)} %copy-done.11), channel_id=1, source_target_pairs={{0,2},{1,3},{2,0},{3,1},{4,6},{5,7},{6,4},{7,5},{8,10},{9,11},{10,... | collective-permute-start | bytes 1572872 | tf_op jit(solution)/shard_map/ppermute | solution.py:449
  123.1 19.8 %collective-permute-start.5 = (bf16[128,2048]{1,0:T(8,128)(2,1)S(1)}, bf16[128,2048]{1,0:T(8,128)(2,1)S(1)}, u32[]{:S(2)}, u32[]{:S(2)}) collective-permute-start(bf16[128,2048]{1,0:T(8,128)(2,1)S(1)} %multiply_convert_fusion.3), channel_id=1, source_target_pairs={{0,2},{1,3},{2,0},{3,1},{4,6},{5,7},{6,4},{7,5},{8,10},{9,11},{10,... | collective-permute-start | bytes 1572872 | tf_op jit(solution)/shard_map/ppermute | solution.py:449
  125.0 18.0 %collective-permute-start.12 = (bf16[128,2048]{1,0:T(8,128)(2,1)S(1)}, bf16[128,2048]{1,0:T(8,128)(2,1)S(1)}, u32[]{:S(2)}, u32[]{:S(2)}) collective-permute-start(bf16[128,2048]{1,0:T(8,128)(2,1)S(1)} %copy-done.11), channel_id=1, source_target_pairs={{0,1},{1,0},{2,3},{3,2},{4,5},{5,4},{6,7},{7,6},{8,9},{9,8},{10,11... | collective-permute-start | bytes 1572872 | tf_op jit(solution)/shard_map/ppermute | solution.py:449
  132.3 10.9 collective-permute-start.11
  132.3 12.5 %collective-permute-start.7 = (bf16[128,2048]{1,0:T(8,128)(2,1)S(1)}, bf16[128,2048]{1,0:T(8,128)(2,1)S(1)}, u32[]{:S(2)}, u32[]{:S(2)}) collective-permute-start(bf16[128,2048]{1,0:T(8,128)(2,1)S(1)} %multiply_convert_fusion.3), channel_id=1, source_target_pairs={{0,1},{1,0},{2,3},{3,2},{4,5},{5,4},{6,7},{7,6},{8,9},{9,8},{10,11... | collective-permute-start | bytes 1572872 | tf_op jit(solution)/shard_map/ppermute | solution.py:449
  142.9 2.2 collective-permute-start.6
  168.2 24.7 %collective-permute-start.8 = (bf16[2,128,2048]{2,1,0:T(8,128)(2,1)S(1)}, bf16[2,128,2048]{2,1,0:T(8,128)(2,1)S(1)}, u32[]{:S(2)}, u32[]{:S(2)}) collective-permute-start(bf16[2,128,2048]{2,1,0:T(8,128)(2,1)S(1)} %fusion.3), channel_id=1, source_target_pairs={{0,1},{1,0},{2,3},{3,2},{4,5},{5,4},{6,7},{7,6},{8,9},{9,8},{10,11... | collective-permute-start | bytes 3145736 | tf_op jit(solution)/shard_map/ppermute | solution.py:449
  192.3 2.9 collective-permute-start.13
  193.3 25.5 %collective-permute-start.9 = (bf16[128,2048]{1,0:T(8,128)(2,1)S(1)}, bf16[128,2048]{1,0:T(8,128)(2,1)S(1)}, u32[]{:S(2)}, u32[]{:S(2)}) collective-permute-start(bf16[128,2048]{1,0:T(8,128)(2,1)S(1)} %fusion.17), channel_id=1, source_target_pairs={{0,2},{1,3},{2,0},{3,1},{4,6},{5,7},{6,4},{7,5},{8,10},{9,11},{10,... | collective-permute-start | bytes 1572872 | tf_op jit(solution)/shard_map/ppermute | solution.py:449
  195.6 22.9 %collective-permute-start.14 = (bf16[128,2048]{1,0:T(8,128)(2,1)S(1)}, bf16[128,2048]{1,0:T(8,128)(2,1)S(1)}, u32[]{:S(2)}, u32[]{:S(2)}) collective-permute-start(bf16[128,2048]{1,0:T(8,128)(2,1)S(1)} %fusion.18), channel_id=1, source_target_pairs={{0,2},{1,3},{2,0},{3,1},{4,6},{5,7},{6,4},{7,5},{8,10},{9,11},{10,... | collective-permute-start | bytes 1572872 | tf_op jit(solution)/shard_map/ppermute | solution.py:449
  220.5 13.0 %collective-permute-start.15 = (bf16[128,2048]{1,0:T(8,128)(2,1)S(1)}, bf16[128,2048]{1,0:T(8,128)(2,1)S(1)}, u32[]{:S(2)}, u32[]{:S(2)}) collective-permute-start(bf16[128,2048]{1,0:T(8,128)(2,1)S(1)} %get-tuple-element.102), channel_id=1, source_target_pairs={{0,2},{1,3},{2,0},{3,1},{4,6},{5,7},{6,4},{7,5},{8,10},{9,11},{10,... | collective-permute-start | bytes 1572872 | tf_op jit(solution)/shard_map/ppermute | solution.py:449
  227.6 11.0 collective-permute-start.17
  233.5 5.3 collective-permute-start.16
  244.1 27.3 %copy-start.5 = (bf16[512,2048]{1,0:T(8,128)(2,1)S(1)}, bf16[512,2048]{1,0:T(8,128)(2,1)}, u32[]{:S(2)}) copy-start(bf16[512,2048]{1,0:T(8,128)(2,1)} %copy-done.4) | copy-start | bytes 6291460
  293.0 3.0 collective-permute-start.18
  297.2 14.5 %collective-permute-start.19 = (bf16[128,2048]{1,0:T(8,128)(2,1)}, bf16[128,2048]{1,0:T(8,128)(2,1)}, u32[]{:S(2)}, u32[]{:S(2)}) collective-permute-start(bf16[128,2048]{1,0:T(8,128)(2,1)} %fusion.19), channel_id=1, source_target_pairs={{0,2},{1,3},{2,0},{3,1},{4,6},{5,7},{6,4},{7,5},{8,10},{9,11},{10,... | collective-permute-start | bytes 1572872 | tf_op jit(solution)/shard_map/ppermute | solution.py:449
  313.2 59.6 %copy-start.32 = (f32[128]{0:T(128)S(1)}, f32[128]{0:T(128)}, u32[]{:S(2)}) copy-start(f32[128]{0:T(128)} %get-tuple-element.122) | copy-start | bytes 1540
  (46 other events, 293.3 us)
Sparse Core Ops, SparseCore 0:
  283.1 832.5 all-reduce.5

commit v2 on v1

--- a/solution.py
+++ b/solution.py
@@ -11,6 +11,7 @@
 CONV = 4
 SPAN = 128
 PAD = 8
+ROWS_MOST = 8192
 
 
 EPS_NORM = 1e-06
@@ -515,6 +516,28 @@
     return jnp.einsum(equation, left, right, preferred_element_type=FULL)
 
 
+def ffn_terms(rows, grad_rows, gate_weight, up_weight, down_weight):
+    gate_pre = dot_full("td,df->tf", rows, gate_weight)
+    up_pre = dot_full("td,df->tf", rows, up_weight)
+    d_hidden = dot_full("td,fd->tf", grad_rows, down_weight)
+    gate_swish = sigmoid_linear(gate_pre)
+    hidden_low = (gate_swish * up_pre).astype(LOW)
+    d_gate_low = (d_hidden * up_pre * sigmoid_slope(gate_pre)).astype(LOW)
+    d_up_low = (d_hidden * gate_swish).astype(LOW)
+    return hidden_low, d_gate_low, d_up_low
+
+
+def ffn_grads(rows, grad_rows, gate_weight, up_weight, down_weight):
+    hidden_low, d_gate_low, d_up_low = ffn_terms(
+        rows, grad_rows, gate_weight, up_weight, down_weight
+    )
+    return (
+        dot_full("td,tf->df", rows, d_gate_low),
+        dot_full("td,tf->df", rows, d_up_low),
+        dot_full("tf,td->fd", hidden_low, grad_rows),
+    )
+
+
 def on_device(
     inputs,
     doc_lengths,
@@ -541,6 +564,9 @@
     taps = conv_weight.reshape(3 * CONV, width)
     gain_row = head_gain[None, :]
 
+    everyone = group_rows * lax.axis_size("dp") <= ROWS_MOST
+    if everyone:
+        all_grad_rows = lax.all_gather(cotangent, ("dp", "mp"), axis=0, tiled=True)
     residual_in = inputs.astype(FULL)
     scale_one = inverse_root(residual_in, EPS_NORM)
     normed = gather_rows((residual_in * scale_one * norm_gain).astype(LOW))
@@ -552,23 +578,26 @@
     attended = scatter_sum(dot_full("tf,fd->td", mixer_low, output_weight))
     residual_mid = residual_in + attended
     scale_two = inverse_root(residual_mid, EPS_NORM)
-    ffn_input = gather_rows((residual_mid * scale_two * ffn_gain).astype(LOW))
-
-    gate_pre = dot_full("td,df->tf", ffn_input, gate_weight)
-    up_pre = dot_full("td,df->tf", ffn_input, up_weight)
-    d_hidden = dot_full("td,fd->tf", grad_rows, down_weight)
-    gate_swish = sigmoid_linear(gate_pre)
-    hidden_low = (gate_swish * up_pre).astype(LOW)
-    d_gate_low = (d_hidden * up_pre * sigmoid_slope(gate_pre)).astype(LOW)
-    d_up_low = (d_hidden * gate_swish).astype(LOW)
+    ffn_local = (residual_mid * scale_two * ffn_gain).astype(LOW)
+    ffn_input = gather_rows(ffn_local)
+    if everyone:
+        all_ffn_input = lax.all_gather(ffn_local, ("dp", "mp"), axis=0, tiled=True)
+
+    hidden_low, d_gate_low, d_up_low = ffn_terms(
+        ffn_input, grad_rows, gate_weight, up_weight, down_weight
+    )
     d_ffn_norm = scatter_sum(
         dot_full("tf,df->td", d_gate_low, gate_weight) + dot_full("tf,df->td", d_up_low, up_weight)
     )
     ffn_out = scatter_sum(dot_full("tf,fd->td", hidden_low, down_weight))
     output = (residual_mid + ffn_out).astype(LOW)
-    d_down = dot_full("tf,td->fd", hidden_low, grad_rows)
-    d_gate_w = dot_full("td,tf->df", ffn_input, d_gate_low)
-    d_up_w = dot_full("td,tf->df", ffn_input, d_up_low)
+    d_ffn = None
+    if not everyone:
+        d_ffn = (
+            dot_full("td,tf->df", ffn_input, d_gate_low),
+            dot_full("td,tf->df", ffn_input, d_up_low),
+            dot_full("tf,td->fd", hidden_low, grad_rows),
+        )
 
     d_mid = cotangent.astype(FULL) + norm_back(residual_mid, scale_two, ffn_gain, d_ffn_norm)
     ffn_gain_part = jnp.sum(d_ffn_norm * residual_mid * scale_two, axis=0)
@@ -594,10 +623,14 @@
     size = small.shape[0]
     padded = -(-size // (16 * 512)) * 16 * 512
     small = jnp.pad(small, (0, padded - size)).reshape(-1, 512).astype(LOW)
-    wide = [grads.astype(LOW) for grads in (d_gate_w, d_up_w, d_down)]
-    narrow = proj_grads + [d_output_w.astype(LOW), small]
-    d_gate_w, d_up_w, d_down, *proj_grads, d_output_w, small = [
-        grads.astype(FULL) for grads in lax.psum(tuple(wide + narrow), "dp")
+    if everyone:
+        d_ffn = ffn_grads(all_ffn_input, all_grad_rows, gate_weight, up_weight, down_weight)
+    else:
+        d_ffn = [grads.astype(FULL) for grads in lax.psum([d.astype(LOW) for d in d_ffn], "dp")]
+    d_gate_w, d_up_w, d_down = d_ffn
+    *proj_grads, d_output_w, small = [
+        grads.astype(FULL)
+        for grads in lax.psum(proj_grads + [d_output_w.astype(LOW), small], "dp")
     ]
     small = small.reshape(-1)
     beta_size, taps_size = d_beta_w.size, taps.size

time: 1160 us -> 957 us (0.82)
  waiting for transfers between devices: 816 us -> 439 us
  matrix products: 99.6 us -> 290 us
  other arithmetic: 56.1 us -> 42.7 us
    psum x1, waiting for transfers between devices: 740 us -> 353 us  [on_device(): lax.psum(proj_grads + [d_output_w.astype(LOW), small], 'dp')]
    dot_general x27 -> x30, matrix products: 99.6 us -> 290 us  [dot_full(): return jnp.einsum(equation, left, right, preferred_element_type=FULL)]
    convert_element_type x8 -> x5, other arithmetic: 32 us -> 14.7 us  [on_device(): grads.astype(FULL)]
  transfers between devices with their start and end apart: 21 -> 23, of which waited for: 10 -> 13; matrix products, arithmetic and copies ran while one was open for 6% -> 10% of each run, Pallas kernels for 0% -> 0%
where the time goes in v2:
time: 957 us; the launch traced here: 949 us
  waiting for transfers between devices  439 us (46%)
  matrix products  290 us (30%)
  Pallas kernels  76.1 us (8%)
  blocking collectives  51.6 us (5%)
  other arithmetic  42.7 us (4%)
  starting transfers between devices  16.8 us (2%)
  between operations  16.7 us (2%)
  local copies, waits for them, and re-layouts  15.6 us (2%)
    psum x1, waiting for transfers between devices, on_device(): lax.psum(proj_grads + [d_output_w.astype(LOW), small], 'dp')  353 us
    dot_general x30, matrix products, dot_full(): return jnp.einsum(equation, left, right, preferred_element_type=FULL)  290 us
    ppermute x20, waiting for transfers between devices, by_pairs(): lax.ppermute(values, 'mp', [(here, here ^ bit) for here in range(count)])  85.1 us
    pallas_call x1, Pallas kernels, run_mixer_forward(): pl.pallas_call(functools.partial(mixer_forward, head_count), out_shape=(j...  48.7 us
    psum x1, blocking collectives, on_device(): lax.psum(proj_grads + [d_output_w.astype(LOW), small], 'dp')  40.5 us
    pallas_call x1, Pallas kernels, run_mixer_backward(): pl.pallas_call(functools.partial(mixer_backward, head_count), out_shape=(...  27.4 us
  transfers between devices with their start and end apart: 23, of which 13 were waited for; matrix products, arithmetic and copies ran while one was open for 10% of the time, Pallas kernels for 0%

profile of v2, /device:TPU:0, one launch (start us, length us, event | category | flops | bytes accessed | tf_op | source)
XLA Modules:
  0.0 948.5 jit_solution(14660833756630193300)
XLA Ops:
  16.6 9.7 %collective-permute-done = bf16[128,2048]{1,0:T(8,128)(2,1)S(1)} collective-permute-done((bf16[128,2048]{1,0:T(8,128)(2,1)S(1)}, bf16[128,2048]{1,0:T(8,128)(2,1)S(1)}, u32[]{:S(2)}, u32[]{:S(2)}) %collective-permute-start) | collective-permute-done | bytes 524320 | tf_op jit(solution)/shard_map/ppermute | solution.py:450
  43.6 48.7 %mixer_forward.1 = (bf16[512,512]{1,0:T(8,128)(2,1)}, f32[3,512,512]{2,1,0:T(8,128)}, f32[4,512,128]{2,1,0:T(8,128)}, f32[512,512]{1,0:T(8,128)}, f32[512,512]{1...) custom-call(f32[512,512]{1,0:T(8,128)} %fusion.64.query_ref, ...), custom_call_target="tpu_custom_call" | custom-call | tf_op jit(solution)/shard_map/mixer_forward/pallas_call | solution.py:384
  105.3 7.2 collective-permute-done.10
  112.4 10.4 %collective-permute-done.4 = bf16[128,2048]{1,0:T(8,128)(2,1)} collective-permute-done((bf16[128,2048]{1,0:T(8,128)(2,1)S(1)}, bf16[128,2048]{1,0:T(8,128)(2,1)}, u32[]{:S(2)}, u32[]{:S(2)}) %collective-permute-start.4) | collective-permute-done | bytes 524320 | tf_op jit(solution)/shard_map/ppermute | solution.py:450
  131.5 7.5 collective-permute-done.5
  139.0 6.1 fusion.7
  145.7 5.0 fusion.39
  155.8 9.4 fusion.15
  165.2 7.3 convolution_add_fusion
  173.2 5.4 fusion.14
  183.6 10.5 %collective-permute-done.14 = bf16[128,2048]{1,0:T(8,128)(2,1)S(1)} collective-permute-done((bf16[128,2048]{1,0:T(8,128)(2,1)S(1)}, bf16[128,2048]{1,0:T(8,128)(2,1)S(1)}, u32[]{:S(2)}, u32[]{:S(2)}) %collective-permute-start.14) | collective-permute-done | bytes 524320 | tf_op jit(solution)/shard_map/ppermute | solution.py:450
  194.4 10.4 %collective-permute-done.9 = bf16[128,2048]{1,0:T(8,128)(2,1)S(1)} collective-permute-done((bf16[128,2048]{1,0:T(8,128)(2,1)S(1)}, bf16[128,2048]{1,0:T(8,128)(2,1)S(1)}, u32[]{:S(2)}, u32[]{:S(2)}) %collective-permute-start.9) | collective-permute-done | bytes 524320 | tf_op jit(solution)/shard_map/ppermute | solution.py:450
  209.2 11.9 %collective-permute-done.15 = bf16[128,2048]{1,0:T(8,128)(2,1)S(1)} collective-permute-done((bf16[128,2048]{1,0:T(8,128)(2,1)S(1)}, bf16[128,2048]{1,0:T(8,128)(2,1)S(1)}, u32[]{:S(2)}, u32[]{:S(2)}) %collective-permute-start.15) | collective-permute-done | bytes 524320 | tf_op jit(solution)/shard_map/ppermute | solution.py:450
  228.3 27.4 %mixer_backward.1 = (bf16[512,512]{1,0:T(8,128)(2,1)}, bf16[512,512]{1,0:T(8,128)(2,1)}, bf16[512,512]{1,0:T(8,128)(2,1)}, bf16[512,512]{1,0:T(8,128)(2,1)}, bf1...) custom-call(f32[512,512]{1,0:T(8,128)} %fusion.40.d_mixer_ref, f32[512,512]{1,0:T(8,128)} %fusion.64.query_ref, ...), custom_call_target="tpu_custom_call" | custom-call | tf_op jit(solution)/shard_map/mixer_backward/pallas_call | solution.py:408
  286.7 12.1 %collective-permute-done.19 = bf16[128,2048]{1,0:T(8,128)(2,1)S(1)} collective-permute-done((bf16[128,2048]{1,0:T(8,128)(2,1)S(1)}, bf16[128,2048]{1,0:T(8,128)(2,1)S(1)}, u32[]{:S(2)}, u32[]{:S(2)}) %collective-permute-start.19) | collective-permute-done | bytes 524320 | tf_op jit(solution)/shard_map/ppermute | solution.py:450
  300.7 11.1 %psum.49 = bf16[4224]{0:T(1024)(128)(2,1)S(1)} all-reduce(f32[4224]{0:T(1024)S(1)} %pad_maximum_fusion), channel_id=1, replica_groups=mesh['dp'=8,'mp'=4] {'mp'}, use_global_device_ids=true, to_apply=%region_8.9 | all-reduce | flops 4224 | bytes 25344 | tf_op jit(solution)/shard_map/psum | solution.py:621
  311.8 40.5 %psum.50 = bf16[48,512]{1,0:T(8,128)(2,1)S(1)} all-reduce(bf16[48,512]{1,0:T(8,128)(2,1)S(1)} %convert_element_type.251), channel_id=1, replica_groups=mesh['dp'=8,'mp'=4] {'dp'}, use_global_device_ids=true, to_apply=%region_9.10 | all-reduce | flops 24576 | bytes 98304 | tf_op jit(solution)/shard_map/psum | solution.py:633
  359.7 353.2 %all-reduce.6.cloned.1.call-done = (bf16[2048,512]{1,0:T(8,128)(2,1)}, bf16[2048,512]{1,0:T(8,128)(2,1)}, bf16[2048,512]{1,0:T(8,128)(2,1)}, bf16[2048,512]{1,0:T(8,128)(2,1)}, bf16[512,2048]{1,0:T(8,128)(2,1)}) async-done(((bf16[2048,512]{1,0:T(8,128)(2,1)}, bf16[2048,512]{1,0:T(8,128)(2,1)}, bf16[2048,512]{1,0:T(8,128)(2,1)}, bf16[2048,512]{1,0:T(8,128)(2,1)}, bf16[512,2048]{1,0:T(8,128)(2,1)}), ...) | async-done | bytes 10485776 | tf_op jit(solution)/shard_map/psum | solution.py:633
  727.6 33.5 %fusion.74 = f32[4096,1408]{1,0:T(8,128)} fusion(bf16[4096,2048]{1,0:T(8,128)(2,1)} %all-gather.5.cloned.1.call-done, bf16[1408,2048]{1,0:T(8,128)(2,1)} %param.31), kind=kOutput, calls=%fused_computation.151 | convolution fusion | flops 23622320128 | bytes 45613056 | tf_op jit(solution)/shard_map/td,fd->tf/dot_general | solution.py:516
  761.1 33.1 %fusion.76 = f32[4096,1408]{1,0:T(8,128)} fusion(bf16[4096,2048]{1,0:T(8,128)(2,1)} %all-gather.3.cloned.1.call-done, bf16[2048,1408]{1,0:T(8,128)(2,1)} %param.29), kind=kOutput, calls=%fused_computation.153 | convolution fusion | flops 23622320128 | bytes 45613056 | tf_op jit(solution)/shard_map/td,df->tf/dot_general | solution.py:516
  794.2 31.7 %fusion.75 = f32[4096,1408]{1,0:T(8,128)} fusion(bf16[4096,2048]{1,0:T(8,128)(2,1)S(1)} %copy-done.34, bf16[2048,1408]{1,0:T(8,128)(2,1)} %param.30), kind=kOutput, calls=%fused_computation.152 | convolution fusion | flops 23622320128 | bytes 45613056 | tf_op jit(solution)/shard_map/td,df->tf/dot_general | solution.py:516
  825.9 36.6 %fusion.2 = f32[1408,2048]{1,0:T(8,128)} fusion(bf16[4096,2048]{1,0:T(8,128)(2,1)} %all-gather.5.cloned.1.call-done, f32[4096,1408]{1,0:T(8,128)} %fusion.75, f32[4096,1408]{1,0:T(8,128)} %fusion.76), kind=kOutput, calls=%fused_computation.6 | convolution fusion | flops 23656923136 | bytes 74448896 | tf_op jit(solution)/shard_map/tf,td->fd/dot_general | solution.py:516
  862.5 40.0 %fusion.3 = f32[2048,1408]{1,0:T(8,128)} fusion(bf16[4096,2048]{1,0:T(8,128)(2,1)} %all-gather.3.cloned.1.call-done, f32[4096,1408]{1,0:T(8,128)} %fusion.76, f32[4096,1408]{1,0:T(8,128)} %fusion.74, f32[4096,1408]{1,0:T(8,128)} %fusion.75), kind=kOutput, calls=%fused_computation.7 | convolution fusion | flops 23679991808 | bytes 97517568 | tf_op jit(solution)/shard_map/td,tf->df/dot_general | solution.py:516
  902.5 38.1 %fusion.1 = f32[2048,1408]{1,0:T(8,128)} fusion(bf16[4096,2048]{1,0:T(8,128)(2,1)} %all-gather.3.cloned.1.call-done, f32[4096,1408]{1,0:T(8,128)} %fusion.74, f32[4096,1408]{1,0:T(8,128)} %fusion.76), kind=kOutput, calls=%fused_computation.5 | convolution fusion | flops 23656923136 | bytes 74448896 | tf_op jit(solution)/shard_map/td,tf->df/dot_general | solution.py:516
  (224 shorter events, 125.2 us)
Async XLA Ops:
  8.0 84.3 %copy-start = (bf16[512,2048]{1,0:T(8,128)(2,1)S(1)}, bf16[512,2048]{1,0:T(8,128)(2,1)}, u32[]{:S(2)}) copy-start(bf16[512,2048]{1,0:T(8,128)(2,1)} %param.27) | copy-start | bytes 6291460
  8.0 704.8 %all-reduce.6.cloned.1.call-start = ((), (), s32[]{:S(2)}) async-start(), calls=%async_computation.2 | async-start | bytes 20971520 | tf_op jit(solution)/shard_map/psum | solution.py:633
  10.7 18.4 %collective-permute-start.2 = (bf16[128,2048]{1,0:T(8,128)(2,1)S(1)}, bf16[128,2048]{1,0:T(8,128)(2,1)}, u32[]{:S(2)}, u32[]{:S(2)}) collective-permute-start(bf16[128,2048]{1,0:T(8,128)(2,1)S(1)} %fusion.23), channel_id=1, source_target_pairs={{0,1},{1,0},{2,3},{3,2},{4,5},{5,4},{6,7},{7,6},{8,9},{9,8},{10,11... | collective-permute-start | bytes 1572872 | tf_op jit(solution)/shard_map/ppermute | solution.py:450
  11.2 15.1 %collective-permute-start = (bf16[128,2048]{1,0:T(8,128)(2,1)S(1)}, bf16[128,2048]{1,0:T(8,128)(2,1)S(1)}, u32[]{:S(2)}, u32[]{:S(2)}) collective-permute-start(bf16[128,2048]{1,0:T(8,128)(2,1)S(1)} %fusion.23), channel_id=1, source_target_pairs={{0,2},{1,3},{2,0},{3,1},{4,6},{5,7},{6,4},{7,5},{8,10},{9,11},{10,... | collective-permute-start | bytes 1572872 | tf_op jit(solution)/shard_map/ppermute | solution.py:450
  26.3 4.3 collective-permute-start.1
  96.8 3.0 collective-permute-start.3
  97.4 15.1 %collective-permute-start.10 = (bf16[128,2048]{1,0:T(8,128)(2,1)}, bf16[128,2048]{1,0:T(8,128)(2,1)}, u32[]{:S(2)}, u32[]{:S(2)}) collective-permute-start(bf16[128,2048]{1,0:T(8,128)(2,1)} %param.18), channel_id=1, source_target_pairs={{0,2},{1,3},{2,0},{3,1},{4,6},{5,7},{6,4},{7,5},{8,10},{9,11},{10,... | collective-permute-start | bytes 1572872 | tf_op jit(solution)/shard_map/ppermute | solution.py:450
  103.3 19.5 %collective-permute-start.4 = (bf16[128,2048]{1,0:T(8,128)(2,1)S(1)}, bf16[128,2048]{1,0:T(8,128)(2,1)}, u32[]{:S(2)}, u32[]{:S(2)}) collective-permute-start(bf16[128,2048]{1,0:T(8,128)(2,1)S(1)} %fusion.32), channel_id=1, source_target_pairs={{0,2},{1,3},{2,0},{3,1},{4,6},{5,7},{6,4},{7,5},{8,10},{9,11},{10,... | collective-permute-start | bytes 1572872 | tf_op jit(solution)/shard_map/ppermute | solution.py:450
  105.2 22.2 %collective-permute-start.12 = (bf16[128,2048]{1,0:T(8,128)(2,1)}, bf16[128,2048]{1,0:T(8,128)(2,1)}, u32[]{:S(2)}, u32[]{:S(2)}) collective-permute-start(bf16[128,2048]{1,0:T(8,128)(2,1)} %param.18), channel_id=1, source_target_pairs={{0,1},{1,0},{2,3},{3,2},{4,5},{5,4},{6,7},{7,6},{8,9},{9,8},{10,11... | collective-permute-start | bytes 1572872 | tf_op jit(solution)/shard_map/ppermute | solution.py:450
  112.4 16.9 %collective-permute-start.11 = (bf16[128,2048]{1,0:T(8,128)(2,1)}, bf16[128,2048]{1,0:T(8,128)(2,1)}, u32[]{:S(2)}, u32[]{:S(2)}) collective-permute-start(bf16[128,2048]{1,0:T(8,128)(2,1)} %collective-permute-done.10), channel_id=1, source_target_pairs={{0,1},{1,0},{2,3},{3,2},{4,5},{5,4},{6,7},{7,6},{8,9},{9,8},{10,11... | collective-permute-start | bytes 1572872 | tf_op jit(solution)/shard_map/ppermute | solution.py:450
  125.7 13.3 %collective-permute-start.5 = (bf16[128,2048]{1,0:T(8,128)(2,1)}, bf16[128,2048]{1,0:T(8,128)(2,1)S(1)}, u32[]{:S(2)}, u32[]{:S(2)}) collective-permute-start(bf16[128,2048]{1,0:T(8,128)(2,1)} %multiply_convert_fusion.12), channel_id=1, source_target_pairs={{0,2},{1,3},{2,0},{3,1},{4,6},{5,7},{6,4},{7,5},{8,10},{9,11},{10,... | collective-permute-start | bytes 1572872 | tf_op jit(solution)/shard_map/ppermute | solution.py:450
  131.5 13.6 %collective-permute-start.7 = (bf16[128,2048]{1,0:T(8,128)(2,1)S(1)}, bf16[128,2048]{1,0:T(8,128)(2,1)S(1)}, u32[]{:S(2)}, u32[]{:S(2)}) collective-permute-start(bf16[128,2048]{1,0:T(8,128)(2,1)S(1)} %copy-done.8), channel_id=1, source_target_pairs={{0,1},{1,0},{2,3},{3,2},{4,5},{5,4},{6,7},{7,6},{8,9},{9,8},{10,11... | collective-permute-start | bytes 1572872 | tf_op jit(solution)/shard_map/ppermute | solution.py:450
  139.0 6.4 collective-permute-start.6
  172.6 6.2 collective-permute-start.13
  178.8 2.7 collective-permute-start.8
  179.2 14.8 %collective-permute-start.14 = (bf16[128,2048]{1,0:T(8,128)(2,1)S(1)}, bf16[128,2048]{1,0:T(8,128)(2,1)S(1)}, u32[]{:S(2)}, u32[]{:S(2)}) collective-permute-start(bf16[128,2048]{1,0:T(8,128)(2,1)S(1)} %fusion.34), channel_id=1, source_target_pairs={{0,2},{1,3},{2,0},{3,1},{4,6},{5,7},{6,4},{7,5},{8,10},{9,11},{10,... | collective-permute-start | bytes 1572872 | tf_op jit(solution)/shard_map/ppermute | solution.py:450
  181.9 23.0 %collective-permute-start.9 = (bf16[128,2048]{1,0:T(8,128)(2,1)S(1)}, bf16[128,2048]{1,0:T(8,128)(2,1)S(1)}, u32[]{:S(2)}, u32[]{:S(2)}) collective-permute-start(bf16[128,2048]{1,0:T(8,128)(2,1)S(1)} %fusion.33), channel_id=1, source_target_pairs={{0,2},{1,3},{2,0},{3,1},{4,6},{5,7},{6,4},{7,5},{8,10},{9,11},{10,... | collective-permute-start | bytes 1572872 | tf_op jit(solution)/shard_map/ppermute | solution.py:450
  207.5 13.5 %collective-permute-start.15 = (bf16[128,2048]{1,0:T(8,128)(2,1)S(1)}, bf16[128,2048]{1,0:T(8,128)(2,1)S(1)}, u32[]{:S(2)}, u32[]{:S(2)}) collective-permute-start(bf16[128,2048]{1,0:T(8,128)(2,1)S(1)} %get-tuple-element.99), channel_id=1, source_target_pairs={{0,2},{1,3},{2,0},{3,1},{4,6},{5,7},{6,4},{7,5},{8,10},{9,11},{10,... | collective-permute-start | bytes 1572872 | tf_op jit(solution)/shard_map/ppermute | solution.py:450
  209.2 11.9 %collective-permute-start.17 = (bf16[128,2048]{1,0:T(8,128)(2,1)S(1)}, bf16[128,2048]{1,0:T(8,128)(2,1)S(1)}, u32[]{:S(2)}, u32[]{:S(2)}) collective-permute-start(bf16[128,2048]{1,0:T(8,128)(2,1)S(1)} %get-tuple-element.99), channel_id=1, source_target_pairs={{0,1},{1,0},{2,3},{3,2},{4,5},{5,4},{6,7},{7,6},{8,9},{9,8},{10,11... | collective-permute-start | bytes 1572872 | tf_op jit(solution)/shard_map/ppermute | solution.py:450
  221.1 1.9 collective-permute-start.16
  267.3 460.3 %all-gather.5.cloned.1.call-start = ((), (), s32[]{:S(2)}) async-start(), calls=%async_computation.1 | async-start | bytes 17301504 | tf_op jit(solution)/shard_map/all_gather | solution.py:569
  267.9 493.2 %all-gather.3.cloned.1.call-start = ((), (), s32[]{:S(2)}) async-start(), calls=%async_computation | async-start | bytes 17301504 | tf_op jit(solution)/shard_map/all_gather | solution.py:584
  277.6 2.7 collective-permute-start.18
  282.0 16.8 %collective-permute-start.19 = (bf16[128,2048]{1,0:T(8,128)(2,1)S(1)}, bf16[128,2048]{1,0:T(8,128)(2,1)S(1)}, u32[]{:S(2)}, u32[]{:S(2)}) collective-permute-start(bf16[128,2048]{1,0:T(8,128)(2,1)S(1)} %fusion.35), channel_id=1, source_target_pairs={{0,2},{1,3},{2,0},{3,1},{4,6},{5,7},{6,4},{7,5},{8,10},{9,11},{10,... | collective-permute-start | bytes 1572872 | tf_op jit(solution)/shard_map/ppermute | solution.py:450
  (42 other events, 454.3 us)
Sparse Core Ops, SparseCore 0:
  267.4 445.3 all-reduce.5
Sparse Core Ops, SparseCore 1:
  271.1 233.5 all-gather.4
  507.8 221.9 all-gather.2

commit v3 on v2

--- a/solution.py
+++ b/solution.py
@@ -212,7 +212,6 @@
     d_query_ref,
     d_key_ref,
     d_value_ref,
-    d_gate_ref,
     d_logit_ref,
     d_taps_ref,
     d_gain_ref,
@@ -258,9 +257,6 @@
             mixed = mixed_ref[rows, columns]
             scale = lax.rsqrt(jnp.mean(mixed * mixed, axis=-1, keepdims=True) + EPS_HEAD)
             unit_mixed = mixed * scale
-            d_gate_ref[rows, columns] = (
-                d_mixer * (unit_mixed * gain) * (logistic * (1.0 + gates * (1.0 - logistic)))
-            ).astype(LOW)
             d_normed = d_mixer * (gates * logistic)
             d_gain = d_gain + jnp.sum(d_normed * unit_mixed, axis=0, keepdims=True)
             weighted = d_normed * gain
@@ -411,13 +407,12 @@
             low,
             low,
             low,
-            low,
             jax.ShapeDtypeStruct((rows, DK), LOW),
             jax.ShapeDtypeStruct(taps.shape, FULL),
             jax.ShapeDtypeStruct((1, DK), FULL),
         ),
         in_specs=whole_blocks(17),
-        out_specs=tuple(whole_blocks(7)),
+        out_specs=tuple(whole_blocks(6)),
         scratch_shapes=[
             pltpu.VMEM((head_count, DK, DK), FULL),
             pltpu.VMEM((3, PAD, width), FULL),
@@ -445,6 +440,226 @@
     return jnp.stack(columns, axis=1), blocks.astype(FULL)
 
 
+def mm(left, right, left_dim, right_dim):
+    return lax.dot_general(
+        left, right, (((left_dim,), (right_dim,)), ((), ())), preferred_element_type=FULL
+    )
+
+
+FFN_TILE = 128
+FFN_ROWS = 1024
+TICKS = 8
+X_SENT, X_GOT, OWN, IN_SENT, IN_GOT, MID_SENT, MID_GOT, OUT_SENT, OUT_GOT, BACK_SENT, BACK_GOT, KEPT = range(12)
+
+
+def add_into(target_ref, other_ref):
+    rows = target_ref.shape[0]
+    piece = min(rows, 128)
+
+    def add(index, carry):
+        place = pl.ds(pl.multiple_of(index * piece, piece), piece)
+        target_ref[place, :] = (
+            target_ref[place, :].astype(FULL) + other_ref[place, :].astype(FULL)
+        ).astype(LOW)
+        return carry
+
+    lax.fori_loop(0, rows // piece, add, 0)
+
+
+def ffn_step(rows_ref, grads_ref, gate_ref, up_ref, down_ref, d_gate_ref, d_up_ref, d_down_ref, total):
+    block, tile = pl.program_id(1), gate_ref.shape[1]
+
+    @pl.when(block == 0)
+    def _():
+        total[...] = jnp.zeros_like(total)
+
+    rows, grads = rows_ref[...], grads_ref[...]
+    both = mm(rows, jnp.concatenate([gate_ref[...], up_ref[...]], axis=1), 1, 0)
+    gate_pre, up_pre = both[:, :tile], both[:, tile:]
+    d_hidden = mm(grads, down_ref[...], 1, 1)
+    logistic = sigmoid(gate_pre)
+    gate_swish = gate_pre * logistic
+    hidden_low = (gate_swish * up_pre).astype(LOW)
+    d_gate_low = (d_hidden * up_pre * (logistic * (1.0 + gate_pre * (1.0 - logistic)))).astype(LOW)
+    d_up_low = (d_hidden * gate_swish).astype(LOW)
+    total[: 2 * tile] += mm(jnp.concatenate([d_gate_low, d_up_low], axis=1), rows, 0, 0)
+    total[2 * tile :] += mm(hidden_low, grads, 0, 0)
+
+    @pl.when(block == pl.num_programs(1) - 1)
+    def _():
+        d_gate_ref[...] = total[:tile].T.astype(LOW)
+        d_up_ref[...] = total[tile : 2 * tile].T.astype(LOW)
+        d_down_ref[...] = total[2 * tile :].astype(LOW)
+
+
+def ffn_and_sums(orders, ticks, *refs):
+    count = len(orders)
+    ffn_refs, given = refs[:5], refs[5 : 5 + count]
+    d_refs, made = refs[5 + count : 8 + count], refs[8 + count : 8 + 2 * count]
+    scratch = refs[8 + 2 * count :]
+    total, sems = scratch[0], scratch[1]
+    halves, owns, ins, mids = (
+        scratch[2 + kind * count : 2 + (kind + 1) * count] for kind in range(4)
+    )
+    step = pl.program_id(0) * pl.num_programs(1) + pl.program_id(1)
+    here = lax.axis_index("dp")
+    side, place = here % 2, here // 2
+    pair = here + 1 - 2 * side
+    near = 2 * (place + 1 - 2 * (place % 2)) + side
+    far = 2 * (3 - place) + side
+    middle = (place == 1) | (place == 2)
+    end = (place == 0) | (place == 3)
+
+    @pl.when(step == 0)
+    def _():
+        barrier = pltpu.get_barrier_semaphore()
+        pl.semaphore_signal(barrier, inc=1, device_id={"dp": pair})
+        pl.semaphore_signal(barrier, inc=1, device_id={"dp": near})
+
+        @pl.when(middle)
+        def _():
+            pl.semaphore_signal(barrier, inc=1, device_id={"dp": far})
+            pl.semaphore_wait(barrier, 3)
+
+        @pl.when(end)
+        def _():
+            pl.semaphore_wait(barrier, 2)
+
+    def plan(which):
+        rows = halves[which].shape[0]
+        mine = pl.ds(pl.multiple_of(side * rows, rows), rows)
+        theirs = pl.ds(pl.multiple_of((1 - side) * rows, rows), rows)
+
+        def remote(source, target, sent, got, device):
+            return pltpu.make_async_remote_copy(
+                src_ref=source,
+                dst_ref=target,
+                send_sem=sems.at[which, sent],
+                recv_sem=sems.at[which, got],
+                device_id={"dp": device},
+            )
+
+        def local(source, target, sem):
+            return pltpu.make_async_copy(source, target, sems.at[which, sem])
+
+        return dict(
+            across=lambda: remote(given[which].at[theirs], halves[which], X_SENT, X_GOT, pair),
+            own=lambda: local(given[which].at[mine], owns[which], OWN),
+            inward=lambda: remote(halves[which], ins[which], IN_SENT, IN_GOT, near),
+            middle=lambda: remote(halves[which], mids[which], MID_SENT, MID_GOT, far),
+            outward=lambda: remote(halves[which], made[which].at[mine], OUT_SENT, OUT_GOT, near),
+            back_end=lambda: remote(made[which].at[mine], made[which].at[mine], BACK_SENT, BACK_GOT, pair),
+            back_middle=lambda: remote(halves[which], made[which].at[mine], BACK_SENT, BACK_GOT, pair),
+            back_got=lambda: remote(made[which].at[theirs], made[which].at[theirs], BACK_SENT, BACK_GOT, pair),
+            kept=lambda: local(halves[which], made[which].at[mine], KEPT),
+        )
+
+    def stage(which, number):
+        copies = plan(which)
+        if number == 0:
+            copies["across"]().start()
+            copies["own"]().start()
+        elif number == 1:
+            copies["own"]().wait()
+            copies["across"]().wait()
+            add_into(halves[which], owns[which])
+
+            @pl.when(end)
+            def _():
+                copies["inward"]().start()
+        elif number == 2:
+
+            @pl.when(end)
+            def _():
+                copies["inward"]().wait_send()
+
+            @pl.when(middle)
+            def _():
+                copies["inward"]().wait_recv()
+                add_into(halves[which], ins[which])
+                copies["middle"]().start()
+        elif number == 3:
+
+            @pl.when(middle)
+            def _():
+                copies["middle"]().wait()
+                add_into(halves[which], mids[which])
+                copies["outward"]().start()
+                copies["back_middle"]().start()
+                copies["kept"]().start()
+        elif number == 4:
+
+            @pl.when(end)
+            def _():
+                copies["outward"]().wait_recv()
+                copies["back_end"]().start()
+
+            @pl.when(middle)
+            def _():
+                copies["outward"]().wait_send()
+                copies["kept"]().wait()
+        else:
+
+            @pl.when(end)
+            def _():
+                copies["back_end"]().wait_send()
+
+            @pl.when(middle)
+            def _():
+                copies["back_middle"]().wait_send()
+            copies["back_got"]().wait_recv()
+
+    for tick in range(TICKS):
+
+        @pl.when(step == ticks[tick])
+        def _(tick=tick):
+            for which, order in reversed(list(enumerate(orders))):
+                if 0 <= tick - order <= 5:
+                    stage(which, tick - order)
+
+    ffn_step(*ffn_refs, *d_refs, total)
+
+
+def run_ffn_and_sums(rows, grads, gate_weight, up_weight, down_weight, given, orders):
+    total_rows, features = rows.shape
+    units = gate_weight.shape[1]
+    block_rows = min(FFN_ROWS, total_rows)
+    blocks, tiles = total_rows // block_rows, units // FFN_TILE
+    steps = blocks * tiles
+    ticks = [((steps - 1) * tick) // (TICKS - 1) for tick in range(TICKS)]
+    across = pl.BlockSpec((features, FFN_TILE), lambda tile, block: (0, tile))
+    down = pl.BlockSpec((FFN_TILE, features), lambda tile, block: (tile, 0))
+    tall = pl.BlockSpec((block_rows, features), lambda tile, block: (block, 0))
+    anywhere = [pl.BlockSpec(memory_space=pl.ANY)] * len(given)
+    half_shapes = [(values.shape[0] // 2, values.shape[1]) for values in given]
+    return pl.pallas_call(
+        functools.partial(ffn_and_sums, orders, ticks),
+        grid=(tiles, blocks),
+        in_specs=[tall, tall, across, across, down] + anywhere,
+        out_specs=[across, across, down] + anywhere,
+        out_shape=[
+            jax.ShapeDtypeStruct((features, units), LOW),
+            jax.ShapeDtypeStruct((features, units), LOW),
+            jax.ShapeDtypeStruct((units, features), LOW),
+        ]
+        + [jax.ShapeDtypeStruct(values.shape, LOW) for values in given],
+        scratch_shapes=[
+            pltpu.VMEM((3 * FFN_TILE, features), FULL),
+            pltpu.SemaphoreType.DMA((len(given), 12)),
+        ]
+        + [pltpu.VMEM(shape, LOW) for kind in range(4) for shape in half_shapes],
+        compiler_params=pltpu.CompilerParams(
+            vmem_limit_bytes=60 * 1024 * 1024, collective_id=0, has_side_effects=True
+        ),
+        cost_estimate=pl.CostEstimate(
+            flops=12 * total_rows * features * units,
+            bytes_accessed=4 * tiles * total_rows * features,
+            transcendentals=total_rows * units,
+        ),
+        name="ffn_and_sums",
+    )(rows, grads, gate_weight, up_weight, down_weight, *given)
+
+
 def by_pairs(values, bit):
     count = lax.axis_size("mp")
     return lax.ppermute(values, "mp", [(here, here ^ bit) for here in range(count)])
@@ -504,6 +719,13 @@
     return logistic * (1.0 + values * (1.0 - logistic))
 
 
+def gate_back(d_mixer, mixed, gates, head_gain):
+    shape = mixed.shape
+    heads = mixed.reshape(shape[0], shape[1] // DK, DK)
+    normed = (heads * inverse_root(heads, EPS_HEAD) * head_gain).reshape(shape)
+    return (d_mixer * normed * sigmoid_slope(gates)).astype(LOW)
+
+
 def doc_index(lengths, length):
     starts = jnp.cumsum(lengths, axis=1) - lengths
     places = jnp.arange(length, dtype=jnp.int32)
@@ -525,17 +747,6 @@
     d_gate_low = (d_hidden * up_pre * sigmoid_slope(gate_pre)).astype(LOW)
     d_up_low = (d_hidden * gate_swish).astype(LOW)
     return hidden_low, d_gate_low, d_up_low
-
-
-def ffn_grads(rows, grad_rows, gate_weight, up_weight, down_weight):
-    hidden_low, d_gate_low, d_up_low = ffn_terms(
-        rows, grad_rows, gate_weight, up_weight, down_weight
-    )
-    return (
-        dot_full("td,tf->df", rows, d_gate_low),
-        dot_full("td,tf->df", rows, d_up_low),
-        dot_full("tf,td->fd", hidden_low, grad_rows),
-    )
 
 
 def on_device(
@@ -564,13 +775,12 @@
     taps = conv_weight.reshape(3 * CONV, width)
     gain_row = head_gain[None, :]
 
-    everyone = group_rows * lax.axis_size("dp") <= ROWS_MOST
+    everyone = group_rows * lax.axis_size("dp") <= ROWS_MOST and lax.axis_size("dp") == 8
     if everyone:
         all_grad_rows = lax.all_gather(cotangent, ("dp", "mp"), axis=0, tiled=True)
     residual_in = inputs.astype(FULL)
     scale_one = inverse_root(residual_in, EPS_NORM)
     normed = gather_rows((residual_in * scale_one * norm_gain).astype(LOW))
-    grad_rows = gather_rows(cotangent)
     weights = (query_weight, key_weight, value_weight, gating_weight)
     projections = tuple(dot_full("td,df->tf", normed, weight) for weight in weights)
     logits = dot_full("td,df->tf", normed, beta_weight)
@@ -581,7 +791,13 @@
     ffn_local = (residual_mid * scale_two * ffn_gain).astype(LOW)
     ffn_input = gather_rows(ffn_local)
     if everyone:
+        ffn_input, all_grad_rows = lax.optimization_barrier((ffn_input, all_grad_rows))
         all_ffn_input = lax.all_gather(ffn_local, ("dp", "mp"), axis=0, tiled=True)
+        grad_rows = lax.dynamic_slice_in_dim(
+            all_grad_rows, lax.axis_index("dp") * group_rows, group_rows, 0
+        )
+    else:
+        grad_rows = gather_rows(cotangent)
 
     hidden_low, d_gate_low, d_up_low = ffn_terms(
         ffn_input, grad_rows, gate_weight, up_weight, down_weight
@@ -589,8 +805,6 @@
     d_ffn_norm = scatter_sum(
         dot_full("tf,df->td", d_gate_low, gate_weight) + dot_full("tf,df->td", d_up_low, up_weight)
     )
-    ffn_out = scatter_sum(dot_full("tf,fd->td", hidden_low, down_weight))
-    output = (residual_mid + ffn_out).astype(LOW)
     d_ffn = None
     if not everyone:
         d_ffn = (
@@ -602,36 +816,54 @@
     d_mid = cotangent.astype(FULL) + norm_back(residual_mid, scale_two, ffn_gain, d_ffn_norm)
     ffn_gain_part = jnp.sum(d_ffn_norm * residual_mid * scale_two, axis=0)
     mid_rows = gather_rows(d_mid.astype(LOW))
-    d_output_w = dot_full("tf,td->fd", mixer_low, mid_rows)
     d_mixer = dot_full("td,fd->tf", mid_rows, output_weight)
+    d_gate_low = gate_back(d_mixer, kept[5], projections[3], head_gain)
+    early = [
+        dot_full("tf,td->fd", mixer_low, mid_rows).astype(LOW),
+        dot_full("td,tf->df", normed, d_gate_low).astype(LOW),
+    ]
+    d_mixer, *early = lax.optimization_barrier((d_mixer, *early))
+    early = lax.psum(early, "dp")
     *low_grads, d_logits, d_taps, head_gain_part = run_mixer_backward(
         d_mixer, projections, logits, taps, gain_row, meta, ids, kept
     )
     d_logits = d_logits[:, :head_count]
     summed = dot_full("tf,df->td", d_logits, beta_weight)
-    for grads, weight in zip(low_grads, weights):
+    for grads, weight in zip(low_grads + [d_gate_low], weights):
         summed = summed + dot_full("tf,df->td", grads, weight)
+    summed, hidden_low = lax.optimization_barrier((summed, hidden_low))
     d_normed = scatter_sum(summed)
+    ffn_out = scatter_sum(dot_full("tf,fd->td", hidden_low, down_weight))
+    output = (residual_mid + ffn_out).astype(LOW)
     input_grad = d_mid + norm_back(residual_in, scale_one, norm_gain, d_normed)
     norm_gain_part = jnp.sum(d_normed * residual_in * scale_one, axis=0)
-    proj_grads = [dot_full("td,tf->df", normed, grads).astype(LOW) for grads in low_grads]
+    late = [dot_full("td,tf->df", normed, grads).astype(LOW) for grads in low_grads]
     d_beta_w = dot_full("td,tf->df", normed, d_logits)
 
     gains = jnp.concatenate([norm_gain_part, ffn_gain_part, head_gain_part[0]])
-    gains = lax.psum(gains, "mp")
+    if lax.axis_size("mp") == 4:
+        for bit in (1, 2):
+            gains = gains + by_pairs(gains, bit)
+    else:
+        gains = lax.psum(gains, "mp")
     small = jnp.concatenate([d_beta_w.reshape(-1), d_taps.reshape(-1), gains])
     size = small.shape[0]
-    padded = -(-size // (16 * 512)) * 16 * 512
+    padded = -(-size // (32 * 512)) * 32 * 512
     small = jnp.pad(small, (0, padded - size)).reshape(-1, 512).astype(LOW)
+    late.append(small)
     if everyone:
-        d_ffn = ffn_grads(all_ffn_input, all_grad_rows, gate_weight, up_weight, down_weight)
+        *d_ffn, d_query_w, d_key_w, d_value_w, small = run_ffn_and_sums(
+            all_ffn_input, all_grad_rows, gate_weight, up_weight, down_weight, late, (0, 1, 2, 2)
+        )
     else:
-        d_ffn = [grads.astype(FULL) for grads in lax.psum([d.astype(LOW) for d in d_ffn], "dp")]
-    d_gate_w, d_up_w, d_down = d_ffn
-    *proj_grads, d_output_w, small = [
-        grads.astype(FULL)
-        for grads in lax.psum(proj_grads + [d_output_w.astype(LOW), small], "dp")
+        d_query_w, d_key_w, d_value_w, small = lax.psum(late, "dp")
+        d_ffn = lax.psum([grads.astype(LOW) for grads in d_ffn], "dp")
+    d_gate_w, d_up_w, d_down = [grads.astype(FULL) for grads in d_ffn]
+    proj_grads = [
+        grads.astype(FULL) for grads in (d_query_w, d_key_w, d_value_w, early[1])
     ]
+    d_output_w = early[0].astype(FULL)
+    small = small.astype(FULL)
     small = small.reshape(-1)
     beta_size, taps_size = d_beta_w.size, taps.size
     d_beta_w = small[:beta_size].reshape(d_beta_w.shape)

time: 957 us -> 632 us (0.66)
  waiting for transfers between devices: 439 us -> 96.9 us
  Pallas kernels: 76.1 us -> 326 us
  matrix products: 290 us -> 67 us
  blocking collectives: 51.6 us -> 0 us
  other arithmetic: 42.7 us -> 74.2 us
  local copies, waits for them, and re-layouts: 15.6 us -> 28.1 us
    psum x1, waiting for transfers between devices: 353 us -> 0.01 us  [on_device(): early = lax.psum(early, 'dp')]
    pallas_call x0 -> x1, Pallas kernels: none -> 249 us  [run_ffn_and_sums(): pl.pallas_call(functools.partial(ffn_and_sums, orders, ticks), grid=(tile...]
    dot_general x30 -> x24, matrix products: 290 us -> 67 us  [dot_full(): return jnp.einsum(equation, left, right, preferred_element_type=FULL)]
    psum x2 -> x0, blocking collectives: 51.6 us -> none  [the longest x1 40.5 us: on_device(): lax.psum(proj_grads + [d_output_w.astype(LOW), small], 'dp')]
    convert_element_type x0 -> x5, other arithmetic: none -> 25.4 us  [the longest x3 21.9 us: on_device(): d_gate_w, d_up_w, d_down = [grads.astype(FULL) for grads in d_ffn]]
    ppermute x20 -> x19, waiting for transfers between devices: 85.1 us -> 96.2 us  [by_pairs(): lax.ppermute(values, 'mp', [(here, here ^ bit) for here in range(count)])]
  transfers between devices with their start and end apart: 23 -> 22, of which waited for: 13 -> 10; matrix products, arithmetic and copies ran while one was open for 10% -> 24% of each run, Pallas kernels for 0% -> 52%
where the time goes in v3:
time: 632 us; the launch traced here: 624 us
  Pallas kernels  326 us (52%)
  waiting for transfers between devices  96.9 us (15%)
  other arithmetic  74.2 us (12%)
  matrix products  67 us (11%)
  local copies, waits for them, and re-layouts  28.1 us (4%)
  starting transfers between devices  17.1 us (3%)
  between operations  14.8 us (2%)
    pallas_call x1, Pallas kernels, run_ffn_and_sums(): pl.pallas_call(functools.partial(ffn_and_sums, orders, ticks), grid=(tile...  249 us
    ppermute x19, waiting for transfers between devices, by_pairs(): lax.ppermute(values, 'mp', [(here, here ^ bit) for here in range(count)])  96.2 us
    dot_general x24, matrix products, dot_full(): return jnp.einsum(equation, left, right, preferred_element_type=FULL)  67 us
    pallas_call x1, Pallas kernels, run_mixer_forward(): pl.pallas_call(functools.partial(mixer_forward, head_count), out_shape=(j...  48.9 us
    pallas_call x1, Pallas kernels, run_mixer_backward(): pl.pallas_call(functools.partial(mixer_backward, head_count), out_shape=(...  27.5 us
    convert_element_type x3, other arithmetic, on_device(): d_gate_w, d_up_w, d_down = [grads.astype(FULL) for grads in d_ffn]  21.9 us
    ppermute x19, starting transfers between devices, by_pairs(): lax.ppermute(values, 'mp', [(here, here ^ bit) for here in range(count)])  17 us
    convert_element_type x4, other arithmetic, on_device(): grads.astype(FULL)  13.9 us
  transfers between devices with their start and end apart: 22, of which 10 were waited for; matrix products, arithmetic and copies ran while one was open for 24% of the time, Pallas kernels for 52%

profile of v3, /device:TPU:0, one launch (start us, length us, event | category | flops | bytes accessed | tf_op | source)
XLA Modules:
  0.0 623.7 jit_solution(16258634521907985757)
XLA Ops:
  15.1 13.0 %collective-permute-done = bf16[128,2048]{1,0:T(8,128)(2,1)S(1)} collective-permute-done((bf16[128,2048]{1,0:T(8,128)(2,1)S(1)}, bf16[128,2048]{1,0:T(8,128)(2,1)S(1)}, u32[]{:S(2)}, u32[]{:S(2)}) %collective-permute-start) | collective-permute-done | bytes 524320 | tf_op jit(solution)/shard_map/ppermute | solution.py:665
  45.7 48.9 %mixer_forward.1 = (bf16[512,512]{1,0:T(8,128)(2,1)}, f32[3,512,512]{2,1,0:T(8,128)}, f32[4,512,128]{2,1,0:T(8,128)}, f32[512,512]{1,0:T(8,128)}, f32[512,512]{1...) custom-call(f32[512,512]{1,0:T(8,128)} %fusion.48.query_ref, ...), custom_call_target="tpu_custom_call" | custom-call | tf_op jit(solution)/shard_map/mixer_forward/pallas_call | solution.py:380
  108.2 12.5 %collective-permute-done.4 = bf16[128,2048]{1,0:T(8,128)(2,1)} collective-permute-done((bf16[128,2048]{1,0:T(8,128)(2,1)S(1)}, bf16[128,2048]{1,0:T(8,128)(2,1)}, u32[]{:S(2)}, u32[]{:S(2)}) %collective-permute-start.4) | collective-permute-done | bytes 524320 | tf_op jit(solution)/shard_map/ppermute | solution.py:665
  125.5 12.1 %collective-permute-done.5 = bf16[128,2048]{1,0:T(8,128)(2,1)} collective-permute-done((bf16[128,2048]{1,0:T(8,128)(2,1)}, bf16[128,2048]{1,0:T(8,128)(2,1)}, u32[]{:S(2)}, u32[]{:S(2)}) %collective-permute-start.5) | collective-permute-done | bytes 524320 | tf_op jit(solution)/shard_map/ppermute | solution.py:665
  144.3 6.6 %fusion.1 = f32[512,1408]{1,0:T(8,128)S(1)} fusion(bf16[1408,2048]{1,0:T(8,128)(2,1)} %refs_4_.1, bf16[4096,2048]{1,0:T(8,128)(2,1)} %all-gather.3.cloned.1.call-done.refs_1_, s32[]{:T(128)S(6)} %select_n.116), kind=kOutput, calls=%fused_computation.30 | convolution fusion | flops 2952790016 | bytes 10747908 | tf_op jit(solution)/shard_map/td,fd->tf/dot_general | solution.py:738
  151.0 5.9 fusion.54
  157.0 5.5 multiply_convert_fusion
  162.5 5.9 fusion.3
  168.4 3.5 convolution_add_fusion
  176.8 12.5 %collective-permute-done.9 = bf16[128,2048]{1,0:T(8,128)(2,1)S(1)} collective-permute-done((bf16[128,2048]{1,0:T(8,128)(2,1)S(1)}, bf16[128,2048]{1,0:T(8,128)(2,1)S(1)}, u32[]{:S(2)}, u32[]{:S(2)}) %collective-permute-start.9) | collective-permute-done | bytes 524320 | tf_op jit(solution)/shard_map/ppermute | solution.py:665
  192.9 23.0 %collective-permute-done.10 = bf16[128,2048]{1,0:T(8,128)(2,1)} collective-permute-done((bf16[128,2048]{1,0:T(8,128)(2,1)}, bf16[128,2048]{1,0:T(8,128)(2,1)}, u32[]{:S(2)}, u32[]{:S(2)}) %collective-permute-start.10) | collective-permute-done | bytes 524320 | tf_op jit(solution)/shard_map/ppermute | solution.py:665
  231.4 2.8 convolution_convert_fusion.4
  234.2 27.5 %mixer_backward.1 = (bf16[512,512]{1,0:T(8,128)(2,1)}, bf16[512,512]{1,0:T(8,128)(2,1)}, bf16[512,512]{1,0:T(8,128)(2,1)}, bf16[512,128]{1,0:T(8,128)(2,1)}, f32[12,512]{1,0:T(8,128)}, /*index=5*/f32[1,128]{1,0:T(1,128)}) custom-call(f32[512,512]{1,0:T(8,128)} %get-tuple-element.47.d_mixer_ref, f32[512,512]{1,0:T(8,128)} %fusion.48.query_ref, ...), custom_call_target="tpu_custom_call" | custom-call | tf_op jit(solution)/shard_map/mixer_backward/pallas_call | solution.py:404
  273.2 3.4 fusion.59
  283.1 3.7 convolution_convert_fusion.2.refs_5_
  286.9 2.6 convolution_convert_fusion.1.refs_6_
  299.2 10.9 %collective-permute-done.16 = bf16[128,2048]{1,0:T(8,128)(2,1)S(1)} collective-permute-done((bf16[128,2048]{1,0:T(8,128)(2,1)S(1)}, bf16[128,2048]{1,0:T(8,128)(2,1)S(1)}, u32[]{:S(2)}, u32[]{:S(2)}) %collective-permute-start.16) | collective-permute-done | bytes 524320 | tf_op jit(solution)/shard_map/ppermute | solution.py:665
  314.3 6.8 %collective-permute-done.14 = bf16[128,2048]{1,0:T(8,128)(2,1)S(1)} collective-permute-done((bf16[128,2048]{1,0:T(8,128)(2,1)S(1)}, bf16[128,2048]{1,0:T(8,128)(2,1)S(1)}, u32[]{:S(2)}, u32[]{:S(2)}) %collective-permute-start.14) | collective-permute-done | bytes 524320 | tf_op jit(solution)/shard_map/ppermute | solution.py:665
  322.8 249.1 %ffn_and_sums.1 = (bf16[2048,1408]{1,0:T(8,128)(2,1)}, bf16[2048,1408]{1,0:T(8,128)(2,1)}, bf16[1408,2048]{1,0:T(8,128)(2,1)}, bf16[2048,512]{1,0:T(8,128)(2,1)}...) custom-call(bf16[4096,2048]{1,0:T(8,128)(2,1)} %all-gather.5.cloned.1.call-done.refs_0_, ...), custom_call_target="tpu_custom_call" | custom-call | flops 141733920768 | bytes 369098752 | tf_op jit(solution)/shard_map/ffn_and_sums/pallas_call | solution.py:635
  574.8 4.3 convert_element_type.261
  588.2 8.0 %convert_element_type.266 = f32[2048,1408]{1,0:T(8,128)} convert(bf16[2048,1408]{1,0:T(8,128)(2,1)} %get-tuple-element.68) | non-fusion elementwise | flops 2883584 | bytes 17301504 | tf_op jit(solution)/shard_map/convert_element_type | solution.py:861
  596.1 7.9 %convert_element_type.267 = f32[2048,1408]{1,0:T(8,128)} convert(bf16[2048,1408]{1,0:T(8,128)(2,1)} %get-tuple-element.69) | non-fusion elementwise | flops 2883584 | bytes 17301504 | tf_op jit(solution)/shard_map/convert_element_type | solution.py:861
  604.1 6.0 convert_element_type.268
  610.1 4.3 convert_element_type.264
  (251 shorter events, 121.8 us)
Async XLA Ops:
  7.2 87.4 %copy-start = (bf16[512,2048]{1,0:T(8,128)(2,1)S(1)}, bf16[512,2048]{1,0:T(8,128)(2,1)}, u32[]{:S(2)}) copy-start(bf16[512,2048]{1,0:T(8,128)(2,1)} %param.27) | copy-start | bytes 6291460
  7.2 137.1 %all-gather.3.cloned.1.call-start = ((), (), s32[]{:S(2)}) async-start(), calls=%async_computation | async-start | bytes 17301504 | tf_op jit(solution)/shard_map/all_gather | solution.py:780
  8.0 314.8 %all-gather.5.cloned.1.call-start = ((), (), s32[]{:S(2)}) async-start(), calls=%async_computation.1 | async-start | bytes 17301504 | tf_op jit(solution)/shard_map/all_gather | solution.py:795
  10.5 19.6 %collective-permute-start.2 = (bf16[128,2048]{1,0:T(8,128)(2,1)S(1)}, bf16[128,2048]{1,0:T(8,128)(2,1)}, u32[]{:S(2)}, u32[]{:S(2)}) collective-permute-start(bf16[128,2048]{1,0:T(8,128)(2,1)S(1)} %fusion.11), channel_id=1, source_target_pairs={{0,1},{1,0},{2,3},{3,2},{4,5},{5,4},{6,7},{7,6},{8,9},{9,8},{10,11... | collective-permute-start | bytes 1572872 | tf_op jit(solution)/shard_map/ppermute | solution.py:665
  11.0 17.1 %collective-permute-start = (bf16[128,2048]{1,0:T(8,128)(2,1)S(1)}, bf16[128,2048]{1,0:T(8,128)(2,1)S(1)}, u32[]{:S(2)}, u32[]{:S(2)}) collective-permute-start(bf16[128,2048]{1,0:T(8,128)(2,1)S(1)} %fusion.11), channel_id=1, source_target_pairs={{0,2},{1,3},{2,0},{3,1},{4,6},{5,7},{6,4},{7,5},{8,10},{9,11},{10,... | collective-permute-start | bytes 1572872 | tf_op jit(solution)/shard_map/ppermute | solution.py:665
  28.1 3.6 collective-permute-start.1
  99.0 3.0 collective-permute-start.3
  105.7 15.0 %collective-permute-start.4 = (bf16[128,2048]{1,0:T(8,128)(2,1)S(1)}, bf16[128,2048]{1,0:T(8,128)(2,1)}, u32[]{:S(2)}, u32[]{:S(2)}) collective-permute-start(bf16[128,2048]{1,0:T(8,128)(2,1)S(1)} %fusion.24), channel_id=1, source_target_pairs={{0,2},{1,3},{2,0},{3,1},{4,6},{5,7},{6,4},{7,5},{8,10},{9,11},{10,... | collective-permute-start | bytes 1572872 | tf_op jit(solution)/shard_map/ppermute | solution.py:665
  123.6 486.5 %all-reduce.6.cloned.1.call-start = ((), (), s32[]{:S(2)}) async-start(), calls=%async_computation.2 | async-start | bytes 8388608 | tf_op jit(solution)/shard_map/psum | solution.py:826
  123.6 14.0 %collective-permute-start.5 = (bf16[128,2048]{1,0:T(8,128)(2,1)}, bf16[128,2048]{1,0:T(8,128)(2,1)}, u32[]{:S(2)}, u32[]{:S(2)}) collective-permute-start(bf16[128,2048]{1,0:T(8,128)(2,1)} %multiply_convert_fusion.5), channel_id=1, source_target_pairs={{0,2},{1,3},{2,0},{3,1},{4,6},{5,7},{6,4},{7,5},{8,10},{9,11},{10,... | collective-permute-start | bytes 1572872 | tf_op jit(solution)/shard_map/ppermute | solution.py:665
  125.5 12.1 %collective-permute-start.7 = (bf16[128,2048]{1,0:T(8,128)(2,1)}, bf16[128,2048]{1,0:T(8,128)(2,1)}, u32[]{:S(2)}, u32[]{:S(2)}) collective-permute-start(bf16[128,2048]{1,0:T(8,128)(2,1)} %multiply_convert_fusion.5), channel_id=1, source_target_pairs={{0,1},{1,0},{2,3},{3,2},{4,5},{5,4},{6,7},{7,6},{8,9},{9,8},{10,11... | collective-permute-start | bytes 1572872 | tf_op jit(solution)/shard_map/ppermute | solution.py:665
  137.6 2.3 collective-permute-start.6
  172.1 2.7 collective-permute-start.8
  175.2 14.1 %collective-permute-start.9 = (bf16[128,2048]{1,0:T(8,128)(2,1)S(1)}, bf16[128,2048]{1,0:T(8,128)(2,1)S(1)}, u32[]{:S(2)}, u32[]{:S(2)}) collective-permute-start(bf16[128,2048]{1,0:T(8,128)(2,1)S(1)} %fusion.25), channel_id=1, source_target_pairs={{0,2},{1,3},{2,0},{3,1},{4,6},{5,7},{6,4},{7,5},{8,10},{9,11},{10,... | collective-permute-start | bytes 1572872 | tf_op jit(solution)/shard_map/ppermute | solution.py:665
  191.4 24.6 %collective-permute-start.10 = (bf16[128,2048]{1,0:T(8,128)(2,1)}, bf16[128,2048]{1,0:T(8,128)(2,1)}, u32[]{:S(2)}, u32[]{:S(2)}) collective-permute-start(bf16[128,2048]{1,0:T(8,128)(2,1)} %get-tuple-element.167), channel_id=1, source_target_pairs={{0,2},{1,3},{2,0},{3,1},{4,6},{5,7},{6,4},{7,5},{8,10},{9,11},{10,... | collective-permute-start | bytes 1572872 | tf_op jit(solution)/shard_map/ppermute | solution.py:665
  192.9 28.7 %collective-permute-start.12 = (bf16[128,2048]{1,0:T(8,128)(2,1)}, bf16[128,2048]{1,0:T(8,128)(2,1)}, u32[]{:S(2)}, u32[]{:S(2)}) collective-permute-start(bf16[128,2048]{1,0:T(8,128)(2,1)} %get-tuple-element.167), channel_id=1, source_target_pairs={{0,1},{1,0},{2,3},{3,2},{4,5},{5,4},{6,7},{7,6},{8,9},{9,8},{10,11... | collective-permute-start | bytes 1572872 | tf_op jit(solution)/shard_map/ppermute | solution.py:665
  215.9 7.6 %collective-permute-start.11 = (bf16[128,2048]{1,0:T(8,128)(2,1)}, bf16[128,2048]{1,0:T(8,128)(2,1)}, u32[]{:S(2)}, u32[]{:S(2)}) collective-permute-start(bf16[128,2048]{1,0:T(8,128)(2,1)} %collective-permute-done.10), channel_id=1, source_target_pairs={{0,1},{1,0},{2,3},{3,2},{4,5},{5,4},{6,7},{7,6},{8,9},{9,8},{10,11... | collective-permute-start | bytes 1572872 | tf_op jit(solution)/shard_map/ppermute | solution.py:665
  234.2 27.6 %copy-start.35 = (bf16[512,512]{1,0:T(8,128)(2,1)S(1)}, bf16[512,512]{1,0:T(8,128)(2,1)}, u32[]{:S(2)}) copy-start(bf16[512,512]{1,0:T(8,128)(2,1)} %copy-done.34) | copy-start | bytes 1572868
  270.3 21.8 %collective-permute-start.15 = (bf16[2,128,2048]{2,1,0:T(8,128)(2,1)}, bf16[2,128,2048]{2,1,0:T(8,128)(2,1)}, u32[]{:S(2)}, u32[]{:S(2)}) collective-permute-start(bf16[2,128,2048]{2,1,0:T(8,128)(2,1)} %fusion.8), channel_id=1, source_target_pairs={{0,1},{1,0},{2,3},{3,2},{4,5},{5,4},{6,7},{7,6},{8,9},{9,8},{10,11... | collective-permute-start | bytes 3145736 | tf_op jit(solution)/shard_map/ppermute | solution.py:665
  279.7 17.7 %collective-permute-start.13 = (bf16[2,128,2048]{2,1,0:T(8,128)(2,1)}, bf16[2,128,2048]{2,1,0:T(8,128)(2,1)}, u32[]{:S(2)}, u32[]{:S(2)}) collective-permute-start(bf16[2,128,2048]{2,1,0:T(8,128)(2,1)} %fusion.7), channel_id=1, source_target_pairs={{0,1},{1,0},{2,3},{3,2},{4,5},{5,4},{6,7},{7,6},{8,9},{9,8},{10,11... | collective-permute-start | bytes 3145736 | tf_op jit(solution)/shard_map/ppermute | solution.py:665
  295.2 14.9 %collective-permute-start.16 = (bf16[128,2048]{1,0:T(8,128)(2,1)S(1)}, bf16[128,2048]{1,0:T(8,128)(2,1)S(1)}, u32[]{:S(2)}, u32[]{:S(2)}) collective-permute-start(bf16[128,2048]{1,0:T(8,128)(2,1)S(1)} %fusion.27), channel_id=1, source_target_pairs={{0,2},{1,3},{2,0},{3,1},{4,6},{5,7},{6,4},{7,5},{8,10},{9,11},{10,... | collective-permute-start | bytes 1572872 | tf_op jit(solution)/shard_map/ppermute | solution.py:665
  299.0 22.0 %collective-permute-start.14 = (bf16[128,2048]{1,0:T(8,128)(2,1)S(1)}, bf16[128,2048]{1,0:T(8,128)(2,1)S(1)}, u32[]{:S(2)}, u32[]{:S(2)}) collective-permute-start(bf16[128,2048]{1,0:T(8,128)(2,1)S(1)} %fusion.26), channel_id=1, source_target_pairs={{0,2},{1,3},{2,0},{3,1},{4,6},{5,7},{6,4},{7,5},{8,10},{9,11},{10,... | collective-permute-start | bytes 1572872 | tf_op jit(solution)/shard_map/ppermute | solution.py:665
  310.5 1.6 collective-permute-start.17
  312.1 9.9 %collective-permute-start.18 = (f32[4224]{0:T(1024)S(1)}, f32[4224]{0:T(1024)S(1)}, u32[]{:S(2)}, u32[]{:S(2)}) collective-permute-start(f32[4224]{0:T(1024)S(1)} %fusion.46), channel_id=1, source_target_pairs={{0,2},{1,3},{2,0},{3,1},{4,6},{5,7},{6,4},{7,5},{8,10},{9,11},{10,... | collective-permute-start | bytes 50696 | tf_op jit(solution)/shard_map/ppermute | solution.py:665
  (53 other events, 361.4 us)
Sparse Core Ops, SparseCore 0:
  10.9 119.2 all-gather.2
  133.1 123.2 all-gather.4
  283.2 202.2 all-reduce.5

commit v4 on v3

--- a/solution.py
+++ b/solution.py
@@ -1,4 +1,5 @@
 import functools
+import math
 
 import jax
 import jax.numpy as jnp
@@ -102,9 +103,24 @@
         else:
             result_parts = parts_of(result)
             inner = product(parts_of(link), result_parts)
+            yield
             result = result - product(result_parts, parts_of(inner))
+            yield
         step = 2 * step
     return result
+
+
+def side_by_side(works):
+    works = list(works)
+    while works:
+        left = []
+        for work in works:
+            try:
+                next(work)
+                left.append(work)
+            except StopIteration:
+                pass
+        works = left
 
 
 def mixer_forward(
@@ -140,7 +156,7 @@
         closing = spread(meta_ref, start, 5)
         carried = spread(meta_ref, start, 6)
         betas = sigmoid(logit_ref[rows, :])
-        for head in range(head_count):
+        def work(head):
             columns = slice(head * DK, (head + 1) * DK)
             acts = []
             for which, ref in enumerate((query_ref, key_ref, value_ref)):
@@ -160,31 +176,38 @@
                 for act in acts[:2]
             ]
             queries, keys, values = unit[0].astype(LOW), unit[1].astype(LOW), acts[2].astype(LOW)
+            yield
             beta = jnp.broadcast_to(betas[:, head : head + 1], (SPAN, DK))
             gram = product((keys,), (keys,), 1, 1)
-            solve = inverse_lower(beta * gram * strict, row_ids, col_ids)
+            yield
+            solve = yield from inverse_lower(beta * gram * strict, row_ids, col_ids)
             solve_ref[head, rows, :] = solve
             solve_parts = parts_of(solve)
             w_rows = product(solve_parts, parts_of(beta * keys.astype(FULL)))
             u_rows = product(solve_parts, parts_of(beta * values.astype(FULL)))
             w_ref[rows, columns] = w_rows
             u_ref[rows, columns] = u_rows
+            yield
             probes = product((queries,), (keys,), 1, 1) * inclusive
             before = state[head]
             states_ref[head, rows, :] = before
             before_parts = parts_of(before)
             new_value = u_rows - opening * product(parts_of(w_rows), before_parts)
             new_ref[rows, columns] = new_value
+            yield
             mixed = opening * product((queries,), before_parts) + product(
                 parts_of(probes), parts_of(new_value)
             )
             mixed_ref[rows, columns] = mixed
+            yield
             state[head] = carried * before + product(
                 (keys,), parts_of(closing * new_value), 0, 0
             )
             scale = lax.rsqrt(jnp.mean(mixed * mixed, axis=-1, keepdims=True) + EPS_HEAD)
             gates = gate_ref[rows, columns]
             mixer_ref[rows, columns] = (mixed * scale * gain * (gates * sigmoid(gates))).astype(LOW)
+
+        side_by_side(work(head) for head in range(head_count))
         return carry
 
     lax.fori_loop(0, query_ref.shape[0] // SPAN, step, 0)
@@ -249,7 +272,8 @@
         lanes = lax.broadcasted_iota(jnp.int32, (SPAN, DK), 1)
         d_logits = jnp.zeros((SPAN, DK), FULL)
         d_gain = jnp.zeros((1, DK), FULL)
-        for head in range(head_count):
+        def work(head):
+            nonlocal d_gain, d_logits
             columns = slice(head * DK, (head + 1) * DK)
             d_mixer = d_mixer_ref[rows, columns]
             gates = gate_ref[rows, columns]
@@ -262,6 +286,7 @@
             weighted = d_normed * gain
             inner = jnp.mean(weighted * mixed, axis=-1, keepdims=True)
             d_out = scale * weighted - mixed * (scale * scale * scale) * inner
+            yield
             convs = [conv_ref[which, rows, columns] for which in range(3)]
             logistics = [sigmoid(conv) for conv in convs]
             acts = [conv * logistic for conv, logistic in zip(convs, logistics)]
@@ -281,12 +306,14 @@
             new_value = new_ref[rows, columns]
             new_parts = parts_of(new_value)
             before_parts = parts_of(states_ref[head, rows, :])
+            yield
             d_after = d_state[head]
             d_after_parts = parts_of(d_after)
             d_out_parts = parts_of(d_out)
             d_new = product(parts_of(probes), d_out_parts, 0, 0) + closing * product(
                 (keys,), d_after_parts
             )
+            yield
             opened_out = opening * d_out
             opened_new = opening * d_new
             d_state[head] = (
@@ -294,17 +321,23 @@
                 + product((queries,), parts_of(opened_out), 0, 0)
                 - product(w_parts, parts_of(opened_new), 0, 0)
             )
+            yield
             d_probe = product(d_out_parts, new_parts, 1, 1) * inclusive
             d_probe_parts = parts_of(d_probe)
+            yield
             d_query = product(d_probe_parts, (keys,)) + product(
                 parts_of(opened_out), before_parts, 1, 1
             )
+            yield
             d_key = product(d_probe_parts, (queries,), 0, 0) + closing * product(
                 new_parts, d_after_parts, 1, 1
             )
+            yield
             d_w = -product(parts_of(opened_new), before_parts, 1, 1)
+            yield
             right_w = product(solve_parts, parts_of(d_w), 0, 0)
             right_u = product(solve_parts, parts_of(d_new), 0, 0)
+            yield
             d_lower = (
                 -(
                     product(parts_of(right_w), w_parts, 1, 1)
@@ -312,6 +345,7 @@
                 )
                 * strict
             )
+            yield
             d_beta = jnp.sum(
                 right_w * keys.astype(FULL) + right_u * values.astype(FULL) + d_lower * gram,
                 axis=-1,
@@ -321,6 +355,7 @@
             d_logits = d_logits + jnp.where(
                 lanes == head, d_beta * beta_col * (1.0 - beta_col), 0.0
             )
+            yield
             d_gram_parts = parts_of(beta * d_lower)
             d_key = (
                 d_key
@@ -328,7 +363,9 @@
                 + product(d_gram_parts, (keys,))
                 + product(d_gram_parts, (keys,), 0, 0)
             )
+            yield
             d_value = beta * right_u
+            yield
             d_acts = [
                 scales[which] * grads
                 - acts[which]
@@ -361,6 +398,8 @@
                 for lag_step in range(CONV):
                     place = slice(tap + lag_step, tap + lag_step + 1)
                     d_taps_ref[place, columns] = d_taps_ref[place, columns] + d_taps[lag_step]
+
+        side_by_side(work(head) for head in range(head_count))
         d_logit_ref[rows, :] = d_logits.astype(LOW)
         d_gain_ref[...] = d_gain_ref[...] + d_gain
         return carry
@@ -448,7 +487,7 @@
 
 FFN_TILE = 128
 FFN_ROWS = 1024
-TICKS = 8
+TICKS = 9
 X_SENT, X_GOT, OWN, IN_SENT, IN_GOT, MID_SENT, MID_GOT, OUT_SENT, OUT_GOT, BACK_SENT, BACK_GOT, KEPT = range(12)
 
 
@@ -492,8 +531,8 @@
         d_down_ref[...] = total[2 * tile :].astype(LOW)
 
 
-def ffn_and_sums(orders, ticks, *refs):
-    count = len(orders)
+def ffn_and_sums(plans, ticks, *refs):
+    count = len(plans)
     ffn_refs, given = refs[:5], refs[5 : 5 + count]
     d_refs, made = refs[5 + count : 8 + count], refs[8 + count : 8 + 2 * count]
     scratch = refs[8 + 2 * count :]
@@ -545,6 +584,7 @@
         return dict(
             across=lambda: remote(given[which].at[theirs], halves[which], X_SENT, X_GOT, pair),
             own=lambda: local(given[which].at[mine], owns[which], OWN),
+            whole=lambda: local(given[which], halves[which], OWN),
             inward=lambda: remote(halves[which], ins[which], IN_SENT, IN_GOT, near),
             middle=lambda: remote(halves[which], mids[which], MID_SENT, MID_GOT, far),
             outward=lambda: remote(halves[which], made[which].at[mine], OUT_SENT, OUT_GOT, near),
@@ -560,9 +600,13 @@
             copies["across"]().start()
             copies["own"]().start()
         elif number == 1:
-            copies["own"]().wait()
-            copies["across"]().wait()
-            add_into(halves[which], owns[which])
+            if plans[which][0] is None:
+                copies["whole"]().start()
+                copies["whole"]().wait()
+            else:
+                copies["own"]().wait()
+                copies["across"]().wait()
+                add_into(halves[which], owns[which])
 
             @pl.when(end)
             def _():
@@ -613,14 +657,14 @@
 
         @pl.when(step == ticks[tick])
         def _(tick=tick):
-            for which, order in reversed(list(enumerate(orders))):
-                if 0 <= tick - order <= 5:
-                    stage(which, tick - order)
+            for which, places in enumerate(plans):
+                if tick in places:
+                    stage(which, places.index(tick))
 
     ffn_step(*ffn_refs, *d_refs, total)
 
 
-def run_ffn_and_sums(rows, grads, gate_weight, up_weight, down_weight, given, orders):
+def run_ffn_and_sums(rows, grads, gate_weight, up_weight, down_weight, given, plans):
     total_rows, features = rows.shape
     units = gate_weight.shape[1]
     block_rows = min(FFN_ROWS, total_rows)
@@ -631,9 +675,15 @@
     down = pl.BlockSpec((FFN_TILE, features), lambda tile, block: (tile, 0))
     tall = pl.BlockSpec((block_rows, features), lambda tile, block: (block, 0))
     anywhere = [pl.BlockSpec(memory_space=pl.ANY)] * len(given)
-    half_shapes = [(values.shape[0] // 2, values.shape[1]) for values in given]
+    half_shapes = [
+        values.shape if places[0] is None else (values.shape[0] // 2, values.shape[1])
+        for values, places in zip(given, plans)
+    ]
+    own_shapes = [
+        (16, 128) if places[0] is None else shape for shape, places in zip(half_shapes, plans)
+    ]
     return pl.pallas_call(
-        functools.partial(ffn_and_sums, orders, ticks),
+        functools.partial(ffn_and_sums, plans, ticks),
         grid=(tiles, blocks),
         in_specs=[tall, tall, across, across, down] + anywhere,
         out_specs=[across, across, down] + anywhere,
@@ -642,12 +692,15 @@
             jax.ShapeDtypeStruct((features, units), LOW),
             jax.ShapeDtypeStruct((units, features), LOW),
         ]
-        + [jax.ShapeDtypeStruct(values.shape, LOW) for values in given],
+        + [jax.ShapeDtypeStruct((2 * rows, width), LOW) for rows, width in half_shapes],
         scratch_shapes=[
             pltpu.VMEM((3 * FFN_TILE, features), FULL),
             pltpu.SemaphoreType.DMA((len(given), 12)),
         ]
-        + [pltpu.VMEM(shape, LOW) for kind in range(4) for shape in half_shapes],
+        + [
+            pltpu.VMEM(shape, LOW)
+            for shape in half_shapes + own_shapes + half_shapes + half_shapes
+        ],
         compiler_params=pltpu.CompilerParams(
             vmem_limit_bytes=60 * 1024 * 1024, collective_id=0, has_side_effects=True
         ),
@@ -660,19 +713,20 @@
     )(rows, grads, gate_weight, up_weight, down_weight, *given)
 
 
-def by_pairs(values, bit):
-    count = lax.axis_size("mp")
-    return lax.ppermute(values, "mp", [(here, here ^ bit) for here in range(count)])
-
-
-def gather_rows(values):
-    if lax.axis_size("mp") != 4:
-        return lax.all_gather(values, "mp", axis=0, tiled=True)
-    here = lax.axis_index("mp")
-    other_core = by_pairs(values, 1)
-    other_chip = by_pairs(values, 2)
-    far = by_pairs(other_chip, 1)
-    odd_core, odd_chip = here % 2 == 1, here // 2 == 1
+CHIP_AXES = ("y", "core")
+
+
+def swapped(values, name):
+    return lax.ppermute(values, name, [(0, 1), (1, 0)])
+
+
+def gather_rows(values, mp_axes):
+    if mp_axes != CHIP_AXES:
+        return lax.all_gather(values, mp_axes, axis=0, tiled=True)
+    other_core = swapped(values, "core")
+    other_chip = swapped(values, "y")
+    far = swapped(other_chip, "core")
+    odd_core, odd_chip = lax.axis_index("core") == 1, lax.axis_index("y") == 1
     near_pair = jnp.where(
         odd_core,
         jnp.concatenate([other_core, values]),
@@ -686,18 +740,32 @@
     )
 
 
-def scatter_sum(values):
-    if lax.axis_size("mp") != 4:
-        return lax.psum_scatter(values, "mp", scatter_dimension=0, tiled=True)
-    here = lax.axis_index("mp")
-    core, chip = here % 2, here // 2
+def scatter_near(values):
+    core, chip = lax.axis_index("core"), lax.axis_index("y")
     quarters = values.reshape(2, 2, values.shape[0] // 4, values.shape[1])
     sent = lax.dynamic_index_in_dim(quarters, 1 - core, 1, keepdims=False).astype(LOW)
     kept = lax.dynamic_index_in_dim(quarters, core, 1, keepdims=False)
-    halves = kept + by_pairs(sent, 1).astype(FULL)
+    halves = kept + swapped(sent, "core").astype(FULL)
     sent = lax.dynamic_index_in_dim(halves, 1 - chip, 0, keepdims=False).astype(LOW)
-    kept = lax.dynamic_index_in_dim(halves, chip, 0, keepdims=False)
-    return kept + by_pairs(sent, 2).astype(FULL)
+    return lax.dynamic_index_in_dim(halves, chip, 0, keepdims=False), sent
+
+
+def scatter_sum(values, mp_axes):
+    if mp_axes != CHIP_AXES:
+        return lax.psum_scatter(values, mp_axes, scatter_dimension=0, tiled=True)
+    kept, sent = scatter_near(values)
+    return kept + swapped(sent, "y").astype(FULL)
+
+
+def half_of(values, which):
+    size = values.shape[0] // 2
+    return lax.dynamic_slice_in_dim(values, which * size, size, 0)
+
+
+def pair_sum(values):
+    side = lax.axis_index("dp") % 2
+    sent = lax.ppermute(half_of(values, 1 - side), "dp", [(here, here ^ 1) for here in range(8)])
+    return (half_of(values, side).astype(FULL) + sent.astype(FULL)).astype(LOW)
 
 
 def inverse_root(values, epsilon):
@@ -750,6 +818,7 @@
 
 
 def on_device(
+    mp_axes,
     inputs,
     doc_lengths,
     cotangent,
@@ -768,43 +837,51 @@
     down_weight,
 ):
     local_rows = inputs.shape[0]
-    group_rows = local_rows * lax.axis_size("mp")
+    group_rows = local_rows * math.prod(lax.axis_size(name) for name in mp_axes)
     width = query_weight.shape[1]
     head_count = width // DK
     meta, ids = document_tables(doc_index(doc_lengths, group_rows // doc_lengths.shape[0]))
     taps = conv_weight.reshape(3 * CONV, width)
     gain_row = head_gain[None, :]
 
-    everyone = group_rows * lax.axis_size("dp") <= ROWS_MOST and lax.axis_size("dp") == 8
+    everyone = (
+        mp_axes == CHIP_AXES
+        and lax.axis_size("dp") == 8
+        and group_rows * lax.axis_size("dp") <= ROWS_MOST
+    )
     if everyone:
-        all_grad_rows = lax.all_gather(cotangent, ("dp", "mp"), axis=0, tiled=True)
+        all_grad_rows = lax.all_gather(cotangent, ("dp", *mp_axes), axis=0, tiled=True)
     residual_in = inputs.astype(FULL)
     scale_one = inverse_root(residual_in, EPS_NORM)
-    normed = gather_rows((residual_in * scale_one * norm_gain).astype(LOW))
+    normed = gather_rows((residual_in * scale_one * norm_gain).astype(LOW), mp_axes)
     weights = (query_weight, key_weight, value_weight, gating_weight)
     projections = tuple(dot_full("td,df->tf", normed, weight) for weight in weights)
     logits = dot_full("td,df->tf", normed, beta_weight)
     mixer_low, *kept = run_mixer_forward(projections, logits, taps, gain_row, meta, ids)
-    attended = scatter_sum(dot_full("tf,fd->td", mixer_low, output_weight))
+    attended = scatter_sum(dot_full("tf,fd->td", mixer_low, output_weight), mp_axes)
     residual_mid = residual_in + attended
     scale_two = inverse_root(residual_mid, EPS_NORM)
     ffn_local = (residual_mid * scale_two * ffn_gain).astype(LOW)
-    ffn_input = gather_rows(ffn_local)
+    ffn_input = gather_rows(ffn_local, mp_axes)
     if everyone:
-        ffn_input, all_grad_rows = lax.optimization_barrier((ffn_input, all_grad_rows))
-        all_ffn_input = lax.all_gather(ffn_local, ("dp", "mp"), axis=0, tiled=True)
+        half_rows = lax.dynamic_slice_in_dim(
+            ffn_input, lax.axis_index("core") * (group_rows // 2), group_rows // 2, 0
+        )
+        all_ffn_input = lax.all_gather(half_rows, ("dp", "core"), axis=0, tiled=True)
         grad_rows = lax.dynamic_slice_in_dim(
             all_grad_rows, lax.axis_index("dp") * group_rows, group_rows, 0
         )
     else:
-        grad_rows = gather_rows(cotangent)
+        grad_rows = gather_rows(cotangent, mp_axes)
 
     hidden_low, d_gate_low, d_up_low = ffn_terms(
         ffn_input, grad_rows, gate_weight, up_weight, down_weight
     )
     d_ffn_norm = scatter_sum(
-        dot_full("tf,df->td", d_gate_low, gate_weight) + dot_full("tf,df->td", d_up_low, up_weight)
-    )
+        dot_full("tf,df->td", d_gate_low, gate_weight) + dot_full("tf,df->td", d_up_low, up_weight),
+        mp_axes,
+    )
+    ffn_part = dot_full("tf,fd->td", hidden_low, down_weight)
     d_ffn = None
     if not everyone:
         d_ffn = (
@@ -815,60 +892,81 @@
 
     d_mid = cotangent.astype(FULL) + norm_back(residual_mid, scale_two, ffn_gain, d_ffn_norm)
     ffn_gain_part = jnp.sum(d_ffn_norm * residual_mid * scale_two, axis=0)
-    mid_rows = gather_rows(d_mid.astype(LOW))
+    mid_rows = gather_rows(d_mid.astype(LOW), mp_axes)
+    mid_rows, ffn_part = lax.optimization_barrier((mid_rows, ffn_part))
+    ffn_out = scatter_sum(ffn_part, mp_axes)
+    output = (residual_mid + ffn_out).astype(LOW)
+    d_output_w = dot_full("tf,td->fd", mixer_low, mid_rows).astype(LOW)
     d_mixer = dot_full("td,fd->tf", mid_rows, output_weight)
     d_gate_low = gate_back(d_mixer, kept[5], projections[3], head_gain)
-    early = [
-        dot_full("tf,td->fd", mixer_low, mid_rows).astype(LOW),
-        dot_full("td,tf->df", normed, d_gate_low).astype(LOW),
-    ]
-    d_mixer, *early = lax.optimization_barrier((d_mixer, *early))
-    early = lax.psum(early, "dp")
+    d_gating_w = dot_full("td,tf->df", normed, d_gate_low).astype(LOW)
+    d_mixer, d_output_w, d_gating_w = lax.optimization_barrier((d_mixer, d_output_w, d_gating_w))
+    if everyone:
+        d_output_w, d_gating_w = pair_sum(d_output_w), pair_sum(d_gating_w)
     *low_grads, d_logits, d_taps, head_gain_part = run_mixer_backward(
         d_mixer, projections, logits, taps, gain_row, meta, ids, kept
     )
     d_logits = d_logits[:, :head_count]
+    d_beta_w = dot_full("td,tf->df", normed, d_logits)
+    small = jnp.concatenate([d_beta_w.reshape(-1), d_taps.reshape(-1)])
+    size = small.shape[0]
+    padded = -(-size // (32 * 512)) * 32 * 512
+    small = jnp.pad(small, (0, padded - size)).reshape(-1, 512).astype(LOW)
+    narrow = [d_output_w, d_gating_w]
+    narrow += [dot_full("td,tf->df", normed, grads).astype(LOW) for grads in low_grads]
+    narrow.append(small)
     summed = dot_full("tf,df->td", d_logits, beta_weight)
     for grads, weight in zip(low_grads + [d_gate_low], weights):
         summed = summed + dot_full("tf,df->td", grads, weight)
-    summed, hidden_low = lax.optimization_barrier((summed, hidden_low))
-    d_normed = scatter_sum(summed)
-    ffn_out = scatter_sum(dot_full("tf,fd->td", hidden_low, down_weight))
-    output = (residual_mid + ffn_out).astype(LOW)
+    if everyone:
+        kept_rows, sent_rows = scatter_near(summed)
+        sent_rows, *narrow = lax.optimization_barrier((sent_rows, *narrow))
+        got_rows = swapped(sent_rows, "y")
+        *d_ffn, d_output_w, d_gating_w, d_query_w, d_key_w, d_value_w, small = run_ffn_and_sums(
+            all_ffn_input,
+            all_grad_rows,
+            gate_weight,
+            up_weight,
+            down_weight,
+            narrow,
+            (
+                (None, 0, 1, 2, 3, 4),
+                (None, 1, 2, 3, 4, 5),
+                (0, 2, 3, 4, 5, 6),
+                (1, 3, 4, 5, 6, 7),
+                (2, 4, 5, 6, 7, 8),
+                (2, 4, 5, 6, 7, 8),
+            ),
+        )
+        got_rows, small = lax.optimization_barrier((got_rows, small))
+        d_normed = kept_rows + got_rows.astype(FULL)
+    else:
+        d_normed = scatter_sum(summed, mp_axes)
+        d_output_w, d_gating_w, d_query_w, d_key_w, d_value_w, small = lax.psum(narrow, "dp")
+        d_ffn = lax.psum([grads.astype(LOW) for grads in d_ffn], "dp")
     input_grad = d_mid + norm_back(residual_in, scale_one, norm_gain, d_normed)
     norm_gain_part = jnp.sum(d_normed * residual_in * scale_one, axis=0)
-    late = [dot_full("td,tf->df", normed, grads).astype(LOW) for grads in low_grads]
-    d_beta_w = dot_full("td,tf->df", normed, d_logits)
-
     gains = jnp.concatenate([norm_gain_part, ffn_gain_part, head_gain_part[0]])
-    if lax.axis_size("mp") == 4:
-        for bit in (1, 2):
-            gains = gains + by_pairs(gains, bit)
-    else:
-        gains = lax.psum(gains, "mp")
-    small = jnp.concatenate([d_beta_w.reshape(-1), d_taps.reshape(-1), gains])
-    size = small.shape[0]
-    padded = -(-size // (32 * 512)) * 32 * 512
-    small = jnp.pad(small, (0, padded - size)).reshape(-1, 512).astype(LOW)
-    late.append(small)
-    if everyone:
-        *d_ffn, d_query_w, d_key_w, d_value_w, small = run_ffn_and_sums(
-            all_ffn_input, all_grad_rows, gate_weight, up_weight, down_weight, late, (0, 1, 2, 2)
-        )
-    else:
-        d_query_w, d_key_w, d_value_w, small = lax.psum(late, "dp")
-        d_ffn = lax.psum([grads.astype(LOW) for grads in d_ffn], "dp")
     d_gate_w, d_up_w, d_down = [grads.astype(FULL) for grads in d_ffn]
-    proj_grads = [
-        grads.astype(FULL) for grads in (d_query_w, d_key_w, d_value_w, early[1])
-    ]
-    d_output_w = early[0].astype(FULL)
+    proj_grads = [grads.astype(FULL) for grads in (d_query_w, d_key_w, d_value_w, d_gating_w)]
+    d_output_w = d_output_w.astype(FULL)
+    wide = [d_gate_w, d_up_w, d_down, d_output_w] + proj_grads
+    place = 0
+    for name in (*mp_axes, "dp"):
+        count = lax.axis_size(name)
+        bit = 1
+        while bit < count:
+            got = lax.ppermute(gains, name, [(here, here ^ bit) for here in range(count)])
+            if place < len(wide):
+                got, wide[place] = lax.optimization_barrier((got, wide[place]))
+            gains = gains + got
+            place, bit = place + 1, 2 * bit
+    d_gate_w, d_up_w, d_down, d_output_w, *proj_grads = wide
     small = small.astype(FULL)
     small = small.reshape(-1)
     beta_size, taps_size = d_beta_w.size, taps.size
     d_beta_w = small[:beta_size].reshape(d_beta_w.shape)
     d_conv = small[beta_size : beta_size + taps_size].reshape(conv_weight.shape)
-    gains = small[beta_size + taps_size : size]
     features = inputs.shape[1]
     return (
         output,
@@ -890,44 +988,21 @@
 
 
 def solution(mesh):
-    rows, columns = P(("dp", "mp"), None), P(None, "mp")
+    mp_axes = ("mp",)
+    if mesh.shape["mp"] == 4:
+        mp_axes = CHIP_AXES
+        mesh = jax.sharding.Mesh(mesh.devices.reshape(-1, 2, 2), ("dp", *CHIP_AXES))
+    rows, columns, every = P(("dp", *mp_axes), None), P(None, mp_axes), P()
+    heads = P(None, None, mp_axes)
+    units = P(mp_axes, None)
     return jax.shard_map(
-        on_device,
+        functools.partial(on_device, mp_axes),
         mesh=mesh,
-        in_specs=(
-            rows,
-            P("dp", None),
-            rows,
-            P(),
-            columns,
-            columns,
-            columns,
-            columns,
-            columns,
-            P(None, None, "mp"),
-            P(),
-            P("mp", None),
-            P(),
-            columns,
-            columns,
-            P("mp", None),
-        ),
-        out_specs=(
-            rows,
-            rows,
-            P(),
-            columns,
-            columns,
-            columns,
-            columns,
-            columns,
-            P(None, None, "mp"),
-            P(),
-            P("mp", None),
-            P(),
-            columns,
-            columns,
-            P("mp", None),
-        ),
+        in_specs=(rows, P("dp", None), rows, every)
+        + (columns,) * 5
+        + (heads, every, units, every, columns, columns, units),
+        out_specs=(rows, rows, every)
+        + (columns,) * 5
+        + (heads, every, units, every, columns, columns, units),
         check_vma=False,
     )

time: 632 us -> 575 us (0.910)
  Pallas kernels: 326 us -> 253 us
  waiting for transfers between devices: 96.9 us -> 111 us
  matrix products: 67 us -> 75.2 us
    pallas_call x1, Pallas kernels: 249 us -> 211 us  [run_ffn_and_sums(): pl.pallas_call(functools.partial(ffn_and_sums, plans, ticks), grid=(tiles...]
    pallas_call x1, Pallas kernels: 48.9 us -> 20.6 us  [run_mixer_forward(): pl.pallas_call(functools.partial(mixer_forward, head_count), out_shape=(j...]
    ppermute x19 -> x24, waiting for transfers between devices: 96.2 us -> 110 us  [the longest x17 86.7 us: swapped(): return lax.ppermute(values, name, [(0, 1), (1, 0)])]
    dot_general x24, matrix products: 67 us -> 75.2 us  [dot_full(): return jnp.einsum(equation, left, right, preferred_element_type=FULL)]
    pallas_call x1, Pallas kernels: 27.5 us -> 21.1 us  [run_mixer_backward(): pl.pallas_call(functools.partial(mixer_backward, head_count), out_shape=(...]
    unnamed x115 -> x127, local copies, waits for them, and re-layouts: 12.8 us -> 9.73 us
    ppermute x19 -> x24, starting transfers between devices: 17 us -> 15.8 us  [the longest x17 11.2 us: swapped(): return lax.ppermute(values, name, [(0, 1), (1, 0)])]
  transfers between devices with their start and end apart: 22 -> 26, of which waited for: 10 -> 12; matrix products, arithmetic and copies ran while one was open for 24% -> 29% of each run, Pallas kernels for 52% -> 44%
where the time goes in v4:
time: 575 us; the launch traced here: 569 us
  Pallas kernels  253 us (44%)
  waiting for transfers between devices  111 us (19%)
  matrix products  75.2 us (13%)
  other arithmetic  74.2 us (13%)
  local copies, waits for them, and re-layouts  24.4 us (4%)
  starting transfers between devices  15.9 us (3%)
  between operations  15.4 us (3%)
    pallas_call x1, Pallas kernels, run_ffn_and_sums(): pl.pallas_call(functools.partial(ffn_and_sums, plans, ticks), grid=(tiles...  211 us
    ppermute x17, waiting for transfers between devices, swapped(): return lax.ppermute(values, name, [(0, 1), (1, 0)])  86.7 us
    dot_general x24, matrix products, dot_full(): return jnp.einsum(equation, left, right, preferred_element_type=FULL)  75.2 us
    pallas_call x1, Pallas kernels, run_mixer_backward(): pl.pallas_call(functools.partial(mixer_backward, head_count), out_shape=(...  21.1 us
    pallas_call x1, Pallas kernels, run_mixer_forward(): pl.pallas_call(functools.partial(mixer_forward, head_count), out_shape=(j...  20.6 us
    ppermute x2, waiting for transfers between devices, pair_sum(): lax.ppermute(half_of(values, 1 - side), 'dp', [(here, here ^ 1) for here...  17.8 us
    convert_element_type x3, other arithmetic, on_device(): d_gate_w, d_up_w, d_down = [grads.astype(FULL) for grads in d_ffn]  16.3 us
  transfers between devices with their start and end apart: 26, of which 12 were waited for; matrix products, arithmetic and copies ran while one was open for 29% of the time, Pallas kernels for 44%

profile of v4, /device:TPU:0, one launch (start us, length us, event | category | flops | bytes accessed | tf_op | source)
XLA Modules:
  0.0 569.4 jit_solution(6677227043097294340)
XLA Ops:
  15.6 13.5 %collective-permute-done = bf16[128,2048]{1,0:T(8,128)(2,1)S(1)} collective-permute-done((bf16[128,2048]{1,0:T(8,128)(2,1)S(1)}, bf16[128,2048]{1,0:T(8,128)(2,1)S(1)}, u32[]{:S(2)}, u32[]{:S(2)}) %collective-permute-start) | collective-permute-done | bytes 524320 | tf_op jit(solution)/shard_map/ppermute | solution.py:720
  46.8 20.6 %mixer_forward.1 = (bf16[512,512]{1,0:T(8,128)(2,1)}, f32[3,512,512]{2,1,0:T(8,128)}, f32[4,512,128]{2,1,0:T(8,128)}, f32[512,512]{1,0:T(8,128)}, f32[512,512]{1...) custom-call(f32[512,512]{1,0:T(8,128)} %fusion.47.query_ref, ...), custom_call_target="tpu_custom_call" | custom-call | tf_op jit(solution)/shard_map/mixer_forward/pallas_call | solution.py:419
  78.5 2.6 collective-permute-start.4
  81.1 24.0 %collective-permute-done.4 = bf16[128,2048]{1,0:T(8,128)(2,1)} collective-permute-done((bf16[128,2048]{1,0:T(8,128)(2,1)S(1)}, bf16[128,2048]{1,0:T(8,128)(2,1)}, u32[]{:S(2)}, u32[]{:S(2)}) %collective-permute-start.4) | collective-permute-done | bytes 524320 | tf_op jit(solution)/shard_map/ppermute | solution.py:720
  110.0 21.7 %collective-permute-done.5 = bf16[128,2048]{1,0:T(8,128)(2,1)} collective-permute-done((bf16[128,2048]{1,0:T(8,128)(2,1)}, bf16[128,2048]{1,0:T(8,128)(2,1)}, u32[]{:S(2)}, u32[]{:S(2)}) %collective-permute-start.5) | collective-permute-done | bytes 524320 | tf_op jit(solution)/shard_map/ppermute | solution.py:720
  139.5 8.4 %fusion.54 = f32[512,1408]{1,0:T(8,128)} fusion(bf16[512,2048]{1,0:T(8,128)(2,1)} %copy-done.14, bf16[2048,1408]{1,0:T(8,128)(2,1)} %refs_2_.1), kind=kOutput, calls=%fused_computation.131 | convolution fusion | flops 2952790016 | bytes 10747904 | tf_op jit(solution)/shard_map/td,df->tf/dot_general | solution.py:806
  147.9 7.9 %fusion.53 = f32[512,1408]{1,0:T(8,128)} fusion(bf16[512,2048]{1,0:T(8,128)(2,1)S(1)} %copy-done.15, bf16[2048,1408]{1,0:T(8,128)(2,1)} %refs_3_.1), kind=kOutput, calls=%fused_computation.130 | convolution fusion | flops 2952790016 | bytes 10747904 | tf_op jit(solution)/shard_map/td,df->tf/dot_general | solution.py:806
  155.8 7.5 %fusion.1 = f32[512,1408]{1,0:T(8,128)S(1)} fusion(bf16[1408,2048]{1,0:T(8,128)(2,1)} %refs_4_.1, bf16[4096,2048]{1,0:T(8,128)(2,1)} %all-gather.3.cloned.1.call-done.refs_1_, s32[]{:T(128)S(6)} %select_n.106), kind=kOutput, calls=%fused_computation.32 | convolution fusion | flops 2952790016 | bytes 10747908 | tf_op jit(solution)/shard_map/td,fd->tf/dot_general | solution.py:806
  163.3 6.9 %fusion.3 = f32[512,2048]{1,0:T(8,128)S(1)} fusion(bf16[2048,1408]{1,0:T(8,128)(2,1)} %refs_2_.1, f32[512,1408]{1,0:T(8,128)S(1)} %copy-done.55, f32[512,1408]{1,0:T(8,128)S(1)} %fusion.1, f32[512,1408]{1,0:T(8,128)S(1)} %copy-done.56), kind=kOutput, calls=%fused_computation.34 | convolution fusion | flops 2959998976 | bytes 18612224 | tf_op jit(solution)/shard_map/tf,df->td/dot_general | solution.py:806
  170.3 3.5 convolution_add_fusion
  177.1 14.0 %collective-permute-done.9 = bf16[128,2048]{1,0:T(8,128)(2,1)S(1)} collective-permute-done((bf16[128,2048]{1,0:T(8,128)(2,1)S(1)}, bf16[128,2048]{1,0:T(8,128)(2,1)S(1)}, u32[]{:S(2)}, u32[]{:S(2)}) %collective-permute-start.9) | collective-permute-done | bytes 524320 | tf_op jit(solution)/shard_map/ppermute | solution.py:720
  198.9 8.2 %collective-permute-done.10 = bf16[128,2048]{1,0:T(8,128)(2,1)} collective-permute-done((bf16[128,2048]{1,0:T(8,128)(2,1)}, bf16[128,2048]{1,0:T(8,128)(2,1)}, u32[]{:S(2)}, u32[]{:S(2)}) %collective-permute-start.10) | collective-permute-done | bytes 524320 | tf_op jit(solution)/shard_map/ppermute | solution.py:720
  207.2 7.5 %fusion.4 = f32[512,2048]{1,0:T(8,128)S(1)} fusion(bf16[1408,2048]{1,0:T(8,128)(2,1)} %refs_4_.1, f32[512,1408]{1,0:T(8,128)} %fusion.53, f32[512,1408]{1,0:T(8,128)} %fusion.54), kind=kOutput, calls=%fused_computation.35 | convolution fusion | flops 2957115392 | bytes 15728640 | tf_op jit(solution)/shard_map/tf,fd->td/dot_general | solution.py:806
  230.8 21.1 %mixer_backward.1 = (bf16[512,512]{1,0:T(8,128)(2,1)}, bf16[512,512]{1,0:T(8,128)(2,1)}, bf16[512,512]{1,0:T(8,128)(2,1)}, bf16[512,128]{1,0:T(8,128)(2,1)}, f32[12,512]{1,0:T(8,128)}, /*index=5*/f32[1,128]{1,0:T(1,128)}) custom-call(f32[512,512]{1,0:T(8,128)} %get-tuple-element.66.d_mixer_ref, f32[512,512]{1,0:T(8,128)} %fusion.47.query_ref, ...), custom_call_target="tpu_custom_call" | custom-call | tf_op jit(solution)/shard_map/mixer_backward/pallas_call | solution.py:443
  275.5 3.2 add_convert_fusion.refs_6_
  278.7 17.8 %collective-permute-done.16 = bf16[256,2048]{1,0:T(8,128)(2,1)} collective-permute-done((bf16[256,2048]{1,0:T(8,128)(2,1)S(1)}, bf16[256,2048]{1,0:T(8,128)(2,1)}, u32[]{:S(2)}, u32[]{:S(2)}) %collective-permute-start.16) | collective-permute-done | bytes 1048608 | tf_op jit(solution)/shard_map/ppermute | solution.py:767
  300.0 211.5 %ffn_and_sums.1 = (bf16[2048,1408]{1,0:T(8,128)(2,1)}, bf16[2048,1408]{1,0:T(8,128)(2,1)}, bf16[1408,2048]{1,0:T(8,128)(2,1)}, bf16[512,2048]{1,0:T(8,128)(2,1)}...) custom-call(bf16[4096,2048]{1,0:T(8,128)(2,1)} %all-gather.5.cloned., ...), custom_call_target="tpu_custom_call" | custom-call | flops 141733920768 | bytes 369098752 | tf_op jit(solution)/shard_map/ffn_and_sums/pallas_call | solution.py:685
  516.7 5.2 convert_element_type.285
  528.2 2.7 convert_element_type.290
  531.0 2.7 convert_element_type.291
  534.7 2.7 convert_element_type.293
  537.4 5.2 convert_element_type.286
  542.7 6.0 %convert_element_type.287 = f32[1408,2048]{1,0:T(8,128)} convert(bf16[1408,2048]{1,0:T(8,128)(2,1)S(1)} %bitcast.154) | non-fusion elementwise | flops 2883584 | bytes 17301504 | tf_op jit(solution)/shard_map/convert_element_type | solution.py:950
  549.2 3.3 collective-permute-done.21
  (278 shorter events, 126.3 us)
Async XLA Ops:
  7.2 148.6 %all-gather.3.cloned.1.call-start = ((), (), s32[]{:S(2)}) async-start(), calls=%async_computation | async-start | bytes 17301504 | tf_op jit(solution)/shard_map/all_gather | solution.py:853
  8.0 292.1 %all-gather.5.cloned.1.call-start = ((), (), s32[]{:S(2)}) async-start(), calls=%async_computation.1 | async-start | bytes 17825792 | tf_op jit(solution)/shard_map/all_gather | solution.py:870
  11.0 20.2 %collective-permute-start.2 = (bf16[128,2048]{1,0:T(8,128)(2,1)S(1)}, bf16[128,2048]{1,0:T(8,128)(2,1)}, u32[]{:S(2)}, u32[]{:S(2)}) collective-permute-start(bf16[128,2048]{1,0:T(8,128)(2,1)S(1)} %fusion.12), channel_id=1, source_target_pairs={{0,1},{1,0},{2,3},{3,2},{4,5},{5,4},{6,7},{7,6},{8,9},{9,8},{10,11... | collective-permute-start | bytes 1572872 | tf_op jit(solution)/shard_map/ppermute | solution.py:720
  11.5 17.6 %collective-permute-start = (bf16[128,2048]{1,0:T(8,128)(2,1)S(1)}, bf16[128,2048]{1,0:T(8,128)(2,1)S(1)}, u32[]{:S(2)}, u32[]{:S(2)}) collective-permute-start(bf16[128,2048]{1,0:T(8,128)(2,1)S(1)} %fusion.12), channel_id=1, source_target_pairs={{0,2},{2,0},{1,3},{3,1},{4,6},{6,4},{5,7},{7,5},{8,10},{10,8},{9,1... | collective-permute-start | bytes 1572872 | tf_op jit(solution)/shard_map/ppermute | solution.py:720
  29.2 3.6 collective-permute-start.1
  71.8 3.0 collective-permute-start.3
  78.5 26.7 %collective-permute-start.4 = (bf16[128,2048]{1,0:T(8,128)(2,1)S(1)}, bf16[128,2048]{1,0:T(8,128)(2,1)}, u32[]{:S(2)}, u32[]{:S(2)}) collective-permute-start(bf16[128,2048]{1,0:T(8,128)(2,1)S(1)} %fusion.25), channel_id=1, source_target_pairs={{0,2},{2,0},{1,3},{3,1},{4,6},{6,4},{5,7},{7,5},{8,10},{10,8},{9,1... | collective-permute-start | bytes 1572872 | tf_op jit(solution)/shard_map/ppermute | solution.py:720
  108.1 23.6 %collective-permute-start.5 = (bf16[128,2048]{1,0:T(8,128)(2,1)}, bf16[128,2048]{1,0:T(8,128)(2,1)}, u32[]{:S(2)}, u32[]{:S(2)}) collective-permute-start(bf16[128,2048]{1,0:T(8,128)(2,1)} %multiply_convert_fusion.6), channel_id=1, source_target_pairs={{0,2},{2,0},{1,3},{3,1},{4,6},{6,4},{5,7},{7,5},{8,10},{10,8},{9,1... | collective-permute-start | bytes 1572872 | tf_op jit(solution)/shard_map/ppermute | solution.py:720
  110.0 21.7 %collective-permute-start.7 = (bf16[128,2048]{1,0:T(8,128)(2,1)}, bf16[128,2048]{1,0:T(8,128)(2,1)}, u32[]{:S(2)}, u32[]{:S(2)}) collective-permute-start(bf16[128,2048]{1,0:T(8,128)(2,1)} %multiply_convert_fusion.6), channel_id=1, source_target_pairs={{0,1},{1,0},{2,3},{3,2},{4,5},{5,4},{6,7},{7,6},{8,9},{9,8},{10,11... | collective-permute-start | bytes 1572872 | tf_op jit(solution)/shard_map/ppermute | solution.py:720
  177.0 14.0 %collective-permute-start.9 = (bf16[128,2048]{1,0:T(8,128)(2,1)S(1)}, bf16[128,2048]{1,0:T(8,128)(2,1)S(1)}, u32[]{:S(2)}, u32[]{:S(2)}) collective-permute-start(bf16[128,2048]{1,0:T(8,128)(2,1)S(1)} %fusion.26), channel_id=1, source_target_pairs={{0,2},{2,0},{1,3},{3,1},{4,6},{6,4},{5,7},{7,5},{8,10},{10,8},{9,1... | collective-permute-start | bytes 1572872 | tf_op jit(solution)/shard_map/ppermute | solution.py:720
  193.6 13.6 %collective-permute-start.10 = (bf16[128,2048]{1,0:T(8,128)(2,1)}, bf16[128,2048]{1,0:T(8,128)(2,1)}, u32[]{:S(2)}, u32[]{:S(2)}) collective-permute-start(bf16[128,2048]{1,0:T(8,128)(2,1)} %get-tuple-element.203), channel_id=1, source_target_pairs={{0,2},{2,0},{1,3},{3,1},{4,6},{6,4},{5,7},{7,5},{8,10},{10,8},{9,1... | collective-permute-start | bytes 1572872 | tf_op jit(solution)/shard_map/ppermute | solution.py:720
  198.9 15.8 %collective-permute-start.12 = (bf16[128,2048]{1,0:T(8,128)(2,1)}, bf16[128,2048]{1,0:T(8,128)(2,1)S(1)}, u32[]{:S(2)}, u32[]{:S(2)}) collective-permute-start(bf16[128,2048]{1,0:T(8,128)(2,1)} %get-tuple-element.203), channel_id=1, source_target_pairs={{0,1},{1,0},{2,3},{3,2},{4,5},{5,4},{6,7},{7,6},{8,9},{9,8},{10,11... | collective-permute-start | bytes 1572872 | tf_op jit(solution)/shard_map/ppermute | solution.py:720
  207.1 9.9 %collective-permute-start.11 = (bf16[128,2048]{1,0:T(8,128)(2,1)}, bf16[128,2048]{1,0:T(8,128)(2,1)S(1)}, u32[]{:S(2)}, u32[]{:S(2)}) collective-permute-start(bf16[128,2048]{1,0:T(8,128)(2,1)} %collective-permute-done.10), channel_id=1, source_target_pairs={{0,1},{1,0},{2,3},{3,2},{4,5},{5,4},{6,7},{7,6},{8,9},{9,8},{10,11... | collective-permute-start | bytes 1572872 | tf_op jit(solution)/shard_map/ppermute | solution.py:720
  220.8 293.7 %collective-permute-start.13 = (bf16[2,128,2048]{2,1,0:T(8,128)(2,1)}, bf16[2,128,2048]{2,1,0:T(8,128)(2,1)}, u32[]{:S(2)}, u32[]{:S(2)}) collective-permute-start(bf16[2,128,2048]{2,1,0:T(8,128)(2,1)} %fusion.8), channel_id=1, source_target_pairs={{0,1},{1,0},{2,3},{3,2},{4,5},{5,4},{6,7},{7,6},{8,9},{9,8},{10,11... | collective-permute-start | bytes 3145736 | tf_op jit(solution)/shard_map/ppermute | solution.py:720
  229.4 46.0 %collective-permute-start.17 = (bf16[1024,512]{1,0:T(8,128)(2,1)}, bf16[1024,512]{1,0:T(8,128)(2,1)}, u32[]{:S(2)}, u32[]{:S(2)}) collective-permute-start(bf16[1024,512]{1,0:T(8,128)(2,1)} %constant_dynamic-slice_fusion.1), channel_id=1, source_target_pairs={{0,4},{4,0},{8,12},{12,8},{16,20},{20,16},{24,28},{28,24},{1,5},{5... | collective-permute-start | bytes 3145736 | tf_op jit(solution)/shard_map/ppermute | solution.py:767
  260.5 11.6 %collective-permute-start.15 = (bf16[2,128,2048]{2,1,0:T(8,128)(2,1)}, bf16[2,128,2048]{2,1,0:T(8,128)(2,1)}, u32[]{:S(2)}, u32[]{:S(2)}) collective-permute-start(bf16[2,128,2048]{2,1,0:T(8,128)(2,1)} %fusion.9), channel_id=1, source_target_pairs={{0,1},{1,0},{2,3},{3,2},{4,5},{5,4},{6,7},{7,6},{8,9},{9,8},{10,11... | collective-permute-start | bytes 3145736 | tf_op jit(solution)/shard_map/ppermute | solution.py:720
  270.8 25.7 %collective-permute-start.16 = (bf16[256,2048]{1,0:T(8,128)(2,1)S(1)}, bf16[256,2048]{1,0:T(8,128)(2,1)}, u32[]{:S(2)}, u32[]{:S(2)}) collective-permute-start(bf16[256,2048]{1,0:T(8,128)(2,1)S(1)} %constant_dynamic-slice_fusion.2), channel_id=1, source_target_pairs={{0,4},{4,0},{8,12},{12,8},{16,20},{20,16},{24,28},{28,24},{1,5},{5... | collective-permute-start | bytes 3145736 | tf_op jit(solution)/shard_map/ppermute | solution.py:767
  299.1 212.5 %collective-permute-start.18 = (bf16[128,2048]{1,0:T(8,128)(2,1)}, bf16[128,2048]{1,0:T(8,128)(2,1)S(1)}, u32[]{:S(2)}, u32[]{:S(2)}) collective-permute-start(bf16[128,2048]{1,0:T(8,128)(2,1)} %fusion.28), channel_id=1, source_target_pairs={{0,2},{2,0},{1,3},{3,1},{4,6},{6,4},{5,7},{7,5},{8,10},{10,8},{9,1... | collective-permute-start | bytes 1572872 | tf_op jit(solution)/shard_map/ppermute | solution.py:720
  513.4 8.5 %collective-permute-start.19 = (f32[4224]{0:T(1024)S(1)}, f32[4224]{0:T(1024)S(1)}, u32[]{:S(2)}, u32[]{:S(2)}) collective-permute-start(f32[4224]{0:T(1024)S(1)} %pad_maximum_fusion), channel_id=1, source_target_pairs={{0,2},{2,0},{1,3},{3,1},{4,6},{6,4},{5,7},{7,5},{8,10},{10,8},{9,1... | collective-permute-start | bytes 50696 | tf_op jit(solution)/shard_map/ppermute | solution.py:959
  521.9 26.7 %collective-permute-start.20 = (f32[4224]{0:T(1024)S(1)}, f32[4224]{0:T(1024)S(1)}, u32[]{:S(2)}, u32[]{:S(2)}) collective-permute-start(f32[4224]{0:T(1024)S(1)} %fusion.44), channel_id=1, source_target_pairs={{0,1},{1,0},{2,3},{3,2},{4,5},{5,4},{6,7},{7,6},{8,9},{9,8},{10,11... | collective-permute-start | bytes 50696 | tf_op jit(solution)/shard_map/ppermute | solution.py:959
  522.1 35.0 %collective-permute-start.14 = (bf16[128,2048]{1,0:T(8,128)(2,1)S(1)}, bf16[128,2048]{1,0:T(8,128)(2,1)S(1)}, u32[]{:S(2)}, u32[]{:S(2)}) collective-permute-start(bf16[128,2048]{1,0:T(8,128)(2,1)S(1)} %fusion.27), channel_id=1, source_target_pairs={{0,2},{2,0},{1,3},{3,1},{4,6},{6,4},{5,7},{7,5},{8,10},{10,8},{9,1... | collective-permute-start | bytes 1572872 | tf_op jit(solution)/shard_map/ppermute | solution.py:720
  548.7 3.8 collective-permute-start.21
  552.5 3.8 collective-permute-start.22
  556.3 4.7 collective-permute-start.23
  (65 other events, 1140.9 us)
Sparse Core Ops, SparseCore 0:
  10.9 139.3 all-gather.2
  152.5 141.4 all-gather.4

commit v5 on v4

--- a/solution.py
+++ b/solution.py
@@ -881,7 +881,6 @@
         dot_full("tf,df->td", d_gate_low, gate_weight) + dot_full("tf,df->td", d_up_low, up_weight),
         mp_axes,
     )
-    ffn_part = dot_full("tf,fd->td", hidden_low, down_weight)
     d_ffn = None
     if not everyone:
         d_ffn = (
@@ -893,9 +892,6 @@
     d_mid = cotangent.astype(FULL) + norm_back(residual_mid, scale_two, ffn_gain, d_ffn_norm)
     ffn_gain_part = jnp.sum(d_ffn_norm * residual_mid * scale_two, axis=0)
     mid_rows = gather_rows(d_mid.astype(LOW), mp_axes)
-    mid_rows, ffn_part = lax.optimization_barrier((mid_rows, ffn_part))
-    ffn_out = scatter_sum(ffn_part, mp_axes)
-    output = (residual_mid + ffn_out).astype(LOW)
     d_output_w = dot_full("tf,td->fd", mixer_low, mid_rows).astype(LOW)
     d_mixer = dot_full("td,fd->tf", mid_rows, output_weight)
     d_gate_low = gate_back(d_mixer, kept[5], projections[3], head_gain)
@@ -906,6 +902,9 @@
     *low_grads, d_logits, d_taps, head_gain_part = run_mixer_backward(
         d_mixer, projections, logits, taps, gain_row, meta, ids, kept
     )
+    d_logits, hidden_low = lax.optimization_barrier((d_logits, hidden_low))
+    ffn_out = scatter_sum(dot_full("tf,fd->td", hidden_low, down_weight), mp_axes)
+    output = (residual_mid + ffn_out).astype(LOW)
     d_logits = d_logits[:, :head_count]
     d_beta_w = dot_full("td,tf->df", normed, d_logits)
     small = jnp.concatenate([d_beta_w.reshape(-1), d_taps.reshape(-1)])

time: 575 us -> 574 us (level)
  matrix products: 75.2 us -> 67.9 us
    dot_general x24, matrix products: 75.2 us -> 67.9 us  [dot_full(): return jnp.einsum(equation, left, right, preferred_element_type=FULL)]
    unnamed x127 -> x135, local copies, waits for them, and re-layouts: 9.73 us -> 13.8 us
  transfers between devices with their start and end apart: 26 -> 26, of which waited for: 12 -> 12; matrix products, arithmetic and copies ran while one was open for 29% -> 27% of each run, Pallas kernels for 44% -> 45%
where the time goes in v5:
time: 574 us; the launch traced here: 569 us
  Pallas kernels  255 us (44%)
  waiting for transfers between devices  112 us (20%)
  other arithmetic  72.9 us (13%)
  matrix products  67.9 us (12%)
  local copies, waits for them, and re-layouts  27.7 us (5%)
  starting transfers between devices  17.7 us (3%)
  between operations  15.3 us (3%)
    pallas_call x1, Pallas kernels, run_ffn_and_sums(): pl.pallas_call(functools.partial(ffn_and_sums, plans, ticks), grid=(tiles...  213 us
    ppermute x17, waiting for transfers between devices, swapped(): return lax.ppermute(values, name, [(0, 1), (1, 0)])  91.9 us
    dot_general x24, matrix products, dot_full(): return jnp.einsum(equation, left, right, preferred_element_type=FULL)  67.9 us
    pallas_call x1, Pallas kernels, run_mixer_backward(): pl.pallas_call(functools.partial(mixer_backward, head_count), out_shape=(...  21.9 us
    pallas_call x1, Pallas kernels, run_mixer_forward(): pl.pallas_call(functools.partial(mixer_forward, head_count), out_shape=(j...  20.5 us
    convert_element_type x3, other arithmetic, on_device(): d_gate_w, d_up_w, d_down = [grads.astype(FULL) for grads in d_ffn]  16.3 us
    ppermute x2, waiting for transfers between devices, pair_sum(): lax.ppermute(half_of(values, 1 - side), 'dp', [(here, here ^ 1) for here...  13.9 us
    unnamed x135, local copies, waits for them, and re-layouts  13.8 us
  transfers between devices with their start and end apart: 26, of which 12 were waited for; matrix products, arithmetic and copies ran while one was open for 27% of the time, Pallas kernels for 45%

profile of v5, /device:TPU:0, one launch (start us, length us, event | category | flops | bytes accessed | tf_op | source)
XLA Modules:
  0.0 568.7 jit_solution(5695933732472416710)
XLA Ops:
  15.6 13.5 %collective-permute-done = bf16[128,2048]{1,0:T(8,128)(2,1)S(1)} collective-permute-done((bf16[128,2048]{1,0:T(8,128)(2,1)S(1)}, bf16[128,2048]{1,0:T(8,128)(2,1)S(1)}, u32[]{:S(2)}, u32[]{:S(2)}) %collective-permute-start) | collective-permute-done | bytes 524320 | tf_op jit(solution)/shard_map/ppermute | solution.py:720
  46.7 20.5 %mixer_forward.1 = (bf16[512,512]{1,0:T(8,128)(2,1)}, f32[3,512,512]{2,1,0:T(8,128)}, f32[4,512,128]{2,1,0:T(8,128)}, f32[512,512]{1,0:T(8,128)}, f32[512,512]{1...) custom-call(f32[512,512]{1,0:T(8,128)} %fusion.47.query_ref, ...), custom_call_target="tpu_custom_call" | custom-call | tf_op jit(solution)/shard_map/mixer_forward/pallas_call | solution.py:419
  80.9 24.0 %collective-permute-done.4 = bf16[128,2048]{1,0:T(8,128)(2,1)} collective-permute-done((bf16[128,2048]{1,0:T(8,128)(2,1)S(1)}, bf16[128,2048]{1,0:T(8,128)(2,1)}, u32[]{:S(2)}, u32[]{:S(2)}) %collective-permute-start.4) | collective-permute-done | bytes 524320 | tf_op jit(solution)/shard_map/ppermute | solution.py:720
  109.9 21.8 %collective-permute-done.5 = bf16[128,2048]{1,0:T(8,128)(2,1)} collective-permute-done((bf16[128,2048]{1,0:T(8,128)(2,1)}, bf16[128,2048]{1,0:T(8,128)(2,1)}, u32[]{:S(2)}, u32[]{:S(2)}) %collective-permute-start.5) | collective-permute-done | bytes 524320 | tf_op jit(solution)/shard_map/ppermute | solution.py:720
  139.4 6.6 %fusion.53 = f32[512,1408]{1,0:T(8,128)S(1)} fusion(bf16[512,2048]{1,0:T(8,128)(2,1)} %copy-done.14, bf16[2048,1408]{1,0:T(8,128)(2,1)} %refs_2_.1), kind=kOutput, calls=%fused_computation.131 | convolution fusion | flops 2952790016 | bytes 10747904 | tf_op jit(solution)/shard_map/td,df->tf/dot_general | solution.py:806
  147.5 7.9 %multiply_convert_fusion = (bf16[512,1408]{1,0:T(8,128)(2,1)}, f32[512,1408]{1,0:T(8,128)}) fusion(f32[512,1408]{1,0:T(8,128)S(1)} %fusion.53, bf16[512,2048]{1,0:T(8,128)(2,1)S(1)} %copy-done.15, bf16[2048,1408]{1,0:T(8,128)(2,1)} %refs_3_.1), kind=kOutput, calls=%fused_computation.7 | convolution fusion | flops 2957115392 | bytes 15073280 | tf_op jit(solution)/shard_map/td,df->tf/dot_general | solution.py:806
  155.4 7.3 %fusion.1 = f32[512,1408]{1,0:T(8,128)S(1)} fusion(bf16[1408,2048]{1,0:T(8,128)(2,1)} %refs_4_.1, bf16[4096,2048]{1,0:T(8,128)(2,1)} %all-gather.3.cloned.1.call-done.refs_1_, s32[]{:T(128)S(6)} %select_n.106), kind=kOutput, calls=%fused_computation.32 | convolution fusion | flops 2952790016 | bytes 10747908 | tf_op jit(solution)/shard_map/td,fd->tf/dot_general | solution.py:806
  162.8 6.9 %fusion.3 = f32[512,2048]{1,0:T(8,128)S(1)} fusion(bf16[2048,1408]{1,0:T(8,128)(2,1)} %refs_2_.1, f32[512,1408]{1,0:T(8,128)S(1)} %copy-done.56, f32[512,1408]{1,0:T(8,128)S(1)} %fusion.1, f32[512,1408]{1,0:T(8,128)S(1)} %copy-done.57), kind=kOutput, calls=%fused_computation.34 | convolution fusion | flops 2959998976 | bytes 18612224 | tf_op jit(solution)/shard_map/tf,df->td/dot_general | solution.py:806
  169.7 3.5 convolution_add_fusion
  176.5 14.0 %collective-permute-done.9 = bf16[128,2048]{1,0:T(8,128)(2,1)S(1)} collective-permute-done((bf16[128,2048]{1,0:T(8,128)(2,1)S(1)}, bf16[128,2048]{1,0:T(8,128)(2,1)S(1)}, u32[]{:S(2)}, u32[]{:S(2)}) %collective-permute-start.9) | collective-permute-done | bytes 524320 | tf_op jit(solution)/shard_map/ppermute | solution.py:720
  193.4 13.4 %collective-permute-done.10 = bf16[128,2048]{1,0:T(8,128)(2,1)} collective-permute-done((bf16[128,2048]{1,0:T(8,128)(2,1)}, bf16[128,2048]{1,0:T(8,128)(2,1)}, u32[]{:S(2)}, u32[]{:S(2)}) %collective-permute-start.10) | collective-permute-done | bytes 524320 | tf_op jit(solution)/shard_map/ppermute | solution.py:720
  221.6 21.9 %mixer_backward.1 = (bf16[512,512]{1,0:T(8,128)(2,1)}, bf16[512,512]{1,0:T(8,128)(2,1)}, bf16[512,512]{1,0:T(8,128)(2,1)}, bf16[512,128]{1,0:T(8,128)(2,1)}, f32[12,512]{1,0:T(8,128)}, /*index=5*/f32[1,128]{1,0:T(1,128)}) custom-call(f32[512,512]{1,0:T(8,128)} %get-tuple-element.64.d_mixer_ref, f32[512,512]{1,0:T(8,128)} %fusion.47.query_ref, ...), custom_call_target="tpu_custom_call" | custom-call | tf_op jit(solution)/shard_map/mixer_backward/pallas_call | solution.py:443
  259.5 2.6 convolution_convert_fusion.1.refs_8_
  265.5 3.5 fusion.54
  277.2 3.3 add_convert_fusion.refs_6_
  280.5 13.9 %collective-permute-done.16 = bf16[256,2048]{1,0:T(8,128)(2,1)} collective-permute-done((bf16[256,2048]{1,0:T(8,128)(2,1)}, bf16[256,2048]{1,0:T(8,128)(2,1)}, u32[]{:S(2)}, u32[]{:S(2)}) %collective-permute-start.16) | collective-permute-done | bytes 1048608 | tf_op jit(solution)/shard_map/ppermute | solution.py:767
  298.4 212.6 %ffn_and_sums.1 = (bf16[2048,1408]{1,0:T(8,128)(2,1)}, bf16[2048,1408]{1,0:T(8,128)(2,1)}, bf16[1408,2048]{1,0:T(8,128)(2,1)}, bf16[512,2048]{1,0:T(8,128)(2,1)}...) custom-call(bf16[4096,2048]{1,0:T(8,128)(2,1)} %all-gather.5.cloned., ...), custom_call_target="tpu_custom_call" | custom-call | flops 141733920768 | bytes 369098752 | tf_op jit(solution)/shard_map/ffn_and_sums/pallas_call | solution.py:685
  515.8 5.2 convert_element_type.285
  527.7 2.7 convert_element_type.290
  530.5 2.7 convert_element_type.291
  534.2 2.7 convert_element_type.293
  536.9 5.2 convert_element_type.286
  542.1 6.0 %convert_element_type.287 = f32[1408,2048]{1,0:T(8,128)} convert(bf16[1408,2048]{1,0:T(8,128)(2,1)S(1)} %bitcast.153) | non-fusion elementwise | flops 2883584 | bytes 17301504 | tf_op jit(solution)/shard_map/convert_element_type | solution.py:949
  548.6 3.4 collective-permute-done.21
  (286 shorter events, 128.3 us)
Async XLA Ops:
  7.2 148.2 %all-gather.3.cloned.1.call-start = ((), (), s32[]{:S(2)}) async-start(), calls=%async_computation | async-start | bytes 17301504 | tf_op jit(solution)/shard_map/all_gather | solution.py:853
  8.0 290.5 %all-gather.5.cloned.1.call-start = ((), (), s32[]{:S(2)}) async-start(), calls=%async_computation.1 | async-start | bytes 17825792 | tf_op jit(solution)/shard_map/all_gather | solution.py:870
  11.0 20.2 %collective-permute-start.2 = (bf16[128,2048]{1,0:T(8,128)(2,1)S(1)}, bf16[128,2048]{1,0:T(8,128)(2,1)}, u32[]{:S(2)}, u32[]{:S(2)}) collective-permute-start(bf16[128,2048]{1,0:T(8,128)(2,1)S(1)} %fusion.11), channel_id=1, source_target_pairs={{0,1},{1,0},{2,3},{3,2},{4,5},{5,4},{6,7},{7,6},{8,9},{9,8},{10,11... | collective-permute-start | bytes 1572872 | tf_op jit(solution)/shard_map/ppermute | solution.py:720
  11.5 17.6 %collective-permute-start = (bf16[128,2048]{1,0:T(8,128)(2,1)S(1)}, bf16[128,2048]{1,0:T(8,128)(2,1)S(1)}, u32[]{:S(2)}, u32[]{:S(2)}) collective-permute-start(bf16[128,2048]{1,0:T(8,128)(2,1)S(1)} %fusion.11), channel_id=1, source_target_pairs={{0,2},{2,0},{1,3},{3,1},{4,6},{6,4},{5,7},{7,5},{8,10},{10,8},{9,1... | collective-permute-start | bytes 1572872 | tf_op jit(solution)/shard_map/ppermute | solution.py:720
  29.2 3.6 collective-permute-start.1
  71.7 3.0 collective-permute-start.3
  78.4 26.6 %collective-permute-start.4 = (bf16[128,2048]{1,0:T(8,128)(2,1)S(1)}, bf16[128,2048]{1,0:T(8,128)(2,1)}, u32[]{:S(2)}, u32[]{:S(2)}) collective-permute-start(bf16[128,2048]{1,0:T(8,128)(2,1)S(1)} %fusion.24), channel_id=1, source_target_pairs={{0,2},{2,0},{1,3},{3,1},{4,6},{6,4},{5,7},{7,5},{8,10},{10,8},{9,1... | collective-permute-start | bytes 1572872 | tf_op jit(solution)/shard_map/ppermute | solution.py:720
  108.0 23.8 %collective-permute-start.5 = (bf16[128,2048]{1,0:T(8,128)(2,1)}, bf16[128,2048]{1,0:T(8,128)(2,1)}, u32[]{:S(2)}, u32[]{:S(2)}) collective-permute-start(bf16[128,2048]{1,0:T(8,128)(2,1)} %multiply_convert_fusion.5), channel_id=1, source_target_pairs={{0,2},{2,0},{1,3},{3,1},{4,6},{6,4},{5,7},{7,5},{8,10},{10,8},{9,1... | collective-permute-start | bytes 1572872 | tf_op jit(solution)/shard_map/ppermute | solution.py:720
  109.9 21.9 %collective-permute-start.7 = (bf16[128,2048]{1,0:T(8,128)(2,1)}, bf16[128,2048]{1,0:T(8,128)(2,1)}, u32[]{:S(2)}, u32[]{:S(2)}) collective-permute-start(bf16[128,2048]{1,0:T(8,128)(2,1)} %multiply_convert_fusion.5), channel_id=1, source_target_pairs={{0,1},{1,0},{2,3},{3,2},{4,5},{5,4},{6,7},{7,6},{8,9},{9,8},{10,11... | collective-permute-start | bytes 1572872 | tf_op jit(solution)/shard_map/ppermute | solution.py:720
  176.4 14.1 %collective-permute-start.9 = (bf16[128,2048]{1,0:T(8,128)(2,1)S(1)}, bf16[128,2048]{1,0:T(8,128)(2,1)S(1)}, u32[]{:S(2)}, u32[]{:S(2)}) collective-permute-start(bf16[128,2048]{1,0:T(8,128)(2,1)S(1)} %fusion.25), channel_id=1, source_target_pairs={{0,2},{2,0},{1,3},{3,1},{4,6},{6,4},{5,7},{7,5},{8,10},{10,8},{9,1... | collective-permute-start | bytes 1572872 | tf_op jit(solution)/shard_map/ppermute | solution.py:720
  193.1 13.7 %collective-permute-start.10 = (bf16[128,2048]{1,0:T(8,128)(2,1)}, bf16[128,2048]{1,0:T(8,128)(2,1)}, u32[]{:S(2)}, u32[]{:S(2)}) collective-permute-start(bf16[128,2048]{1,0:T(8,128)(2,1)} %get-tuple-element.203), channel_id=1, source_target_pairs={{0,2},{2,0},{1,3},{3,1},{4,6},{6,4},{5,7},{7,5},{8,10},{10,8},{9,1... | collective-permute-start | bytes 1572872 | tf_op jit(solution)/shard_map/ppermute | solution.py:720
  193.4 18.4 %collective-permute-start.12 = (bf16[128,2048]{1,0:T(8,128)(2,1)}, bf16[128,2048]{1,0:T(8,128)(2,1)}, u32[]{:S(2)}, u32[]{:S(2)}) collective-permute-start(bf16[128,2048]{1,0:T(8,128)(2,1)} %get-tuple-element.203), channel_id=1, source_target_pairs={{0,1},{1,0},{2,3},{3,2},{4,5},{5,4},{6,7},{7,6},{8,9},{9,8},{10,11... | collective-permute-start | bytes 1572872 | tf_op jit(solution)/shard_map/ppermute | solution.py:720
  206.8 7.0 %collective-permute-start.11 = (bf16[128,2048]{1,0:T(8,128)(2,1)}, bf16[128,2048]{1,0:T(8,128)(2,1)}, u32[]{:S(2)}, u32[]{:S(2)}) collective-permute-start(bf16[128,2048]{1,0:T(8,128)(2,1)} %collective-permute-done.10), channel_id=1, source_target_pairs={{0,1},{1,0},{2,3},{3,2},{4,5},{5,4},{6,7},{7,6},{8,9},{9,8},{10,11... | collective-permute-start | bytes 1572872 | tf_op jit(solution)/shard_map/ppermute | solution.py:720
  244.5 32.6 %collective-permute-start.17 = (bf16[1024,512]{1,0:T(8,128)(2,1)}, bf16[1024,512]{1,0:T(8,128)(2,1)}, u32[]{:S(2)}, u32[]{:S(2)}) collective-permute-start(bf16[1024,512]{1,0:T(8,128)(2,1)} %constant_dynamic-slice_fusion.1), channel_id=1, source_target_pairs={{0,4},{4,0},{8,12},{12,8},{16,20},{20,16},{24,28},{28,24},{1,5},{5... | collective-permute-start | bytes 3145736 | tf_op jit(solution)/shard_map/ppermute | solution.py:767
  247.3 47.1 %collective-permute-start.16 = (bf16[256,2048]{1,0:T(8,128)(2,1)}, bf16[256,2048]{1,0:T(8,128)(2,1)}, u32[]{:S(2)}, u32[]{:S(2)}) collective-permute-start(bf16[256,2048]{1,0:T(8,128)(2,1)} %constant_dynamic-slice_fusion.2), channel_id=1, source_target_pairs={{0,4},{4,0},{8,12},{12,8},{16,20},{20,16},{24,28},{28,24},{1,5},{5... | collective-permute-start | bytes 3145736 | tf_op jit(solution)/shard_map/ppermute | solution.py:767
  255.0 20.1 %collective-permute-start.15 = (bf16[2,128,2048]{2,1,0:T(8,128)(2,1)S(1)}, bf16[2,128,2048]{2,1,0:T(8,128)(2,1)S(1)}, u32[]{:S(2)}, u32[]{:S(2)}) collective-permute-start(bf16[2,128,2048]{2,1,0:T(8,128)(2,1)S(1)} %fusion.8), channel_id=1, source_target_pairs={{0,1},{1,0},{2,3},{3,2},{4,5},{5,4},{6,7},{7,6},{8,9},{9,8},{10,11... | collective-permute-start | bytes 3145736 | tf_op jit(solution)/shard_map/ppermute | solution.py:720
  274.1 239.5 %collective-permute-start.13 = (bf16[2,128,2048]{2,1,0:T(8,128)(2,1)}, bf16[2,128,2048]{2,1,0:T(8,128)(2,1)}, u32[]{:S(2)}, u32[]{:S(2)}) collective-permute-start(bf16[2,128,2048]{2,1,0:T(8,128)(2,1)} %fusion.7), channel_id=1, source_target_pairs={{0,1},{1,0},{2,3},{3,2},{4,5},{5,4},{6,7},{7,6},{8,9},{9,8},{10,11... | collective-permute-start | bytes 3145736 | tf_op jit(solution)/shard_map/ppermute | solution.py:720
  297.0 214.1 %collective-permute-start.18 = (bf16[128,2048]{1,0:T(8,128)(2,1)S(1)}, bf16[128,2048]{1,0:T(8,128)(2,1)S(1)}, u32[]{:S(2)}, u32[]{:S(2)}) collective-permute-start(bf16[128,2048]{1,0:T(8,128)(2,1)S(1)} %fusion.27), channel_id=1, source_target_pairs={{0,2},{2,0},{1,3},{3,1},{4,6},{6,4},{5,7},{7,5},{8,10},{10,8},{9,1... | collective-permute-start | bytes 1572872 | tf_op jit(solution)/shard_map/ppermute | solution.py:720
  512.9 8.1 %collective-permute-start.19 = (f32[4224]{0:T(1024)S(1)}, f32[4224]{0:T(1024)S(1)}, u32[]{:S(2)}, u32[]{:S(2)}) collective-permute-start(f32[4224]{0:T(1024)S(1)} %pad_maximum_fusion), channel_id=1, source_target_pairs={{0,2},{2,0},{1,3},{3,1},{4,6},{6,4},{5,7},{7,5},{8,10},{10,8},{9,1... | collective-permute-start | bytes 50696 | tf_op jit(solution)/shard_map/ppermute | solution.py:958
  521.0 27.1 %collective-permute-start.20 = (f32[4224]{0:T(1024)S(1)}, f32[4224]{0:T(1024)S(1)}, u32[]{:S(2)}, u32[]{:S(2)}) collective-permute-start(f32[4224]{0:T(1024)S(1)} %fusion.44), channel_id=1, source_target_pairs={{0,1},{1,0},{2,3},{3,2},{4,5},{5,4},{6,7},{7,6},{8,9},{9,8},{10,11... | collective-permute-start | bytes 50696 | tf_op jit(solution)/shard_map/ppermute | solution.py:958
  521.2 35.5 %collective-permute-start.14 = (bf16[128,2048]{1,0:T(8,128)(2,1)S(1)}, bf16[128,2048]{1,0:T(8,128)(2,1)S(1)}, u32[]{:S(2)}, u32[]{:S(2)}) collective-permute-start(bf16[128,2048]{1,0:T(8,128)(2,1)S(1)} %fusion.26), channel_id=1, source_target_pairs={{0,2},{2,0},{1,3},{3,1},{4,6},{6,4},{5,7},{7,5},{8,10},{10,8},{9,1... | collective-permute-start | bytes 1572872 | tf_op jit(solution)/shard_map/ppermute | solution.py:720
  548.1 3.8 collective-permute-start.21
  552.0 3.8 collective-permute-start.22
  555.8 4.7 collective-permute-start.23
  (69 other events, 1165.4 us)
Sparse Core Ops, SparseCore 0:
  10.9 139.5 all-gather.2
  152.7 126.0 all-gather.4
